TPU v7x, 32 devices: a whole 2x2x4 slice. The times are simulated.
32 devices in a mesh: seq: 8 (over z, y), tp: 4 (over x, core).
Axes of the slice: x: 2, y: 2, z: 4, core: 2. Of those that a mesh axis runs over, the one named last changes fastest.
Arguments:
- layer_input: bfloat16 [8, 2048, 1024], P('tp', 'seq'), may hold values from -6 to 6
- first_values: bfloat16 [8, 1024, 2048], P(None, 'tp', 'seq'), may hold values from -16 to 16
- doc_lengths: int32 [8, 16], replicated, may hold values from 1 to 1024, 2048 in all within a row
- attn_gain: bfloat16 [1024], replicated, may hold values from 0.25 to 1.75
- query_weight: bfloat16 [1024, 1024], P('tp'), may hold values from -0.1875 to 0.1875
- key_weight: bfloat16 [1024, 1024], P('tp'), may hold values from -0.1875 to 0.1875
- value_weight: bfloat16 [1024, 1024], P('tp'), may hold values from -0.1875 to 0.1875
- output_weight: bfloat16 [1024, 1024], P('tp'), may hold values from -0.75 to 0.75
- feed_gain: bfloat16 [1024], replicated, may hold values from 0.25 to 1.75
- gate_weight: bfloat16 [1024, 2816], P(None, 'tp'), may hold values from -0.1875 to 0.1875
- up_weight: bfloat16 [1024, 2816], P(None, 'tp'), may hold values from -0.1875 to 0.1875
- down_weight: bfloat16 [2816, 1024], P('tp'), may hold values from -0.21875 to 0.21875
- out_cotangent: bfloat16 [8, 2048, 1024], P('tp', 'seq'), may hold values from -6 to 6
Outputs:
- layer_output: bfloat16 [8, 2048, 1024], P('tp', 'seq')
- input_grad: bfloat16 [8, 2048, 1024], P('tp', 'seq')
- first_grad: float32 [8, 1024, 2048], P(None, 'tp', 'seq')
- attn_gain_grad: float32 [1024], replicated
- query_grad: float32 [1024, 1024], P('tp')
- key_grad: float32 [1024, 1024], P('tp')
- value_grad: float32 [1024, 1024], P('tp')
- output_proj_grad: float32 [1024, 1024], P('tp')
- feed_gain_grad: float32 [1024], replicated
- gate_grad: float32 [1024, 2816], P(None, 'tp')
- up_grad: float32 [1024, 2816], P(None, 'tp')
- down_grad: float32 [2816, 1024], P('tp')
- value_norms: float32 [2], replicated
Inputs may be any that keep to these rules, and one draw needn't show every extreme that they name: `doc_lengths`: each row's 16 lengths sum to 2048, and its longest document has exactly 1024 tokens.
All inputs are finite; a program needn't handle non-finite values.
Results may differ from a plain program's by a relative error of at most 0.019.
Values may be sent and summed in bfloat16 or wider, within the bound.
A program may use at most 256 MiB of HBM per device.

v0:
```python
import jax
import jax.numpy as jnp
from jax import lax
from jax.sharding import PartitionSpec as P

HD = 64
ROW = 2048


norm_eps = 1e-06
rope_base = 10000.0
masked_score = -1e30


def doc_layout(doc_lengths):
    doc_ends = jnp.cumsum(doc_lengths, axis=-1)
    places = jnp.arange(ROW, dtype=jnp.int32)
    passed = doc_ends[:, None, :] <= places[None, :, None]
    segment = jnp.sum(passed.astype(jnp.int32), axis=-1)
    starts = jnp.max(jnp.where(passed, doc_ends[:, None, :], 0), axis=-1)
    return (segment, places[None, :] - starts)


def rotary_tables(offsets):
    half_dim = HD // 2
    frequency = rope_base ** (-jnp.arange(half_dim, dtype=jnp.float32) * 2.0 / HD)
    angles = offsets.astype(jnp.float32)[..., None] * frequency
    return (jnp.cos(angles)[..., None, :], jnp.sin(angles)[..., None, :])


def rotate(values_in, tables):
    cosine, sine_part = tables
    half_dim = HD // 2
    first_half = values_in[..., :half_dim]
    second_half = values_in[..., half_dim:]
    return jnp.concatenate(
        [
            first_half * cosine - second_half * sine_part,
            second_half * cosine + first_half * sine_part,
        ],
        axis=-1,
    )


def unrotate(grads_in, tables):
    cosine, sine_part = tables
    half_dim = HD // 2
    first_half = grads_in[..., :half_dim]
    second_half = grads_in[..., half_dim:]
    return jnp.concatenate(
        [
            first_half * cosine + second_half * sine_part,
            second_half * cosine - first_half * sine_part,
        ],
        axis=-1,
    )


def norm_rows(values_in):
    inverse = lax.rsqrt(jnp.mean(values_in * values_in, axis=-1, keepdims=True) + norm_eps)
    return (values_in * inverse, inverse)


def norm_back(grads_in, unit_rows, inverse, gain):
    scaled = grads_in * gain
    extra = inverse * (scaled - unit_rows * jnp.mean(scaled * unit_rows, axis=-1, keepdims=True))
    return (extra, jnp.sum(grads_in * unit_rows, axis=(0, 1)))


def allowed_for(seg_query, place_query, seg_keys, place_keys):
    return (seg_query[:, :, None] == seg_keys[:, None, :]) & (
        place_keys[None, None, :] <= place_query[None, :, None]
    )


def score_block(query_block, key_block, allowed):
    raw = jnp.einsum(
        "gqhd,gkhd->ghqk", query_block, key_block, preferred_element_type=jnp.float32
    ) * HD ** (-0.5)
    return jnp.where(allowed[:, None], raw, masked_score)


def prob_block(query_block, key_block, logsum_block, allowed):
    return jnp.exp(
        score_block(query_block, key_block, allowed)
        - jnp.transpose(logsum_block, (0, 2, 1))[..., None]
    )


def shards(
    layer_input,
    first_values,
    doc_lengths,
    attn_gain,
    query_weight,
    key_weight,
    value_weight,
    output_weight,
    feed_gain,
    gate_weight,
    up_weight,
    down_weight,
    out_cotangent,
):
    local_len = layer_input.shape[1]
    row_count = first_values.shape[0]
    width_local = query_weight.shape[0]
    head_count = width_local // HD
    group_rows = min(row_count, max(1, 512 // local_len))
    block_count = row_count // group_rows
    score_scale = HD ** (-0.5)

    def blocked(array_in):
        return array_in.reshape((block_count, group_rows) + array_in.shape[1:])

    def unblocked(array_in):
        return array_in.reshape((row_count,) + array_in.shape[2:])

    segment, offsets = doc_layout(doc_lengths)
    begin = lax.axis_index("seq") * local_len
    seg_own = lax.dynamic_slice_in_dim(segment, begin, local_len, 1)
    off_own = lax.dynamic_slice_in_dim(offsets, begin, local_len, 1)
    places_all = jnp.arange(ROW, dtype=jnp.int32)
    places_own = begin + jnp.arange(local_len, dtype=jnp.int32)
    tables = rotary_tables(off_own)
    attn_scale = attn_gain.astype(jnp.float32)
    feed_scale = feed_gain.astype(jnp.float32)
    first_rows = jnp.swapaxes(first_values, 1, 2)
    source = layer_input.astype(jnp.float32)
    unit_attn, inv_attn = norm_rows(source)
    normed = (unit_attn * attn_scale).astype(jnp.bfloat16)
    normed_all = lax.all_gather(normed, "tp", axis=0, tiled=True)
    stacked_weights = jnp.concatenate([query_weight, key_weight, value_weight], axis=0)
    projected = jnp.einsum(
        "rtd,ed->rte", normed_all, stacked_weights, preferred_element_type=jnp.float32
    )
    queries = rotate(
        projected[..., :width_local].reshape(row_count, local_len, head_count, HD), tables
    ).astype(jnp.bfloat16)
    keys_rot = rotate(
        projected[..., width_local : 2 * width_local].reshape(row_count, local_len, head_count, HD),
        tables,
    ).astype(jnp.bfloat16)
    mixed = (0.5 * projected[..., 2 * width_local :] + 0.5 * first_rows.astype(jnp.float32)).astype(
        jnp.bfloat16
    )
    both_own = jnp.concatenate(
        [keys_rot.reshape(row_count, local_len, width_local), mixed], axis=-1
    )
    both_all = lax.all_gather(both_own, "seq", axis=1, tiled=True)
    keys_all = both_all[..., :width_local].reshape(row_count, ROW, head_count, HD)
    values_all = both_all[..., width_local:].reshape(row_count, ROW, head_count, HD)

    def attend_block(pieces):
        query_block, key_block, value_block, seg_query, seg_keys = pieces
        scores = score_block(
            query_block, key_block, allowed_for(seg_query, places_own, seg_keys, places_all)
        )
        highest = jnp.max(scores, axis=-1, keepdims=True)
        weights = jnp.exp(scores - highest)
        totals = jnp.sum(weights, axis=-1, keepdims=True)
        softmax_low = (weights / totals).astype(jnp.bfloat16)
        result_block = jnp.einsum(
            "ghqk,gkhd->gqhd", softmax_low, value_block, preferred_element_type=jnp.float32
        )
        return (result_block, jnp.transpose((highest + jnp.log(totals))[..., 0], (0, 2, 1)))

    attended_blocks, logsum_blocks = lax.map(
        attend_block,
        (
            blocked(queries),
            blocked(keys_all),
            blocked(values_all),
            blocked(seg_own),
            blocked(segment),
        ),
    )
    attended = (
        unblocked(attended_blocks).reshape(row_count, local_len, width_local).astype(jnp.bfloat16)
    )
    logsum = unblocked(logsum_blocks)
    piece = attended
    middle = source + lax.psum_scatter(
        jnp.einsum("rte,ed->rtd", piece, output_weight, preferred_element_type=jnp.float32),
        "tp",
        scatter_dimension=0,
        tiled=True,
    )
    unit_feed, inv_feed = norm_rows(middle)
    feed_in = (unit_feed * feed_scale).astype(jnp.bfloat16)
    feed_all = lax.all_gather(feed_in, "tp", axis=0, tiled=True)
    gate = jnp.einsum("rtd,df->rtf", feed_all, gate_weight, preferred_element_type=jnp.float32)
    up_part = jnp.einsum("rtd,df->rtf", feed_all, up_weight, preferred_element_type=jnp.float32)
    sigmoid_gate = jax.nn.sigmoid(gate)
    activated = gate * sigmoid_gate
    hidden = (activated * up_part).astype(jnp.bfloat16)
    piece = hidden
    layer_output = (
        middle
        + lax.psum_scatter(
            jnp.einsum(
                "rtf,fd->rtd", piece, down_weight, preferred_element_type=jnp.float32
            ).astype(jnp.bfloat16),
            "tp",
            scatter_dimension=0,
            tiled=True,
        ).astype(jnp.float32)
    ).astype(jnp.bfloat16)
    cotangent = out_cotangent.astype(jnp.float32)
    cot_all = lax.all_gather(out_cotangent, "tp", axis=0, tiled=True)
    down_grad = jnp.einsum("rtf,rtd->fd", hidden, cot_all, preferred_element_type=jnp.float32)
    hidden_g = jnp.einsum("rtd,fd->rtf", cot_all, down_weight, preferred_element_type=jnp.float32)
    gate_g = (hidden_g * up_part * sigmoid_gate * (1.0 + gate * (1.0 - sigmoid_gate))).astype(
        jnp.bfloat16
    )
    up_g = (hidden_g * activated).astype(jnp.bfloat16)
    gate_grad = jnp.einsum("rtd,rtf->df", feed_all, gate_g, preferred_element_type=jnp.float32)
    up_grad = jnp.einsum("rtd,rtf->df", feed_all, up_g, preferred_element_type=jnp.float32)
    feed_in_g = lax.psum_scatter(
        jnp.einsum("rtf,df->rtd", gate_g, gate_weight, preferred_element_type=jnp.float32)
        + jnp.einsum("rtf,df->rtd", up_g, up_weight, preferred_element_type=jnp.float32),
        "tp",
        scatter_dimension=0,
        tiled=True,
    )
    middle_extra, feed_gain_part = norm_back(feed_in_g, unit_feed, inv_feed, feed_scale)
    middle_g = cotangent + middle_extra
    branch_all = lax.all_gather(middle_g.astype(jnp.bfloat16), "tp", axis=0, tiled=True)
    output_proj_grad = jnp.einsum(
        "rte,rtd->ed", attended, branch_all, preferred_element_type=jnp.float32
    )
    attended_g = jnp.einsum(
        "rtd,ed->rte", branch_all, output_weight, preferred_element_type=jnp.float32
    ).astype(jnp.bfloat16)
    grad_heads = attended_g.reshape(row_count, local_len, head_count, HD)

    def back_block(pieces):
        query_block, key_block, value_block, grad_block, logsum_block, seg_query, seg_keys = pieces
        probs_full = prob_block(
            query_block,
            key_block,
            logsum_block,
            allowed_for(seg_query, places_own, seg_keys, places_all),
        )
        prob_grad = jnp.einsum(
            "gqhd,gkhd->ghqk", grad_block, value_block, preferred_element_type=jnp.float32
        )
        centre = jnp.sum(probs_full * prob_grad, axis=-1, keepdims=True)
        score_grad = (probs_full * (prob_grad - centre)).astype(jnp.bfloat16)
        query_part = (
            jnp.einsum("ghqk,gkhd->gqhd", score_grad, key_block, preferred_element_type=jnp.float32)
            * score_scale
        )
        key_part = (
            jnp.einsum(
                "ghqk,gqhd->gkhd", score_grad, query_block, preferred_element_type=jnp.float32
            )
            * score_scale
        )
        value_part = jnp.einsum(
            "ghqk,gqhd->gkhd",
            probs_full.astype(jnp.bfloat16),
            grad_block,
            preferred_element_type=jnp.float32,
        )
        return (query_part, key_part, value_part)

    query_blocks, key_blocks, value_blocks = lax.map(
        back_block,
        (
            blocked(queries),
            blocked(keys_all),
            blocked(values_all),
            blocked(grad_heads),
            blocked(logsum),
            blocked(seg_own),
            blocked(segment),
        ),
    )
    query_g = unblocked(query_blocks)
    key_terms = jnp.concatenate(
        [
            unblocked(key_blocks).reshape(row_count, ROW, width_local),
            unblocked(value_blocks).reshape(row_count, ROW, width_local),
        ],
        axis=-1,
    )
    key_sums = lax.psum_scatter(
        key_terms.astype(jnp.bfloat16), "seq", scatter_dimension=1, tiled=True
    ).astype(jnp.float32)
    keys_own_g = key_sums[..., :width_local]
    values_own_g = key_sums[..., width_local:]
    first_grad = jnp.swapaxes(0.5 * values_own_g, 1, 2)
    value_low = (0.5 * values_own_g).astype(jnp.bfloat16)
    key_low = (
        unrotate(keys_own_g.reshape(row_count, local_len, head_count, HD), tables)
        .astype(jnp.bfloat16)
        .reshape(row_count, local_len, width_local)
    )
    query_low = (
        unrotate(query_g, tables).astype(jnp.bfloat16).reshape(row_count, local_len, width_local)
    )
    stacked_g = jnp.concatenate([query_low, key_low, value_low], axis=-1)
    stacked_grad = jnp.einsum(
        "rte,rtd->ed", stacked_g, normed_all, preferred_element_type=jnp.float32
    )
    piece = stacked_g
    normed_g = lax.psum_scatter(
        jnp.einsum(
            "rte,ed->rtd", piece, stacked_weights, preferred_element_type=jnp.float32
        ).astype(jnp.bfloat16),
        "tp",
        scatter_dimension=0,
        tiled=True,
    ).astype(jnp.float32)
    input_extra, attn_gain_part = norm_back(normed_g, unit_attn, inv_attn, attn_scale)
    input_grad = (middle_g + input_extra).astype(jnp.bfloat16)
    summed = (
        lax.psum(stacked_grad.astype(jnp.bfloat16), "seq").astype(jnp.float32),
        lax.psum(output_proj_grad.astype(jnp.bfloat16), "seq").astype(jnp.float32),
        lax.psum(gate_grad.astype(jnp.bfloat16), "seq").astype(jnp.float32),
        lax.psum(up_grad.astype(jnp.bfloat16), "seq").astype(jnp.float32),
        lax.psum(down_grad.astype(jnp.bfloat16), "seq").astype(jnp.float32),
    )
    first_float = first_values.astype(jnp.float32)
    mixed_float = mixed.astype(jnp.float32)
    squares = jnp.stack([jnp.sum(first_float * first_float), jnp.sum(mixed_float * mixed_float)])
    small = lax.psum((attn_gain_part, feed_gain_part, squares), ("seq", "tp"))
    stacked_total = summed[0]
    return (
        layer_output,
        input_grad,
        first_grad,
        small[0],
        stacked_total[:width_local],
        stacked_total[width_local : 2 * width_local],
        stacked_total[2 * width_local :],
        summed[1],
        small[1],
        summed[2],
        summed[3],
        summed[4],
        jnp.sqrt(small[2]),
    )


def solution(mesh):
    placed = (
        P("tp", "seq", None),
        P(None, "tp", "seq"),
        P(),
        P(),
        P("tp", None),
        P("tp", None),
        P("tp", None),
        P("tp", None),
        P(),
        P(None, "tp"),
        P(None, "tp"),
        P("tp", None),
        P("tp", "seq", None),
    )
    return jax.shard_map(
        shards,
        mesh=mesh,
        in_specs=placed,
        out_specs=(
            P("tp", "seq", None),
            P("tp", "seq", None),
            P(None, "tp", "seq"),
            P(),
            P("tp", None),
            P("tp", None),
            P("tp", None),
            P("tp", None),
            P(),
            P(None, "tp"),
            P(None, "tp"),
            P("tp", None),
            P(),
        ),
        check_vma=False,
    )
```

profile of v0, /device:TPU:0, one launch (start us, length us, event | category | flops | bytes accessed | tf_op | source)
XLA Modules:
  0.0 1586.2 jit_solution(14736709833911528369)
XLA Ops:
  17.1 33.0 %all-gather.6.cloned.1.call-done = bf16[8,256,1024]{2,1,0:T(8,128)(2,1)} async-done(((bf16[2,256,1024]{2,1,0:T(8,128)(2,1)}), bf16[8,256,1024]{2,1,0:T(8,128)(2,1)}) %all-gather.6.cloned.1.call-update) | async-done | bytes 4194320 | tf_op jit(solution)/shard_map/all_gather | solution.py:132
  74.6 224.8 %all-gather.8.cloned.1.call-done = bf16[8,2048,512]{2,1,0:T(8,128)(2,1)} async-done(((bf16[8,256,512]{2,1,0:T(8,128)(2,1)}), bf16[8,2048,512]{2,1,0:T(8,128)(2,1)}) %all-gather.8.cloned.1.call-update) | async-done | bytes 16777232 | tf_op jit(solution)/shard_map/all_gather | solution.py:150
  299.4 11.4 fusion.108
  310.8 11.5 copy.73
  322.4 11.4 copy.71
  333.8 72.0 %while.30 = (s32[]{:T(128)}, bf16[4,2,256,4,64]{2,4,3,1,0:T(8,128)(2,1)}, f32[4,2,256,4]{2,3,1,0:T(4,128)}, bf16[4,2,2048,4,64]{2,4,3,1,0:T(8,128)(2,1)}, s32[4,...) while((s32[]{:T(128)}, ...), condition=%wide.region_7.8_spmd.clone.clone, body=%wide.region_4.7_spmd.clone.sunk.clone | while | flops 1126693120 | bytes 60680308 | solution.py:168
  412.8 69.1 %reduce-scatter.6.cloned.1.call-done = f32[2,256,1024]{2,1,0:T(8,128)} async-done(((f32[8,256,1024]{2,1,0:T(8,128)}), f32[2,256,1024]{2,1,0:T(8,128)}) %reduce-scatter.6.cloned.1.call-update) | async-done | bytes 2097168 | tf_op jit(solution)/shard_map/reduce_scatter | solution.py:183
  486.7 33.5 %all-gather.10.cloned.1.call-done = bf16[8,256,1024]{2,1,0:T(8,128)(2,1)} async-done(((bf16[2,256,1024]{2,1,0:T(8,128)(2,1)}), bf16[8,256,1024]{2,1,0:T(8,128)(2,1)}) %all-gather.10.cloned.1.call-update) | async-done | bytes 4194320 | tf_op jit(solution)/shard_map/all_gather | solution.py:191
  533.7 22.5 %all-gather.12.cloned.1.call-done = bf16[8,256,1024]{2,1,0:T(8,128)(2,1)} async-done(((bf16[2,256,1024]{2,1,0:T(8,128)(2,1)}), bf16[8,256,1024]{2,1,0:T(8,128)(2,1)}) %all-gather.12.cloned.1.call-update) | async-done | bytes 4194320 | tf_op jit(solution)/shard_map/all_gather | solution.py:210
  556.1 10.5 multiply_convert_fusion.1
  575.9 71.5 %reduce-scatter.10.cloned.1.call-done = f32[2,256,1024]{2,1,0:T(8,128)} async-done(((f32[8,256,1024]{2,1,0:T(8,128)}), f32[2,256,1024]{2,1,0:T(8,128)}) %reduce-scatter.10.cloned.1.call-update) | async-done | bytes 2097168 | tf_op jit(solution)/shard_map/reduce_scatter | solution.py:219
  652.7 34.5 %all-gather.14.cloned.1.call-done = bf16[8,256,1024]{2,1,0:T(8,128)(2,1)} async-done(((bf16[2,256,1024]{2,1,0:T(8,128)(2,1)}), bf16[8,256,1024]{2,1,0:T(8,128)(2,1)}) %all-gather.14.cloned.1.call-update) | async-done | bytes 4194320 | tf_op jit(solution)/shard_map/all_gather | solution.py:228
  690.8 234.7 %while.31 = (s32[]{:T(128)}, f32[4,2,256,4,64]{2,4,3,1,0:T(8,128)}, bf16[4,2,2048,4,64]{2,4,3,1,0:T(8,128)(2,1)}, bf16[4,2,2048,4,64]{2,4,3,1,0:T(8,128)(2,1)}, ...) while((s32[]{:T(128)}, f32[4,2,256,4,64]{2,4,3,1,0:T(8,128)}, ...), condition=%wide.region_15.16_spmd.clone.clone, body=%wide.region_13.15_spmd.clone.sunk.clone | while | flops 2751068416 | bytes 206165232 | solution.py:268
  693.7 10.1 fusion.172
  712.7 16.7 %multiply_reduce_fusion.7 = (f32[2,4,256]{2,1,0:T(4,128)S(1)}, f32[2,4,256,2048]{3,2,1,0:T(8,128)}) fusion(f32[2,4,256,2048]{3,2,1,0:T(8,128)} %fusion.172, f32[2,4,256]{2,1,0:T(4,128)S(1)} %dynamic-slice_bitcast_fusion.14, pred[2,256,2048]{2,1,0:T(8,128)(4,1)S(1)} %compare_and_fusion.7, bf16[4,2,2048,4,64]{2,4,3,1,0:T(8,128)(2,1)} %get-tuple-element.604, ...), kind=kOutput, calls=%fused_computation.30.clone.1.clone | convolution fusion | flops 557840384 | bytes 36979712 | tf_op jit(solution)/shard_map/while/body/eval_jaxpr/gqhd,gkhd->ghqk/dot_general | solution.py:245
  729.5 12.1 multiply_convert_fusion.7
  752.2 10.1 fusion.172
  771.3 16.7 %multiply_reduce_fusion.7 = (f32[2,4,256]{2,1,0:T(4,128)S(1)}, f32[2,4,256,2048]{3,2,1,0:T(8,128)}) fusion(f32[2,4,256,2048]{3,2,1,0:T(8,128)} %fusion.172, f32[2,4,256]{2,1,0:T(4,128)S(1)} %dynamic-slice_bitcast_fusion.14, pred[2,256,2048]{2,1,0:T(8,128)(4,1)S(1)} %compare_and_fusion.7, bf16[4,2,2048,4,64]{2,4,3,1,0:T(8,128)(2,1)} %get-tuple-element.604, ...), kind=kOutput, calls=%fused_computation.30.clone.1.clone | convolution fusion | flops 557840384 | bytes 36979712 | tf_op jit(solution)/shard_map/while/body/eval_jaxpr/gqhd,gkhd->ghqk/dot_general | solution.py:245
  788.0 12.1 multiply_convert_fusion.7
  810.8 10.1 fusion.172
  829.9 16.7 %multiply_reduce_fusion.7 = (f32[2,4,256]{2,1,0:T(4,128)S(1)}, f32[2,4,256,2048]{3,2,1,0:T(8,128)}) fusion(f32[2,4,256,2048]{3,2,1,0:T(8,128)} %fusion.172, f32[2,4,256]{2,1,0:T(4,128)S(1)} %dynamic-slice_bitcast_fusion.14, pred[2,256,2048]{2,1,0:T(8,128)(4,1)S(1)} %compare_and_fusion.7, bf16[4,2,2048,4,64]{2,4,3,1,0:T(8,128)(2,1)} %get-tuple-element.604, ...), kind=kOutput, calls=%fused_computation.30.clone.1.clone | convolution fusion | flops 557840384 | bytes 36979712 | tf_op jit(solution)/shard_map/while/body/eval_jaxpr/gqhd,gkhd->ghqk/dot_general | solution.py:245
  846.6 12.1 multiply_convert_fusion.7
  869.3 10.1 fusion.172
  888.4 16.7 %multiply_reduce_fusion.7 = (f32[2,4,256]{2,1,0:T(4,128)S(1)}, f32[2,4,256,2048]{3,2,1,0:T(8,128)}) fusion(f32[2,4,256,2048]{3,2,1,0:T(8,128)} %fusion.172, f32[2,4,256]{2,1,0:T(4,128)S(1)} %dynamic-slice_bitcast_fusion.14, pred[2,256,2048]{2,1,0:T(8,128)(4,1)S(1)} %compare_and_fusion.7, bf16[4,2,2048,4,64]{2,4,3,1,0:T(8,128)(2,1)} %get-tuple-element.604, ...), kind=kOutput, calls=%fused_computation.30.clone.1.clone | convolution fusion | flops 557840384 | bytes 36979712 | tf_op jit(solution)/shard_map/while/body/eval_jaxpr/gqhd,gkhd->ghqk/dot_general | solution.py:245
  905.1 12.1 multiply_convert_fusion.7
  925.5 11.4 copy.76
  936.9 11.4 copy.75
  948.3 13.6 pad_maximum_fusion
  980.0 261.5 %reduce-scatter.12.cloned.1.call-done = bf16[8,256,512]{2,1,0:T(8,128)(2,1)} async-done(((bf16[8,2048,512]{2,1,0:T(8,128)(2,1)}), bf16[8,256,512]{2,1,0:T(8,128)(2,1)}) %reduce-scatter.12.cloned.1.call-update) | async-done | bytes 2097168 | tf_op jit(solution)/shard_map/reduce_scatter | solution.py:288
  1287.7 193.2 %all-reduce.4.cloned.1.call-done = (bf16[768,1024]{1,0:T(8,128)(2,1)}, bf16[256,1024]{1,0:T(8,128)(2,1)}, bf16[1024,704]{0,1:T(8,128)(2,1)}, bf16[1024,704]{0,1:T(8,128)(2,1)}, bf16[704,1024]{1,0:T(8,128)(2,1)}) async-done(((bf16[768,1024]{1,0:T(8,128)(2,1)}, bf16[256,1024]{1,0:T(8,128)(2,1)}, bf16[1024,704]{0,1:T(8,128)(2,1)}, bf16[1024,704]{0,1:T(8,128)(2,1)}, bf16[704,1024]{1,0:T(8,128)(2,1)}), ...) | async-done | bytes 6422544 | tf_op jit(solution)/shard_map/psum | solution.py:319
  1492.3 34.6 %reduce-scatter.14.cloned.1.call-done = bf16[2,256,1024]{2,1,0:T(8,128)(2,1)} async-done(((bf16[8,256,1024]{2,1,0:T(8,128)(2,1)}), bf16[2,256,1024]{2,1,0:T(8,128)(2,1)}) %reduce-scatter.14.cloned.1.call-update) | async-done | bytes 1048592 | tf_op jit(solution)/shard_map/reduce_scatter | solution.py:308
  1529.9 40.2 %all-reduce = (f32[1024]{0:T(1024)}, f32[1024]{0:T(1024)}, f32[2]{0:T(128)}) all-reduce(f32[1024]{0:T(1024)} %get-tuple-element.265, f32[1024]{0:T(1024)} %get-tuple-element.263, f32[2]{0:T(128)} %pad_maximum_fusion.9), channel_id=1, replica_groups=mesh['seq'=8,'tp'=4] {'seq','tp'}, use_global_device_ids=true, to_apply=%region_20.21 | all-reduce | flops 2050 | bytes 16400 | tf_op jit(solution)/shard_map/psum | solution.py:328
  (284 shorter events, 315.4 us)
Async XLA Ops:
  7.2 548.9 %copy-start = (bf16[704,1024]{1,0:T(8,128)(2,1)S(1)}, bf16[704,1024]{1,0:T(8,128)(2,1)}, u32[]{:S(2)}) copy-start(bf16[704,1024]{1,0:T(8,128)(2,1)} %param.28) | copy-start | bytes 4325380
  7.2 42.9 %all-gather.6.cloned.1.call-start = ((), (), s32[]{:S(2)}) async-start(), calls=%async_computation.5 | async-start | bytes 5242880 | tf_op jit(solution)/shard_map/all_gather | solution.py:132
  12.7 286.7 %all-gather.8.cloned.1.call-start = ((), (), s32[]{:S(2)}) async-start(), calls=%async_computation.6 | async-start | bytes 18874368 | tf_op jit(solution)/shard_map/all_gather | solution.py:150
  13.5 42.3 %copy-start.6 = (bf16[8,256,256]{1,2,0:T(8,128)(2,1)}, bf16[8,256,256]{1,2,0:T(8,128)(2,1)S(1)}, u32[]{:S(2)}) copy-start(bf16[8,256,256]{1,2,0:T(8,128)(2,1)S(1)} %copy.69) | copy-start | bytes 3145732
  72.0 409.9 %reduce-scatter.6.cloned.1.call-start = ((), (), s32[]{:S(2)}) async-start(), calls=%async_computation.7 | async-start | bytes 10485760 | tf_op jit(solution)/shard_map/reduce_scatter | solution.py:183
  412.2 108.0 %all-gather.10.cloned.1.call-start = ((), (), s32[]{:S(2)}) async-start(), calls=%async_computation.8 | async-start | bytes 5242880 | tf_op jit(solution)/shard_map/all_gather | solution.py:191
  412.8 237.5 %copy-start.24 = (f32[1024]{0:T(1024)}, f32[1024]{0:T(1024)S(1)}, u32[]{:S(2)}) copy-start(f32[1024]{0:T(1024)S(1)} %convert_element_type.152) | copy-start | bytes 12292
  484.1 166.3 %copy-start.1 = (f32[2,256,1024]{2,1,0:T(8,128)}, f32[2,256,1024]{2,1,0:T(8,128)S(1)}, u32[]{:S(2)}) copy-start(f32[2,256,1024]{2,1,0:T(8,128)S(1)} %get-tuple-element.322) | copy-start | bytes 6291460
  484.1 166.2 %copy-start.28 = (f32[2,256]{1,0:T(2,128)}, f32[2,256]{1,0:T(2,128)S(1)}, u32[]{:S(2)}) copy-start(f32[2,256]{1,0:T(2,128)S(1)} %add_rsqrt_fusion) | copy-start | bytes 6148
  485.6 70.5 %all-gather.12.cloned.1.call-start = ((), (), s32[]{:S(2)}) async-start(), calls=%async_computation.10 | async-start | bytes 5242880 | tf_op jit(solution)/shard_map/all_gather | solution.py:210
  486.2 161.3 %reduce-scatter.10.cloned.1.call-start = ((), (), s32[]{:S(2)}) async-start(), calls=%async_computation.11 | async-start | bytes 10485760 | tf_op jit(solution)/shard_map/reduce_scatter | solution.py:219
  556.1 10.5 copy-start.42
  575.9 111.3 %all-gather.14.cloned.1.call-start = ((), (), s32[]{:S(2)}) async-start(), calls=%async_computation.12 | async-start | bytes 5242880 | tf_op jit(solution)/shard_map/all_gather | solution.py:228
  652.6 588.9 %reduce-scatter.12.cloned.1.call-start = ((), (), s32[]{:S(2)}) async-start(), calls=%async_computation.13 | async-start | bytes 18874368 | tf_op jit(solution)/shard_map/reduce_scatter | solution.py:288
  652.7 38.1 %copy-start.4 = (bf16[4,2,256,4,64]{2,4,3,1,0:T(8,128)(2,1)S(1)}, bf16[4,2,256,4,64]{2,4,3,1,0:T(8,128)(2,1)}, u32[]{:S(2)}) copy-start(bf16[4,2,256,4,64]{2,4,3,1,0:T(8,128)(2,1)} %copy-done.3) | copy-start | bytes 3145732
  692.8 11.0 slice-start
  693.7 10.1 slice-start.1
  712.7 16.8 %copy-start.11 = (bf16[4,2,2048,4,64]{2,4,3,1,0:T(8,128)(2,1)}, bf16[4,2,2048,4,64]{2,4,3,1,0:T(8,128)(2,1)S(1)}, u32[]{:S(2)}) copy-start(bf16[4,2,2048,4,64]{2,4,3,1,0:T(8,128)(2,1)S(1)} %bitcast_dynamic-update-slice_fusion.11) | copy-start | bytes 25165828 | tf_op jit(solution)/shard_map/while
  751.4 11.0 slice-start
  771.3 16.8 %copy-start.11 = (bf16[4,2,2048,4,64]{2,4,3,1,0:T(8,128)(2,1)}, bf16[4,2,2048,4,64]{2,4,3,1,0:T(8,128)(2,1)S(1)}, u32[]{:S(2)}) copy-start(bf16[4,2,2048,4,64]{2,4,3,1,0:T(8,128)(2,1)S(1)} %bitcast_dynamic-update-slice_fusion.11) | copy-start | bytes 25165828 | tf_op jit(solution)/shard_map/while
  809.9 11.0 slice-start
  829.9 16.8 %copy-start.11 = (bf16[4,2,2048,4,64]{2,4,3,1,0:T(8,128)(2,1)}, bf16[4,2,2048,4,64]{2,4,3,1,0:T(8,128)(2,1)S(1)}, u32[]{:S(2)}) copy-start(bf16[4,2,2048,4,64]{2,4,3,1,0:T(8,128)(2,1)S(1)} %bitcast_dynamic-update-slice_fusion.11) | copy-start | bytes 25165828 | tf_op jit(solution)/shard_map/while
  868.5 11.0 slice-start
  888.4 16.8 %copy-start.11 = (bf16[4,2,2048,4,64]{2,4,3,1,0:T(8,128)(2,1)}, bf16[4,2,2048,4,64]{2,4,3,1,0:T(8,128)(2,1)S(1)}, u32[]{:S(2)}) copy-start(bf16[4,2,2048,4,64]{2,4,3,1,0:T(8,128)(2,1)S(1)} %bitcast_dynamic-update-slice_fusion.11) | copy-start | bytes 25165828 | tf_op jit(solution)/shard_map/while
  961.9 519.0 %all-reduce.4.cloned.1.call-start = ((), (), s32[]{:S(2)}) async-start(), calls=%async_computation.15 | async-start | bytes 12845056 | tf_op jit(solution)/shard_map/psum | solution.py:319
  1266.2 260.7 %reduce-scatter.14.cloned.1.call-start = ((), (), s32[]{:S(2)}) async-start(), calls=%async_computation.14 | async-start | bytes 5242880 | tf_op jit(solution)/shard_map/reduce_scatter | solution.py:308
  1273.6 301.1 %reduce-scatter.8.cloned.1.call-start = ((), (), s32[]{:S(2)}) async-start(), calls=%async_computation.9 | async-start | bytes 5242880 | tf_op jit(solution)/shard_map/reduce_scatter | solution.py:200
  1490.4 36.5 %copy-start.27 = (f32[1024]{0:T(1024)S(1)}, f32[1024]{0:T(1024)}, u32[]{:S(2)}) copy-start(f32[1024]{0:T(1024)} %copy-done.26) | copy-start | bytes 12292
  1490.4 36.5 %copy-start.32 = (f32[2,256]{1,0:T(2,128)S(1)}, f32[2,256]{1,0:T(2,128)}, u32[]{:S(2)}) copy-start(f32[2,256]{1,0:T(2,128)} %copy-done.31) | copy-start | bytes 6148
  1490.4 84.3 %copy-start.2 = (f32[2,256,1024]{2,1,0:T(8,128)S(1)}, f32[2,256,1024]{2,1,0:T(8,128)}, u32[]{:S(2)}) copy-start(f32[2,256,1024]{2,1,0:T(8,128)} %copy-done.1) | copy-start | bytes 6291460
  1490.4 84.3 %copy-start.25 = (f32[1024]{0:T(1024)S(1)}, f32[1024]{0:T(1024)}, u32[]{:S(2)}) copy-start(f32[1024]{0:T(1024)} %copy-done.24) | copy-start | bytes 12292
  1490.4 84.3 %copy-start.29 = (f32[2,256]{1,0:T(2,128)S(1)}, f32[2,256]{1,0:T(2,128)}, u32[]{:S(2)}) copy-start(f32[2,256]{1,0:T(2,128)} %copy-done.28) | copy-start | bytes 6148
  (38 other events, 165.7 us)
Sparse Core Ops, SparseCore 0:
  12.9 37.1 all-gather.5
  72.1 227.2 all-gather.7
  412.3 69.5 reduce-scatter.5
  485.7 34.4 all-gather.9
  521.6 34.4 all-gather.11
  576.0 71.4 reduce-scatter.9
  652.7 34.4 all-gather.13
  962.0 279.4 reduce-scatter.11
  1266.3 214.5 all-reduce.3
  1483.3 43.5 reduce-scatter.13
  1529.4 45.2 reduce-scatter.7
where the time goes:
time: 1590 us
  waiting for transfers between devices  981 us (62%)
  matrix products  308 us (19%)
  other arithmetic  150 us (9%)
  local copies, waits for them, and re-layouts  90 us (6%)
  blocking collectives  40.2 us (3%)
    reduce_scatter x1, waiting for transfers between devices, shards(): lax.psum_scatter(key_terms.astype(jnp.bfloat16), 'seq', scatter_dimension...  262 us
    all_gather x1, waiting for transfers between devices, shards(): both_all = lax.all_gather(both_own, 'seq', axis=1, tiled=True)  225 us
    psum x1, waiting for transfers between devices, shards(): lax.psum(stacked_grad.astype(jnp.bfloat16), 'seq').astype(jnp.float32)  193 us
    reduce_scatter x1, waiting for transfers between devices, shards(): lax.psum_scatter(jnp.einsum('rtf,df->rtd', gate_g, gate_weight, preferred...  71.5 us
    reduce_scatter x1, waiting for transfers between devices, shards(): lax.psum_scatter(jnp.einsum('rte,ed->rtd', piece, output_weight, preferre...  69.1 us
    dot_general x4, matrix products, back_block(): jnp.einsum('gqhd,gkhd->ghqk', grad_block, value_block, preferred_element_...  67 us
    dot_general x8, matrix products, score_block(): jnp.einsum('gqhd,gkhd->ghqk', query_block, key_block, preferred_element_t...  59.7 us
    convert_element_type x4, other arithmetic, back_block(): score_grad = (probs_full * (prob_grad - centre)).astype(jnp.bfloat16)  48.3 us
  transfers between devices with their start and end apart: 11, of which 11 were waited for; matrix products, arithmetic and copies ran while one was open for 5% of the time, Pallas kernels for 0%

commit v1 on v0

--- a/solution.py
+++ b/solution.py
@@ -1,10 +1,19 @@
+import functools
+import math
+
 import jax
 import jax.numpy as jnp
 from jax import lax
+from jax.experimental import pallas as pl
+from jax.experimental.pallas import tpu as pltpu
 from jax.sharding import PartitionSpec as P
 
 HD = 64
 ROW = 2048
+BLOCK = 256
+LOG2E = math.log2(math.e)
+LN2 = math.log(2.0)
+MESH = pl.DeviceIdType.MESH
 
 
 norm_eps = 1e-06
@@ -67,24 +76,330 @@
     return (extra, jnp.sum(grads_in * unit_rows, axis=(0, 1)))
 
 
-def allowed_for(seg_query, place_query, seg_keys, place_keys):
-    return (seg_query[:, :, None] == seg_keys[:, None, :]) & (
-        place_keys[None, None, :] <= place_query[None, :, None]
-    )
-
-
-def score_block(query_block, key_block, allowed):
-    raw = jnp.einsum(
-        "gqhd,gkhd->ghqk", query_block, key_block, preferred_element_type=jnp.float32
-    ) * HD ** (-0.5)
-    return jnp.where(allowed[:, None], raw, masked_score)
-
-
-def prob_block(query_block, key_block, logsum_block, allowed):
-    return jnp.exp(
-        score_block(query_block, key_block, allowed)
-        - jnp.transpose(logsum_block, (0, 2, 1))[..., None]
-    )
+def rows_dot(left, right):
+    return lax.dot_general(left, right, (((1,), (1,)), ((), ())), preferred_element_type=jnp.float32)
+
+
+def plain_dot(left, right):
+    return lax.dot_general(left, right, (((1,), (0,)), ((), ())), preferred_element_type=jnp.float32)
+
+
+def head_masked(block, head, heads):
+    if heads == 1:
+        return block
+    lanes = lax.broadcasted_iota(jnp.int32, block.shape, 1)
+    return jnp.where(lanes // HD == head, block, jnp.zeros_like(block))
+
+
+def attend_kernel(low_ref, q_ref, k_ref, v_ref, start_ref, o_ref, lse_ref, v_cols):
+    row = pl.program_id(0)
+    length, lanes = q_ref.shape[1:]
+    heads = lanes // HD
+    blocks = length // BLOCK
+    for j in range(blocks):
+        v_cols[:, j * BLOCK : (j + 1) * BLOCK] = v_ref[0, j * BLOCK : (j + 1) * BLOCK, :].T
+
+    def query_block(i, carry):
+        first = pl.multiple_of(i * BLOCK, BLOCK)
+        q_block = q_ref[0, pl.ds(first, BLOCK), :]
+        q_heads = [head_masked(q_block, h, heads) for h in range(heads)]
+        start = start_ref[0, :, pl.ds(first, BLOCK)]
+        places = first + lax.broadcasted_iota(jnp.int32, (1, BLOCK), 1)
+
+        def key_block(j, state):
+            at = pl.multiple_of(j * BLOCK, BLOCK)
+            k_block = k_ref[0, pl.ds(at, BLOCK), :]
+            keys = at + lax.broadcasted_iota(jnp.int32, (BLOCK, BLOCK), 0)
+            allowed = (keys >= start) & (keys <= places)
+            out = []
+            for h in range(heads):
+                top, total, acc = state[h]
+                scores = jnp.where(allowed, rows_dot(k_block, q_heads[h]), masked_score)
+                new_top = jnp.maximum(top, jnp.max(scores, axis=0, keepdims=True))
+                weights = jnp.exp2(scores - new_top)
+                shrink = jnp.exp2(top - new_top)
+                total = total * shrink + jnp.sum(weights, axis=0, keepdims=True)
+                acc = acc * shrink + plain_dot(
+                    v_cols[h * HD : (h + 1) * HD, pl.ds(at, BLOCK)], weights.astype(jnp.bfloat16)
+                )
+                out.append((new_top, total, acc))
+            return tuple(out)
+
+        begin = tuple(
+            (
+                jnp.full((1, BLOCK), masked_score, jnp.float32),
+                jnp.zeros((1, BLOCK), jnp.float32),
+                jnp.zeros((HD, BLOCK), jnp.float32),
+            )
+            for _ in range(heads)
+        )
+        state = key_block(i, begin)
+        state = lax.fori_loop(low_ref[row * blocks + i], i, key_block, state)
+        columns = jnp.concatenate([acc / total for _, total, acc in state], axis=0)
+        o_ref[0, pl.ds(first, BLOCK), :] = columns.T.astype(jnp.bfloat16)
+        for h in range(heads):
+            top, total, _ = state[h]
+            lse_ref[0, 0, pl.ds(h, 1), pl.ds(first, BLOCK)] = top + jnp.log2(total)
+        return carry
+
+    lax.fori_loop(0, blocks, query_block, 0)
+
+
+def attend(low, queries, keys, values, starts):
+    rows, length, width = queries.shape
+    lanes = min(width, 128)
+    groups = width // lanes
+    heads = lanes // HD
+    wide = pl.BlockSpec((1, length, lanes), lambda r, g, low: (r, 0, g))
+    return pl.pallas_call(
+        attend_kernel,
+        grid_spec=pltpu.PrefetchScalarGridSpec(
+            num_scalar_prefetch=1,
+            grid=(rows, groups),
+            in_specs=[wide, wide, wide, pl.BlockSpec((1, 1, length), lambda r, g, low: (r, 0, 0))],
+            out_specs=[
+                wide,
+                pl.BlockSpec((1, 1, heads, length), lambda r, g, low: (r, g, 0, 0)),
+            ],
+            scratch_shapes=[pltpu.VMEM((lanes, length), jnp.bfloat16)],
+        ),
+        out_shape=[
+            jax.ShapeDtypeStruct(queries.shape, jnp.bfloat16),
+            jax.ShapeDtypeStruct((rows, groups, heads, length), jnp.float32),
+        ],
+        name="attend",
+    )(low, queries, keys, values, starts)
+
+
+def attend_back_kernel(
+    low_ref, q_ref, k_ref, v_ref, o_ref, g_ref, lse_ref, start_ref,
+    qg_ref, kg_ref, vg_ref, k_cols, k_acc, v_acc,
+):
+    row = pl.program_id(0)
+    length, lanes = q_ref.shape[1:]
+    heads = lanes // HD
+    blocks = length // BLOCK
+    for j in range(blocks):
+        k_cols[:, j * BLOCK : (j + 1) * BLOCK] = k_ref[0, j * BLOCK : (j + 1) * BLOCK, :].T
+    k_acc[...] = jnp.zeros_like(k_acc)
+    v_acc[...] = jnp.zeros_like(v_acc)
+    select = (
+        lax.broadcasted_iota(jnp.int32, (8, lanes), 1) // HD
+        == lax.broadcasted_iota(jnp.int32, (8, lanes), 0)
+    ).astype(jnp.float32)
+
+    def query_block(i, carry):
+        first = pl.multiple_of(i * BLOCK, BLOCK)
+        q_block = q_ref[0, pl.ds(first, BLOCK), :]
+        g_block = g_ref[0, pl.ds(first, BLOCK), :]
+        q_heads = [head_masked(q_block, h, heads) for h in range(heads)]
+        g_heads = [head_masked(g_block, h, heads) for h in range(heads)]
+        product = g_block.astype(jnp.float32) * o_ref[0, pl.ds(first, BLOCK), :].astype(jnp.float32)
+        centre = lax.dot_general(
+            select, product, (((1,), (1,)), ((), ())),
+            precision=lax.Precision.HIGHEST, preferred_element_type=jnp.float32,
+        )
+        lse = lse_ref[0, 0, :, pl.ds(first, BLOCK)]
+        start = start_ref[0, :, pl.ds(first, BLOCK)]
+        places = first + lax.broadcasted_iota(jnp.int32, (1, BLOCK), 1)
+
+        def key_block(j, state):
+            at = pl.multiple_of(j * BLOCK, BLOCK)
+            k_block = k_ref[0, pl.ds(at, BLOCK), :]
+            v_block = v_ref[0, pl.ds(at, BLOCK), :]
+            keys = at + lax.broadcasted_iota(jnp.int32, (BLOCK, BLOCK), 0)
+            allowed = (keys >= start) & (keys <= places)
+            k_add = jnp.zeros((BLOCK, lanes), jnp.float32)
+            v_add = jnp.zeros((BLOCK, lanes), jnp.float32)
+            out = []
+            for h in range(heads):
+                scores = jnp.where(allowed, rows_dot(k_block, q_heads[h]), masked_score)
+                probs = jnp.exp2(scores - lse[h : h + 1, :])
+                prob_g = rows_dot(v_block, g_heads[h])
+                score_g = (probs * (prob_g - centre[h : h + 1, :])).astype(jnp.bfloat16)
+                v_add = v_add + plain_dot(probs.astype(jnp.bfloat16), g_heads[h])
+                k_add = k_add + plain_dot(score_g, q_heads[h])
+                out.append(
+                    state[h] + plain_dot(k_cols[h * HD : (h + 1) * HD, pl.ds(at, BLOCK)], score_g)
+                )
+            k_acc[pl.ds(at, BLOCK), :] += k_add
+            v_acc[pl.ds(at, BLOCK), :] += v_add
+            return tuple(out)
+
+        begin = tuple(jnp.zeros((HD, BLOCK), jnp.float32) for _ in range(heads))
+        state = lax.fori_loop(low_ref[row * blocks + i], i + 1, key_block, begin)
+        columns = jnp.concatenate(state, axis=0) * HD ** (-0.5)
+        qg_ref[0, pl.ds(first, BLOCK), :] = columns.T.astype(jnp.bfloat16)
+        return carry
+
+    lax.fori_loop(0, blocks, query_block, 0)
+    kg_ref[0] = (k_acc[...] * LN2).astype(jnp.bfloat16)
+    vg_ref[0] = v_acc[...].astype(jnp.bfloat16)
+
+
+def attend_back(low, queries, keys, values, attended, grads, lse, starts):
+    rows, length, width = queries.shape
+    lanes = min(width, 128)
+    groups = width // lanes
+    heads = lanes // HD
+    wide = pl.BlockSpec((1, length, lanes), lambda r, g, low: (r, 0, g))
+    return pl.pallas_call(
+        attend_back_kernel,
+        grid_spec=pltpu.PrefetchScalarGridSpec(
+            num_scalar_prefetch=1,
+            grid=(rows, groups),
+            in_specs=[wide] * 5
+            + [
+                pl.BlockSpec((1, 1, heads, length), lambda r, g, low: (r, g, 0, 0)),
+                pl.BlockSpec((1, 1, length), lambda r, g, low: (r, 0, 0)),
+            ],
+            out_specs=[wide] * 3,
+            scratch_shapes=[
+                pltpu.VMEM((lanes, length), jnp.bfloat16),
+                pltpu.VMEM((length, lanes), jnp.float32),
+                pltpu.VMEM((length, lanes), jnp.float32),
+            ],
+        ),
+        out_shape=[jax.ShapeDtypeStruct(queries.shape, jnp.bfloat16)] * 3,
+        name="attend_back",
+    )(low, queries, keys, values, attended, grads, lse, starts)
+
+
+def exchange(arrays, out_shapes, plan, number):
+    count = len(arrays)
+
+    def kernel(*refs):
+        sources, targets = refs[:count], refs[count : 2 * count]
+        local_sem, send_sem, receive_sem = refs[2 * count :]
+        me = (lax.axis_index("seq"), lax.axis_index("tp"))
+        sends, receives = plan(*me)
+        barrier = pltpu.get_barrier_semaphore()
+
+        def is_me(place):
+            return (place[0] == me[0]) & (place[1] == me[1])
+
+        for origin, _, _ in receives:
+            @pl.when(jnp.logical_not(is_me(origin)))
+            def _():
+                pl.semaphore_signal(barrier, inc=1, device_id=origin, device_id_type=MESH)
+        others = sum(jnp.where(is_me(destination), 0, 1) for destination, _, _, _ in sends)
+        pl.semaphore_wait(barrier, others)
+
+        def remote(a, n, destination, source, target, at):
+            return pltpu.make_async_remote_copy(
+                src_ref=sources[a].at[source],
+                dst_ref=targets[a].at[target],
+                send_sem=send_sem.at[n * count + a],
+                recv_sem=receive_sem.at[at * count + a],
+                device_id=destination,
+                device_id_type=MESH,
+            )
+
+        def local(a, n, source, target):
+            return pltpu.make_async_copy(
+                sources[a].at[source], targets[a].at[target], local_sem.at[n * count + a]
+            )
+
+        for wait in (False, True):
+            for n, (destination, source, target, at) in enumerate(sends):
+                for a in range(count):
+                    @pl.when(is_me(destination))
+                    def _():
+                        copy = local(a, n, source, target)
+                        copy.wait() if wait else copy.start()
+
+                    @pl.when(jnp.logical_not(is_me(destination)))
+                    def _():
+                        copy = remote(a, n, destination, source, target, at)
+                        copy.wait_send() if wait else copy.start()
+        for origin, target, at in receives:
+            for a in range(count):
+                @pl.when(jnp.logical_not(is_me(origin)))
+                def _():
+                    pltpu.make_async_remote_copy(
+                        src_ref=targets[a].at[target],
+                        dst_ref=targets[a].at[target],
+                        send_sem=send_sem.at[0],
+                        recv_sem=receive_sem.at[at * count + a],
+                        device_id=origin,
+                        device_id_type=MESH,
+                    ).wait_recv()
+
+    total = len(plan(0, 0)[0]) * count
+    return pl.pallas_call(
+        kernel,
+        out_shape=[jax.ShapeDtypeStruct(shape, jnp.bfloat16) for shape in out_shapes],
+        in_specs=[pl.BlockSpec(memory_space=pl.ANY)] * count,
+        out_specs=[pl.BlockSpec(memory_space=pl.ANY)] * count,
+        scratch_shapes=[
+            pltpu.SemaphoreType.DMA((total,)),
+            pltpu.SemaphoreType.DMA((total,)),
+            pltpu.SemaphoreType.DMA((total,)),
+        ],
+        compiler_params=pltpu.CompilerParams(collective_id=number, has_side_effects=True),
+        name=f"exchange_{number}",
+    )(*arrays)
+
+
+def places_to_rows(seq_size, rows_each):
+    def plan(s, t):
+        sends, receives = [], []
+        for i in range(seq_size):
+            other = lax.rem(s + i, seq_size)
+            sends.append(((other, t), (pl.ds(other * rows_each, rows_each),), (slice(None), s), s))
+            origin = lax.rem(s + seq_size - i, seq_size)
+            receives.append(((origin, t), (slice(None), origin), origin))
+        return sends, receives
+
+    return plan
+
+
+def rows_to_places(seq_size, rows_each):
+    def plan(s, t):
+        sends, receives = [], []
+        for i in range(seq_size):
+            other = lax.rem(s + i, seq_size)
+            sends.append(((other, t), (slice(None), other), (pl.ds(s * rows_each, rows_each),), s))
+            origin = lax.rem(s + seq_size - i, seq_size)
+            receives.append(((origin, t), (pl.ds(origin * rows_each, rows_each),), origin))
+        return sends, receives
+
+    return plan
+
+
+def heads_to_owner(seq_size, tp_size, rows_each, rows_local):
+    def plan(s, t):
+        sends, receives = [], []
+        for i in range(seq_size):
+            other = lax.rem(s + i, seq_size)
+            for j in range(rows_each):
+                row = s * rows_each + j
+                slot = lax.rem(row, rows_local)
+                sends.append(((other, row // rows_local), (j, other), (t, slot), t * rows_local + slot))
+        for i in range(tp_size):
+            for slot in range(rows_local):
+                row = t * rows_local + slot
+                receives.append(((row // rows_each, i), (i, slot), i * rows_local + slot))
+        return sends, receives
+
+    return plan
+
+
+def owner_to_heads(seq_size, tp_size, rows_each, rows_local):
+    def plan(s, t):
+        sends, receives = [], []
+        for i in range(tp_size):
+            for slot in range(rows_local):
+                row = t * rows_local + slot
+                j = lax.rem(row, rows_each)
+                sends.append(((row // rows_each, i), (i, slot), (j, s), j * seq_size + s))
+        for j in range(rows_each):
+            row = s * rows_each + j
+            for i in range(seq_size):
+                receives.append(((i, row // rows_local), (j, i), j * seq_size + i))
+        return sends, receives
+
+    return plan
 
 
 def shards(
@@ -106,22 +421,10 @@
     row_count = first_values.shape[0]
     width_local = query_weight.shape[0]
     head_count = width_local // HD
-    group_rows = min(row_count, max(1, 512 // local_len))
-    block_count = row_count // group_rows
-    score_scale = HD ** (-0.5)
-
-    def blocked(array_in):
-        return array_in.reshape((block_count, group_rows) + array_in.shape[1:])
-
-    def unblocked(array_in):
-        return array_in.reshape((row_count,) + array_in.shape[2:])
-
-    segment, offsets = doc_layout(doc_lengths)
+    _, offsets = doc_layout(doc_lengths)
     begin = lax.axis_index("seq") * local_len
-    seg_own = lax.dynamic_slice_in_dim(segment, begin, local_len, 1)
     off_own = lax.dynamic_slice_in_dim(offsets, begin, local_len, 1)
     places_all = jnp.arange(ROW, dtype=jnp.int32)
-    places_own = begin + jnp.arange(local_len, dtype=jnp.int32)
     tables = rotary_tables(off_own)
     attn_scale = attn_gain.astype(jnp.float32)
     feed_scale = feed_gain.astype(jnp.float32)
@@ -134,8 +437,9 @@
     projected = jnp.einsum(
         "rtd,ed->rte", normed_all, stacked_weights, preferred_element_type=jnp.float32
     )
-    queries = rotate(
-        projected[..., :width_local].reshape(row_count, local_len, head_count, HD), tables
+    queries = (
+        rotate(projected[..., :width_local].reshape(row_count, local_len, head_count, HD), tables)
+        * (HD ** (-0.5) * LOG2E)
     ).astype(jnp.bfloat16)
     keys_rot = rotate(
         projected[..., width_local : 2 * width_local].reshape(row_count, local_len, head_count, HD),
@@ -144,47 +448,39 @@
     mixed = (0.5 * projected[..., 2 * width_local :] + 0.5 * first_rows.astype(jnp.float32)).astype(
         jnp.bfloat16
     )
-    both_own = jnp.concatenate(
-        [keys_rot.reshape(row_count, local_len, width_local), mixed], axis=-1
-    )
-    both_all = lax.all_gather(both_own, "seq", axis=1, tiled=True)
-    keys_all = both_all[..., :width_local].reshape(row_count, ROW, head_count, HD)
-    values_all = both_all[..., width_local:].reshape(row_count, ROW, head_count, HD)
-
-    def attend_block(pieces):
-        query_block, key_block, value_block, seg_query, seg_keys = pieces
-        scores = score_block(
-            query_block, key_block, allowed_for(seg_query, places_own, seg_keys, places_all)
+    seq_size = lax.axis_size("seq")
+    tp_size = lax.axis_size("tp")
+    rows_local = layer_input.shape[0]
+    rows_each = row_count // seq_size
+    rows_shape = (rows_each, seq_size, local_len, width_local)
+    my_rows = lax.axis_index("seq") * rows_each
+    starts = lax.dynamic_slice_in_dim(places_all[None, :] - offsets, my_rows, rows_each, 0)
+    low = (starts[:, ::BLOCK] // BLOCK).reshape(-1)
+    starts = starts[:, None, :]
+    queries, keys, values = (
+        part.reshape(rows_each, ROW, width_local)
+        for part in exchange(
+            [
+                queries.reshape(row_count, local_len, width_local),
+                keys_rot.reshape(row_count, local_len, width_local),
+                mixed,
+            ],
+            [rows_shape] * 3,
+            places_to_rows(seq_size, rows_each),
+            0,
         )
-        highest = jnp.max(scores, axis=-1, keepdims=True)
-        weights = jnp.exp(scores - highest)
-        totals = jnp.sum(weights, axis=-1, keepdims=True)
-        softmax_low = (weights / totals).astype(jnp.bfloat16)
-        result_block = jnp.einsum(
-            "ghqk,gkhd->gqhd", softmax_low, value_block, preferred_element_type=jnp.float32
-        )
-        return (result_block, jnp.transpose((highest + jnp.log(totals))[..., 0], (0, 2, 1)))
-
-    attended_blocks, logsum_blocks = lax.map(
-        attend_block,
-        (
-            blocked(queries),
-            blocked(keys_all),
-            blocked(values_all),
-            blocked(seg_own),
-            blocked(segment),
-        ),
-    )
-    attended = (
-        unblocked(attended_blocks).reshape(row_count, local_len, width_local).astype(jnp.bfloat16)
-    )
-    logsum = unblocked(logsum_blocks)
-    piece = attended
-    middle = source + lax.psum_scatter(
-        jnp.einsum("rte,ed->rtd", piece, output_weight, preferred_element_type=jnp.float32),
-        "tp",
-        scatter_dimension=0,
-        tiled=True,
+    )
+    result, logsum = attend(low, queries, keys, values, starts)
+    (pieces,) = exchange(
+        [result.reshape(rows_shape)],
+        [(tp_size, rows_local, local_len, width_local)],
+        heads_to_owner(seq_size, tp_size, rows_each, rows_local),
+        1,
+    )
+    attended = jnp.transpose(pieces, (1, 2, 0, 3)).reshape(rows_local, local_len, -1)
+    output_full = lax.all_gather(output_weight, "tp", axis=0, tiled=True)
+    middle = source + jnp.einsum(
+        "rte,ed->rtd", attended, output_full, preferred_element_type=jnp.float32
     )
     unit_feed, inv_feed = norm_rows(middle)
     feed_in = (unit_feed * feed_scale).astype(jnp.bfloat16)
@@ -217,79 +513,50 @@
     gate_grad = jnp.einsum("rtd,rtf->df", feed_all, gate_g, preferred_element_type=jnp.float32)
     up_grad = jnp.einsum("rtd,rtf->df", feed_all, up_g, preferred_element_type=jnp.float32)
     feed_in_g = lax.psum_scatter(
-        jnp.einsum("rtf,df->rtd", gate_g, gate_weight, preferred_element_type=jnp.float32)
-        + jnp.einsum("rtf,df->rtd", up_g, up_weight, preferred_element_type=jnp.float32),
+        (
+            jnp.einsum("rtf,df->rtd", gate_g, gate_weight, preferred_element_type=jnp.float32)
+            + jnp.einsum("rtf,df->rtd", up_g, up_weight, preferred_element_type=jnp.float32)
+        ).astype(jnp.bfloat16),
         "tp",
         scatter_dimension=0,
         tiled=True,
-    )
+    ).astype(jnp.float32)
     middle_extra, feed_gain_part = norm_back(feed_in_g, unit_feed, inv_feed, feed_scale)
     middle_g = cotangent + middle_extra
-    branch_all = lax.all_gather(middle_g.astype(jnp.bfloat16), "tp", axis=0, tiled=True)
-    output_proj_grad = jnp.einsum(
-        "rte,rtd->ed", attended, branch_all, preferred_element_type=jnp.float32
+    branch_g = middle_g.astype(jnp.bfloat16)
+    output_proj_grad = lax.psum_scatter(
+        jnp.einsum("rte,rtd->ed", attended, branch_g, preferred_element_type=jnp.float32).astype(
+            jnp.bfloat16
+        ),
+        "tp",
+        scatter_dimension=0,
+        tiled=True,
     )
     attended_g = jnp.einsum(
-        "rtd,ed->rte", branch_all, output_weight, preferred_element_type=jnp.float32
+        "rtd,ed->rte", branch_g, output_full, preferred_element_type=jnp.float32
     ).astype(jnp.bfloat16)
-    grad_heads = attended_g.reshape(row_count, local_len, head_count, HD)
-
-    def back_block(pieces):
-        query_block, key_block, value_block, grad_block, logsum_block, seg_query, seg_keys = pieces
-        probs_full = prob_block(
-            query_block,
-            key_block,
-            logsum_block,
-            allowed_for(seg_query, places_own, seg_keys, places_all),
-        )
-        prob_grad = jnp.einsum(
-            "gqhd,gkhd->ghqk", grad_block, value_block, preferred_element_type=jnp.float32
-        )
-        centre = jnp.sum(probs_full * prob_grad, axis=-1, keepdims=True)
-        score_grad = (probs_full * (prob_grad - centre)).astype(jnp.bfloat16)
-        query_part = (
-            jnp.einsum("ghqk,gkhd->gqhd", score_grad, key_block, preferred_element_type=jnp.float32)
-            * score_scale
-        )
-        key_part = (
-            jnp.einsum(
-                "ghqk,gqhd->gkhd", score_grad, query_block, preferred_element_type=jnp.float32
+    (attended_g,) = exchange(
+        [
+            jnp.transpose(
+                attended_g.reshape(rows_local, local_len, tp_size, width_local), (2, 0, 1, 3)
             )
-            * score_scale
-        )
-        value_part = jnp.einsum(
-            "ghqk,gqhd->gkhd",
-            probs_full.astype(jnp.bfloat16),
-            grad_block,
-            preferred_element_type=jnp.float32,
-        )
-        return (query_part, key_part, value_part)
-
-    query_blocks, key_blocks, value_blocks = lax.map(
-        back_block,
-        (
-            blocked(queries),
-            blocked(keys_all),
-            blocked(values_all),
-            blocked(grad_heads),
-            blocked(logsum),
-            blocked(seg_own),
-            blocked(segment),
-        ),
-    )
-    query_g = unblocked(query_blocks)
-    key_terms = jnp.concatenate(
-        [
-            unblocked(key_blocks).reshape(row_count, ROW, width_local),
-            unblocked(value_blocks).reshape(row_count, ROW, width_local),
         ],
-        axis=-1,
-    )
-    key_sums = lax.psum_scatter(
-        key_terms.astype(jnp.bfloat16), "seq", scatter_dimension=1, tiled=True
-    ).astype(jnp.float32)
-    keys_own_g = key_sums[..., :width_local]
-    values_own_g = key_sums[..., width_local:]
+        [rows_shape],
+        owner_to_heads(seq_size, tp_size, rows_each, rows_local),
+        2,
+    )
+    query_rows, key_rows, value_rows = attend_back(
+        low, queries, keys, values, result, attended_g.reshape(result.shape), logsum, starts
+    )
+    query_own_g, keys_own_g, values_own_g = exchange(
+        [query_rows.reshape(rows_shape), key_rows.reshape(rows_shape), value_rows.reshape(rows_shape)],
+        [(row_count, local_len, width_local)] * 3,
+        rows_to_places(seq_size, rows_each),
+        3,
+    )
+    query_g = query_own_g.astype(jnp.float32).reshape(row_count, local_len, head_count, HD)
+    keys_own_g = keys_own_g.astype(jnp.float32)
+    values_own_g = values_own_g.astype(jnp.float32)
     first_grad = jnp.swapaxes(0.5 * values_own_g, 1, 2)
     value_low = (0.5 * values_own_g).astype(jnp.bfloat16)
     key_low = (

time: 1590 us -> 887 us (0.56)
  waiting for transfers between devices: 981 us -> 387 us
  Pallas kernels: 0 us -> 269 us
  matrix products: 308 us -> 81.1 us
  other arithmetic: 150 us -> 46.2 us
  local copies, waits for them, and re-layouts: 90 us -> 36.9 us
    reduce_scatter x3 -> x2, waiting for transfers between devices: 402 us -> 37.4 us  [the longest x1 37.4 us: shards(): lax.psum_scatter((jnp.einsum('rtf,df->rtd', gate_g, gate_weight, preferre...]
    pallas_call x0 -> x6, Pallas kernels: none -> 269 us  [the longest x4 197 us: exchange(): pl.pallas_call(kernel, out_shape=[jax.ShapeDtypeStruct(shape, jnp.bfloat1...]
    all_gather x2 -> x1, waiting for transfers between devices: 259 us -> 0.01 us  [shards(): output_full = lax.all_gather(output_weight, 'tp', axis=0, tiled=True)]
    dot_general x31 -> x3, matrix products: 234 us -> 10 us  [the longest x1 3.85 us: shards(): jnp.einsum('rtd,ed->rte', branch_g, output_full, preferred_element_type=j...]
    convert_element_type x6 -> x1, other arithmetic: 50.5 us -> 1.26 us  [shards(): queries = (rotate(projected[..., :width_local].reshape(row_count, local_l...]
    reduce_scatter x1, waiting for transfers between devices: 2.2 us -> 45 us  [shards(): lax.psum_scatter(jnp.einsum('rtf,fd->rtd', piece, down_weight, preferred_...]
    slice x5 -> x1, local copies, waits for them, and re-layouts: 39 us -> 0.1 us  [shards(): low = (starts[:, ::BLOCK] // BLOCK).reshape(-1)]
    another operation x2 -> x0, local copies, waits for them, and re-layouts: 22.8 us -> none  [the longest x1 11.4 us: shards(): unblocked(key_blocks).reshape(row_count, ROW, width_local)]
  transfers between devices with their start and end apart: 11 -> 9, of which waited for: 11 -> 7; matrix products, arithmetic and copies ran while one was open for 5% -> 13% of each run, Pallas kernels for 0% -> 31%
where the time goes in v1:
time: 887 us; the launch traced here: 879 us
  waiting for transfers between devices  387 us (44%)
  Pallas kernels  269 us (30%)
  matrix products  81.1 us (9%)
  other arithmetic  46.2 us (5%)
  blocking collectives  43.6 us (5%)
  local copies, waits for them, and re-layouts  36.9 us (4%)
  between operations  14.6 us (2%)
    pallas_call x4, Pallas kernels, exchange(): pl.pallas_call(kernel, out_shape=[jax.ShapeDtypeStruct(shape, jnp.bfloat1...  197 us
    psum x1, waiting for transfers between devices, shards(): lax.psum(stacked_grad.astype(jnp.bfloat16), 'seq').astype(jnp.float32)  173 us
    reduce_scatter x1, waiting for transfers between devices, shards(): lax.psum_scatter(jnp.einsum('rtf,fd->rtd', piece, down_weight, preferred_...  45 us
    psum x1, blocking collectives, shards(): small = lax.psum((attn_gain_part, feed_gain_part, squares), ('seq', 'tp'))  43.6 us
    all_gather x1, waiting for transfers between devices, shards(): feed_all = lax.all_gather(feed_in, 'tp', axis=0, tiled=True)  42.4 us
    reduce_scatter x1, waiting for transfers between devices, shards(): lax.psum_scatter((jnp.einsum('rtf,df->rtd', gate_g, gate_weight, preferre...  37.4 us
    pallas_call x1, Pallas kernels, attend_back(): pl.pallas_call(attend_back_kernel, grid_spec=pltpu.PrefetchScalarGridSpec...  36.5 us
    reduce_scatter x1, waiting for transfers between devices, shards(): lax.psum_scatter(jnp.einsum('rte,ed->rtd', piece, stacked_weights, prefer...  35.3 us
  transfers between devices with their start and end apart: 9, of which 7 were waited for; matrix products, arithmetic and copies ran while one was open for 13% of the time, Pallas kernels for 31%

profile of v1, /device:TPU:0, one launch (start us, length us, event | category | flops | bytes accessed | tf_op | source)
XLA Modules:
  0.0 879.4 jit_solution(9542023698148277663)
XLA Ops:
  19.4 30.1 %all-gather.5.cloned.1.call-done = bf16[8,256,1024]{2,1,0:T(8,128)(2,1)} async-done(((bf16[2,256,1024]{2,1,0:T(8,128)(2,1)}), bf16[8,256,1024]{2,1,0:T(8,128)(2,1)}) %all-gather.5.cloned.1.call-update) | async-done | bytes 4194320 | tf_op jit(solution)/shard_map/all_gather | solution.py:435
  49.5 5.7 fusion.45
  55.2 3.1 multiply_reduce_fusion
  58.3 3.3 copy.61
  73.3 56.2 %exchange_0.1 = (bf16[1,8,256,256]{3,2,1,0:T(8,128)(2,1)}, bf16[1,8,256,256]{3,2,1,0:T(8,128)(2,1)}, bf16[1,8,256,256]{3,2,1,0:T(8,128)(2,1)}) custom-call(bf16[8,256,256]{2,1,0:T(8,128)(2,1)} %copy.63.refs_0_, bf16[8,256,256]{2,1,0:T(8,128)(2,1)} %copy.64.refs_1_, bf16[8,256,256]{2,1,0:T(8,128)(2,1)} %get-tuple-element.100.refs_2_), custom_call_target="tpu_custom_call" | custom-call | tf_op jit(solution)/shard_map/exchange_0/pallas_call | solution.py:329
  129.6 35.0 %attend.1 = (bf16[1,2048,256]{2,1,0:T(8,128)(2,1)}, f32[1,2,2,2048]{3,2,1,0:T(2,128)}) custom-call(s32[8]{0:T(128)} %fusion.49.low_ref, bf16[1,2048,256]{2,1,0:T(8,128)(2,1)} %bitcast.104, bf16[1,2048,256]{2,1,0:T(8,128)(2,1)} %bitcast.106, bf16[1,2048,256]{2,1,0:T(8,128)(2,1)} %bitcast.108, s32[1,1,2048]{2,1,0:T(1,128)} %fusion.71.start_ref), custom_call_target="tpu_custom_call" | custom-call | tf_op jit(solution)/shard_map/attend/pallas_call | solution.py:154
  164.6 39.6 %exchange_1.1 = bf16[4,2,256,256]{3,2,1,0:T(8,128)(2,1)} custom-call(bf16[1,8,256,256]{3,2,1,0:T(8,128)(2,1)} %bitcast.110), custom_call_target="tpu_custom_call" | custom-call | tf_op jit(solution)/shard_map/exchange_1/pallas_call | solution.py:329
  206.5 3.5 multiply_reduce_fusion.1
  212.1 42.4 %all-gather.9.cloned.1.call-done = bf16[8,256,1024]{2,1,0:T(8,128)(2,1)} async-done(((bf16[2,256,1024]{2,1,0:T(8,128)(2,1)}), bf16[8,256,1024]{2,1,0:T(8,128)(2,1)}) %all-gather.9.cloned.1.call-update) | async-done | bytes 4194320 | tf_op jit(solution)/shard_map/all_gather | solution.py:487
  254.4 8.5 fusion.39
  262.9 5.0 fusion.43
  267.9 22.4 %all-gather.11.cloned.1.call-done = bf16[8,256,1024]{2,1,0:T(8,128)(2,1)} async-done(((bf16[2,256,1024]{2,1,0:T(8,128)(2,1)}), bf16[8,256,1024]{2,1,0:T(8,128)(2,1)}) %all-gather.11.cloned.1.call-update) | async-done | bytes 4194320 | tf_op jit(solution)/shard_map/all_gather | solution.py:506
  290.3 10.4 %multiply_convert_fusion = (bf16[8,256,704]{1,2,0:T(8,128)(2,1)S(1)}, bf16[8,256,704]{1,2,0:T(8,128)(2,1)S(1)}, bf16[8,256,704]{1,2,0:T(8,128)(2,1)}) fusion(f32[8,256,704]{1,2,0:T(8,128)} %fusion.43, f32[8,256,704]{1,2,0:T(8,128)} %fusion.39, bf16[8,256,1024]{2,1,0:T(8,128)(2,1)} %all-gather.11.cloned.1.call-done, bf16[704,1024]{1,0:T(8,128)(2,1)S(1)} %copy-done), kind=kOutput, calls=%fused_computation.1 | convolution fusion | flops 2974416896 | bytes 25821184 | tf_op jit(solution)/shard_map/rtd,fd->rtf/dot_general | solution.py:508
  300.8 3.5 fusion.41
  304.3 5.1 add_convert_fusion
  309.7 7.0 convolution_convert_fusion
  316.8 37.4 %reduce-scatter.7.cloned.1.call-done = bf16[2,256,1024]{2,1,0:T(8,128)(2,1)} async-done(((bf16[8,256,1024]{2,1,0:T(8,128)(2,1)}), bf16[2,256,1024]{2,1,0:T(8,128)(2,1)}) %reduce-scatter.7.cloned.1.call-update) | async-done | bytes 1048592 | tf_op jit(solution)/shard_map/reduce_scatter | solution.py:515
  356.2 45.0 %reduce-scatter.5.cloned.1.call-done = bf16[2,256,1024]{2,1,0:T(8,128)(2,1)} async-done(((bf16[8,256,1024]{2,1,0:T(8,128)(2,1)}), bf16[2,256,1024]{2,1,0:T(8,128)(2,1)}) %reduce-scatter.5.cloned.1.call-update) | async-done | bytes 1048592 | tf_op jit(solution)/shard_map/reduce_scatter | solution.py:496
  401.2 3.3 fusion.13
  410.1 3.8 fusion.32
  416.7 31.6 %exchange_2.1 = bf16[1,8,256,256]{3,2,1,0:T(8,128)(2,1)} custom-call(bf16[4,2,256,256]{3,2,1,0:T(8,128)(2,1)} %bitcast.102), custom_call_target="tpu_custom_call" | custom-call | tf_op jit(solution)/shard_map/exchange_2/pallas_call | solution.py:329
  448.3 36.5 %attend_back.1 = (bf16[1,2048,256]{2,1,0:T(8,128)(2,1)}, bf16[1,2048,256]{2,1,0:T(8,128)(2,1)}, bf16[1,2048,256]{2,1,0:T(8,128)(2,1)}) custom-call(s32[8]{0:T(128)} %fusion.49.low_ref, bf16[1,2048,256]{2,1,0:T(8,128)(2,1)} %bitcast.105, bf16[1,2048,256]{2,1,0:T(8,128)(2,1)} %bitcast.107, bf16[1,2048,256]{2,1,0:T(8,128)(2,1)} %bitcast.109, ...), custom_call_target="tpu_custom_call" | custom-call | tf_op jit(solution)/shard_map/attend_back/pallas_call | solution.py:246
  484.8 69.9 %exchange_3.1 = (bf16[8,256,256]{2,1,0:T(8,128)(2,1)}, bf16[8,256,256]{2,1,0:T(8,128)(2,1)}, bf16[8,256,256]{2,1,0:T(8,128)(2,1)}) custom-call(bf16[1,8,256,256]{3,2,1,0:T(8,128)(2,1)} %bitcast.116, bf16[1,8,256,256]{3,2,1,0:T(8,128)(2,1)} %bitcast.117, bf16[1,8,256,256]{3,2,1,0:T(8,128)(2,1)} %bitcast.118), custom_call_target="tpu_custom_call" | custom-call | tf_op jit(solution)/shard_map/exchange_3/pallas_call | solution.py:329
  567.7 3.1 fusion.28
  571.7 5.0 convolution_convert_fusion.1
  577.1 7.5 bitcast_convert_fusion.2
  584.6 4.2 bitcast_convert_fusion.3
  588.8 4.2 bitcast_convert_fusion.4
  593.0 5.0 bitcast_convert_fusion.1
  604.8 35.3 %reduce-scatter.9.cloned.1.call-done = bf16[2,256,1024]{2,1,0:T(8,128)(2,1)} async-done(((bf16[8,256,1024]{2,1,0:T(8,128)(2,1)}), bf16[2,256,1024]{2,1,0:T(8,128)(2,1)}) %reduce-scatter.9.cloned.1.call-update) | async-done | bytes 1048592 | tf_op jit(solution)/shard_map/reduce_scatter | solution.py:575
  642.2 43.6 %all-reduce = (f32[1024]{0:T(1024)}, f32[1024]{0:T(1024)}, f32[2]{0:T(128)S(1)}) all-reduce(f32[1024]{0:T(1024)S(1)} %get-tuple-element.89, f32[1024]{0:T(1024)S(1)} %get-tuple-element.87, f32[2]{0:T(128)S(1)} %pad_maximum_fusion.6), channel_id=1, replica_groups=mesh['seq'=8,'tp'=4] {'seq','tp'}, use_global_device_ids=true, to_apply=%region_10.11 | all-reduce | flops 2050 | bytes 16400 | tf_op jit(solution)/shard_map/psum | solution.py:595
  689.2 173.1 %all-reduce.4.cloned.1.call-done = (bf16[768,1024]{1,0:T(8,128)(2,1)}, bf16[256,1024]{1,0:T(8,128)(2,1)}, bf16[1024,704]{0,1:T(8,128)(2,1)}, bf16[1024,704]{0,1:T(8,128)(2,1)}, bf16[704,1024]{1,0:T(8,128)(2,1)}) async-done(((bf16[768,1024]{1,0:T(8,128)(2,1)}, bf16[256,1024]{1,0:T(8,128)(2,1)}, bf16[1024,704]{0,1:T(8,128)(2,1)}, bf16[1024,704]{0,1:T(8,128)(2,1)}, bf16[704,1024]{1,0:T(8,128)(2,1)}), ...) | async-done | bytes 6422544 | tf_op jit(solution)/shard_map/psum | solution.py:586
  (143 shorter events, 75.4 us)
Async XLA Ops:
  7.2 283.2 %copy-start = (bf16[704,1024]{1,0:T(8,128)(2,1)S(1)}, bf16[704,1024]{1,0:T(8,128)(2,1)}, u32[]{:S(2)}) copy-start(bf16[704,1024]{1,0:T(8,128)(2,1)} %param.24) | copy-start | bytes 4325380
  7.2 42.3 %all-gather.5.cloned.1.call-start = ((), (), s32[]{:S(2)}) async-start(), calls=%async_computation.4 | async-start | bytes 5242880 | tf_op jit(solution)/shard_map/all_gather | solution.py:435
  8.8 4.2 copy-start.24
  8.9 4.2 copy-start.23
  8.9 5.5 copy-start.16
  12.2 194.3 %all-gather.7.cloned.1.call-start = ((), (), s32[]{:S(2)}) async-start(), calls=%async_computation.5 | async-start | bytes 2621440 | tf_op jit(solution)/shard_map/all_gather | solution.py:481
  12.9 241.5 %all-gather.9.cloned.1.call-start = ((), (), s32[]{:S(2)}) async-start(), calls=%async_computation.6 | async-start | bytes 5242880 | tf_op jit(solution)/shard_map/all_gather | solution.py:487
  14.9 40.4 %copy-start.3 = (bf16[8,256,256]{1,2,0:T(8,128)(2,1)}, bf16[8,256,256]{1,2,0:T(8,128)(2,1)S(1)}, u32[]{:S(2)}) copy-start(bf16[8,256,256]{1,2,0:T(8,128)(2,1)S(1)} %copy.62) | copy-start | bytes 3145732
  211.3 79.1 %all-gather.11.cloned.1.call-start = ((), (), s32[]{:S(2)}) async-start(), calls=%async_computation.8 | async-start | bytes 5242880 | tf_op jit(solution)/shard_map/all_gather | solution.py:506
  211.8 142.4 %reduce-scatter.7.cloned.1.call-start = ((), (), s32[]{:S(2)}) async-start(), calls=%async_computation.9 | async-start | bytes 5242880 | tf_op jit(solution)/shard_map/reduce_scatter | solution.py:515
  254.4 8.5 copy-start.26
  254.4 8.5 copy-start.28
  290.3 10.5 %copy-start.29 = (bf16[1024,704]{0,1:T(8,128)(2,1)S(1)}, bf16[1024,704]{0,1:T(8,128)(2,1)}, u32[]{:S(2)}) copy-start(bf16[1024,704]{0,1:T(8,128)(2,1)} %param.22) | copy-start | bytes 4325380
  300.8 3.5 copy-start.30
  309.4 91.7 %reduce-scatter.5.cloned.1.call-start = ((), (), s32[]{:S(2)}) async-start(), calls=%async_computation.7 | async-start | bytes 5242880 | tf_op jit(solution)/shard_map/reduce_scatter | solution.py:496
  316.7 84.5 %copy-start.9 = (bf16[2,256,1024]{2,1,0:T(8,128)(2,1)S(1)}, bf16[2,256,1024]{2,1,0:T(8,128)(2,1)}, u32[]{:S(2)}) copy-start(bf16[2,256,1024]{2,1,0:T(8,128)(2,1)} %param.25) | copy-start | bytes 3145732
  316.7 281.3 %reduce-scatter.11.cloned.1.call-start = ((), (), s32[]{:S(2)}) async-start(), calls=%async_computation.11 | async-start | bytes 2621440 | tf_op jit(solution)/shard_map/reduce_scatter | solution.py:527
  401.2 4.7 copy-start.10
  408.5 231.6 %reduce-scatter.9.cloned.1.call-start = ((), (), s32[]{:S(2)}) async-start(), calls=%async_computation.10 | async-start | bytes 5242880 | tf_op jit(solution)/shard_map/reduce_scatter | solution.py:575
  567.7 4.0 copy-start.17
  567.7 4.0 copy-start.18
  567.7 4.0 copy-start.31
  567.7 4.0 copy-start.32
  567.7 4.0 copy-start.33
  576.8 285.5 %all-reduce.4.cloned.1.call-start = ((), (), s32[]{:S(2)}) async-start(), calls=%async_computation.12 | async-start | bytes 12845056 | tf_op jit(solution)/shard_map/psum | solution.py:586
  577.1 7.5 copy-start.27
  577.1 7.5 copy-start.35
  584.6 4.2 copy-start.37
  588.8 4.2 copy-start.19
  588.8 4.2 copy-start.21
  588.8 4.2 copy-start.25
  601.8 38.3 %copy-start.2 = (bf16[2,256,1024]{2,1,0:T(8,128)(2,1)S(1)}, bf16[2,256,1024]{2,1,0:T(8,128)(2,1)}, u32[]{:S(2)}) copy-start(bf16[2,256,1024]{2,1,0:T(8,128)(2,1)} %param.13) | copy-start | bytes 3145732
  (15 other events, 31.5 us)
Sparse Core Ops, SparseCore 0:
  12.3 37.1 all-gather.4
  51.1 22.5 all-gather.6
  211.4 43.0 all-gather.8
  255.9 34.4 all-gather.10
  309.6 44.5 reduce-scatter.6
  356.6 44.5 reduce-scatter.4
  408.6 39.2 reduce-scatter.10
  576.9 63.1 reduce-scatter.8
  645.7 216.5 all-reduce.3

commit v2 on v1

v2 whole, which is shorter than its diff:
```python
import functools
import math

import jax
import jax.numpy as jnp
from jax import lax
from jax.experimental import pallas as pl
from jax.experimental.pallas import tpu as pltpu
from jax.sharding import PartitionSpec as P

HD = 64
ROW = 2048
BLOCK = 256
LOG2E = math.log2(math.e)
LN2 = math.log(2.0)
MESH = pl.DeviceIdType.MESH


norm_eps = 1e-06
rope_base = 10000.0
masked_score = -1e30


def doc_layout(doc_lengths):
    doc_ends = jnp.cumsum(doc_lengths, axis=-1)
    places = jnp.arange(ROW, dtype=jnp.int32)
    passed = doc_ends[:, None, :] <= places[None, :, None]
    segment = jnp.sum(passed.astype(jnp.int32), axis=-1)
    starts = jnp.max(jnp.where(passed, doc_ends[:, None, :], 0), axis=-1)
    return (segment, places[None, :] - starts)


def norm_rows(values_in):
    inverse = lax.rsqrt(jnp.mean(values_in * values_in, axis=-1, keepdims=True) + norm_eps)
    return (values_in * inverse, inverse)


def norm_back(grads_in, unit_rows, inverse, gain):
    scaled = grads_in * gain
    extra = inverse * (scaled - unit_rows * jnp.mean(scaled * unit_rows, axis=-1, keepdims=True))
    return (extra, jnp.sum(grads_in * unit_rows, axis=0))


def rows_dot(left, right):
    return lax.dot_general(left, right, (((1,), (1,)), ((), ())), preferred_element_type=jnp.float32)


def plain_dot(left, right):
    return lax.dot_general(left, right, (((1,), (0,)), ((), ())), preferred_element_type=jnp.float32)


def head_masked(block, head, heads):
    if heads == 1:
        return block
    lanes = lax.broadcasted_iota(jnp.int32, block.shape, 1)
    return jnp.where(lanes // HD == head, block, jnp.zeros_like(block))


def attend_kernel(low_ref, q_ref, k_ref, v_ref, start_ref, o_ref, lse_ref, v_cols):
    row = pl.program_id(0)
    length, lanes = q_ref.shape[1:]
    heads = lanes // HD
    blocks = length // BLOCK
    for j in range(blocks):
        v_cols[:, j * BLOCK : (j + 1) * BLOCK] = v_ref[0, j * BLOCK : (j + 1) * BLOCK, :].T

    def query_block(i, carry):
        first = pl.multiple_of(i * BLOCK, BLOCK)
        q_block = q_ref[0, pl.ds(first, BLOCK), :]
        q_heads = [head_masked(q_block, h, heads) for h in range(heads)]
        start = start_ref[0, :, pl.ds(first, BLOCK)]
        places = first + lax.broadcasted_iota(jnp.int32, (1, BLOCK), 1)

        def key_block(j, state):
            at = pl.multiple_of(j * BLOCK, BLOCK)
            k_block = k_ref[0, pl.ds(at, BLOCK), :]
            keys = at + lax.broadcasted_iota(jnp.int32, (BLOCK, BLOCK), 0)
            allowed = (keys >= start) & (keys <= places)
            out = []
            for h in range(heads):
                top, total, acc = state[h]
                scores = jnp.where(allowed, rows_dot(k_block, q_heads[h]), masked_score)
                new_top = jnp.maximum(top, jnp.max(scores, axis=0, keepdims=True))
                weights = jnp.exp2(scores - new_top)
                shrink = jnp.exp2(top - new_top)
                total = total * shrink + jnp.sum(weights, axis=0, keepdims=True)
                acc = acc * shrink + plain_dot(
                    v_cols[h * HD : (h + 1) * HD, pl.ds(at, BLOCK)], weights.astype(jnp.bfloat16)
                )
                out.append((new_top, total, acc))
            return tuple(out)

        begin = tuple(
            (
                jnp.full((1, BLOCK), masked_score, jnp.float32),
                jnp.zeros((1, BLOCK), jnp.float32),
                jnp.zeros((HD, BLOCK), jnp.float32),
            )
            for _ in range(heads)
        )
        state = key_block(i, begin)
        state = lax.fori_loop(low_ref[row * blocks + i], i, key_block, state)
        columns = jnp.concatenate([acc / total for _, total, acc in state], axis=0)
        o_ref[0, pl.ds(first, BLOCK), :] = columns.T.astype(jnp.bfloat16)
        for h in range(heads):
            top, total, _ = state[h]
            lse_ref[0, 0, pl.ds(h, 1), pl.ds(first, BLOCK)] = top + jnp.log2(total)
        return carry

    lax.fori_loop(0, blocks, query_block, 0)


def attend(low, queries, keys, values, starts):
    rows, length, width = queries.shape
    lanes = min(width, 128)
    groups = width // lanes
    heads = lanes // HD
    wide = pl.BlockSpec((1, length, lanes), lambda r, g, low: (r, 0, g))
    return pl.pallas_call(
        attend_kernel,
        grid_spec=pltpu.PrefetchScalarGridSpec(
            num_scalar_prefetch=1,
            grid=(rows, groups),
            in_specs=[wide, wide, wide, pl.BlockSpec((1, 1, length), lambda r, g, low: (r, 0, 0))],
            out_specs=[
                wide,
                pl.BlockSpec((1, 1, heads, length), lambda r, g, low: (r, g, 0, 0)),
            ],
            scratch_shapes=[pltpu.VMEM((lanes, length), jnp.bfloat16)],
        ),
        out_shape=[
            jax.ShapeDtypeStruct(queries.shape, jnp.bfloat16),
            jax.ShapeDtypeStruct((rows, groups, heads, length), jnp.float32),
        ],
        name="attend",
    )(low, queries, keys, values, starts)


def attend_back_kernel(
    low_ref, q_ref, k_ref, v_ref, o_ref, g_ref, lse_ref, start_ref,
    qg_ref, kg_ref, vg_ref, k_cols, k_acc, v_acc,
):
    row = pl.program_id(0)
    length, lanes = q_ref.shape[1:]
    heads = lanes // HD
    blocks = length // BLOCK
    for j in range(blocks):
        k_cols[:, j * BLOCK : (j + 1) * BLOCK] = k_ref[0, j * BLOCK : (j + 1) * BLOCK, :].T
    k_acc[...] = jnp.zeros_like(k_acc)
    v_acc[...] = jnp.zeros_like(v_acc)
    select = (
        lax.broadcasted_iota(jnp.int32, (8, lanes), 1) // HD
        == lax.broadcasted_iota(jnp.int32, (8, lanes), 0)
    ).astype(jnp.float32)

    def query_block(i, carry):
        first = pl.multiple_of(i * BLOCK, BLOCK)
        q_block = q_ref[0, pl.ds(first, BLOCK), :]
        g_block = g_ref[0, pl.ds(first, BLOCK), :]
        q_heads = [head_masked(q_block, h, heads) for h in range(heads)]
        g_heads = [head_masked(g_block, h, heads) for h in range(heads)]
        product = g_block.astype(jnp.float32) * o_ref[0, pl.ds(first, BLOCK), :].astype(jnp.float32)
        centre = lax.dot_general(
            select, product, (((1,), (1,)), ((), ())),
            precision=lax.Precision.HIGHEST, preferred_element_type=jnp.float32,
        )
        lse = lse_ref[0, 0, :, pl.ds(first, BLOCK)]
        start = start_ref[0, :, pl.ds(first, BLOCK)]
        places = first + lax.broadcasted_iota(jnp.int32, (1, BLOCK), 1)

        def key_block(j, state):
            at = pl.multiple_of(j * BLOCK, BLOCK)
            k_block = k_ref[0, pl.ds(at, BLOCK), :]
            v_block = v_ref[0, pl.ds(at, BLOCK), :]
            keys = at + lax.broadcasted_iota(jnp.int32, (BLOCK, BLOCK), 0)
            allowed = (keys >= start) & (keys <= places)
            k_add = jnp.zeros((BLOCK, lanes), jnp.float32)
            v_add = jnp.zeros((BLOCK, lanes), jnp.float32)
            out = []
            for h in range(heads):
                scores = jnp.where(allowed, rows_dot(k_block, q_heads[h]), masked_score)
                probs = jnp.exp2(scores - lse[h : h + 1, :])
                prob_g = rows_dot(v_block, g_heads[h])
                score_g = (probs * (prob_g - centre[h : h + 1, :])).astype(jnp.bfloat16)
                v_add = v_add + plain_dot(probs.astype(jnp.bfloat16), g_heads[h])
                k_add = k_add + plain_dot(score_g, q_heads[h])
                out.append(
                    state[h] + plain_dot(k_cols[h * HD : (h + 1) * HD, pl.ds(at, BLOCK)], score_g)
                )
            k_acc[pl.ds(at, BLOCK), :] += k_add
            v_acc[pl.ds(at, BLOCK), :] += v_add
            return tuple(out)

        begin = tuple(jnp.zeros((HD, BLOCK), jnp.float32) for _ in range(heads))
        state = lax.fori_loop(low_ref[row * blocks + i], i + 1, key_block, begin)
        columns = jnp.concatenate(state, axis=0) * HD ** (-0.5)
        qg_ref[0, pl.ds(first, BLOCK), :] = columns.T.astype(jnp.bfloat16)
        return carry

    lax.fori_loop(0, blocks, query_block, 0)
    kg_ref[0] = (k_acc[...] * LN2).astype(jnp.bfloat16)
    vg_ref[0] = v_acc[...].astype(jnp.bfloat16)


def attend_back(low, queries, keys, values, attended, grads, lse, starts):
    rows, length, width = queries.shape
    lanes = min(width, 128)
    groups = width // lanes
    heads = lanes // HD
    wide = pl.BlockSpec((1, length, lanes), lambda r, g, low: (r, 0, g))
    return pl.pallas_call(
        attend_back_kernel,
        grid_spec=pltpu.PrefetchScalarGridSpec(
            num_scalar_prefetch=1,
            grid=(rows, groups),
            in_specs=[wide] * 5
            + [
                pl.BlockSpec((1, 1, heads, length), lambda r, g, low: (r, g, 0, 0)),
                pl.BlockSpec((1, 1, length), lambda r, g, low: (r, 0, 0)),
            ],
            out_specs=[wide] * 3,
            scratch_shapes=[
                pltpu.VMEM((lanes, length), jnp.bfloat16),
                pltpu.VMEM((length, lanes), jnp.float32),
                pltpu.VMEM((length, lanes), jnp.float32),
            ],
        ),
        out_shape=[jax.ShapeDtypeStruct(queries.shape, jnp.bfloat16)] * 3,
        name="attend_back",
    )(low, queries, keys, values, attended, grads, lse, starts)


def columns_dot(left, right):
    return lax.dot_general(left, right, (((0,), (0,)), ((), ())), preferred_element_type=jnp.float32)


def feed_kernel(
    chunk, feed_ref, cot_ref, gate_w, up_w, down_w,
    feed_g_ref, out_ref, gate_grad_ref, up_grad_ref, down_grad_ref,
    feed_all, part, core_in, pair_in, gate_acc, up_acc, down_acc,
    feed_send, feed_core, feed_pair, relay_send, part_send, part_core, sum_send, sum_pair,
):
    tokens = feed_ref.shape[0]
    chunks = tokens // chunk
    seq = lax.axis_index("seq")
    me = lax.axis_index("tp")
    pairs = lax.axis_size("tp") // 2
    pair, core = me // 2, lax.rem(me, 2)
    other = pair * 2 + 1 - core

    def peer(offset):
        return lax.rem(pair + offset, pairs) * 2 + core

    def copy(source, target, send, receive, to):
        return pltpu.make_async_remote_copy(
            src_ref=source, dst_ref=target, send_sem=send, recv_sem=receive,
            device_id=(seq, to), device_id_type=MESH,
        )

    barrier = pltpu.get_barrier_semaphore()
    for to in [other] + [peer(offset) for offset in range(1, pairs)]:
        pl.semaphore_signal(barrier, inc=1, device_id=(seq, to), device_id_type=MESH)
    pl.semaphore_wait(barrier, pairs)

    def rows(c):
        return pl.ds(pl.multiple_of(c * chunk, chunk), chunk)

    def feed_to_core(c):
        return copy(
            feed_ref.at[rows(c)], feed_all.at[me, rows(c)],
            feed_send.at[c], feed_core.at[c], other,
        )

    def feed_to_pair(offset, c):
        return copy(
            feed_ref.at[rows(c)], feed_all.at[me, rows(c)],
            feed_send.at[offset * chunks + c],
            feed_pair.at[(pairs - offset) * chunks + c], peer(offset),
        )

    def feed_from_pair(offset, c):
        return copy(
            feed_all.at[peer(offset), rows(c)], feed_all.at[peer(offset), rows(c)],
            feed_send.at[0], feed_pair.at[offset * chunks + c], other,
        )

    def relay(offset, c):
        return copy(
            feed_all.at[peer(offset), rows(c)], feed_all.at[peer(offset), rows(c)],
            relay_send.at[offset * chunks + c], feed_core.at[offset * chunks + c], other,
        )

    def part_to_core(offset, c):
        at = lax.rem(pair + offset, pairs) * 2 + 1 - core
        return copy(
            part.at[at, rows(c)], core_in.at[offset, rows(c)],
            part_send.at[offset * chunks + c], part_core.at[offset * chunks + c], other,
        )

    def sum_to_pair(offset, c):
        return copy(
            part.at[peer(offset), rows(c)], pair_in.at[pairs - offset, rows(c)],
            sum_send.at[offset * chunks + c],
            sum_pair.at[(pairs - offset) * chunks + c], peer(offset),
        )

    for c in range(chunks):
        feed_to_core(c).start()
        for offset in range(1, pairs):
            feed_to_pair(offset, c).start()
    feed_all[me] = feed_ref[...]
    gate_acc[...] = jnp.zeros_like(gate_acc)
    up_acc[...] = jnp.zeros_like(up_acc)
    down_acc[...] = jnp.zeros_like(down_acc)

    def step(n, carry):
        which = lax.rem(n, 2)
        c = lax.rem(n // 2, chunks)
        offset = n // (2 * chunks)
        owner = lax.rem(pair + offset, pairs) * 2 + lax.rem(core + which, 2)

        @pl.when((which == 0) & (offset > 0))
        def _():
            feed_from_pair(offset, c).wait_recv()
            relay(offset, c).start()

        @pl.when(which == 1)
        def _():
            relay(offset, c).wait_recv()

        feed = feed_all[owner, rows(c), :]
        cot = cot_ref[owner, rows(c), :]
        gate = plain_dot(feed, gate_w[...])
        up = plain_dot(feed, up_w[...])
        sigmoid = jax.nn.sigmoid(gate)
        activated = gate * sigmoid
        hidden = (activated * up).astype(jnp.bfloat16)
        hidden_g = rows_dot(cot, down_w[...])
        up_g = (hidden_g * activated).astype(jnp.bfloat16)
        gate_g = (hidden_g * up * sigmoid * (1.0 + gate * (1.0 - sigmoid))).astype(jnp.bfloat16)
        part[owner, rows(c), :] = (
            rows_dot(gate_g, gate_w[...]) + rows_dot(up_g, up_w[...])
        ).astype(jnp.bfloat16)

        @pl.when(which == 1)
        def _():
            part_to_core(offset, c).start()

        out_ref[owner, rows(c), :] = plain_dot(hidden, down_w[...]).astype(jnp.bfloat16)
        gate_acc[...] += columns_dot(feed, gate_g)
        up_acc[...] += columns_dot(feed, up_g)
        down_acc[...] += columns_dot(hidden, cot)

        @pl.when((which == 1) & (offset > 0))
        def _():
            part_to_core(offset, c).wait_recv()
            to = peer(offset)
            part[to, rows(c), :] = (
                part[to, rows(c), :].astype(jnp.float32)
                + core_in[offset, rows(c), :].astype(jnp.float32)
            ).astype(jnp.bfloat16)
            sum_to_pair(offset, c).start()

        return carry

    lax.fori_loop(0, 2 * chunks * pairs, step, 0)
    gate_grad_ref[...] = gate_acc[...].astype(jnp.bfloat16)
    up_grad_ref[...] = up_acc[...].astype(jnp.bfloat16)
    down_grad_ref[...] = down_acc[...].astype(jnp.bfloat16)
    for c in range(chunks):
        part_to_core(0, c).wait_recv()
        for offset in range(1, pairs):
            sum_to_pair(offset, c).wait_recv()
        total = part[me, rows(c), :].astype(jnp.float32) + core_in[0, rows(c), :].astype(jnp.float32)
        for offset in range(1, pairs):
            total = total + pair_in[offset, rows(c), :].astype(jnp.float32)
        feed_g_ref[rows(c), :] = total
    for c in range(chunks):
        feed_to_core(c).wait_send()
        part_to_core(0, c).wait_send()
        for offset in range(1, pairs):
            feed_to_pair(offset, c).wait_send()
            relay(offset, c).wait_send()
            part_to_core(offset, c).wait_send()
            sum_to_pair(offset, c).wait_send()


def feed_forward(feed_in, cot_all, gate_weight, up_weight, down_weight):
    tokens, width = feed_in.shape
    tp_size = cot_all.shape[0]
    pairs = tp_size // 2
    chunk = min(tokens, 256)
    chunks = tokens // chunk
    hidden = gate_weight.shape[1]
    whole = pl.BlockSpec(memory_space=pltpu.VMEM)
    dma = pltpu.SemaphoreType.DMA
    return pl.pallas_call(
        functools.partial(feed_kernel, chunk),
        out_shape=[
            jax.ShapeDtypeStruct((tokens, width), jnp.float32),
            jax.ShapeDtypeStruct(cot_all.shape, jnp.bfloat16),
            jax.ShapeDtypeStruct((width, hidden), jnp.bfloat16),
            jax.ShapeDtypeStruct((width, hidden), jnp.bfloat16),
            jax.ShapeDtypeStruct((hidden, width), jnp.bfloat16),
        ],
        in_specs=[whole] * 5,
        out_specs=[whole] * 5,
        scratch_shapes=[
            pltpu.VMEM(cot_all.shape, jnp.bfloat16),
            pltpu.VMEM(cot_all.shape, jnp.bfloat16),
            pltpu.VMEM((pairs, tokens, width), jnp.bfloat16),
            pltpu.VMEM((pairs, tokens, width), jnp.bfloat16),
            pltpu.VMEM((width, hidden), jnp.float32),
            pltpu.VMEM((width, hidden), jnp.float32),
            pltpu.VMEM((hidden, width), jnp.float32),
        ]
        + [dma((pairs * chunks,))] * 8,
        compiler_params=pltpu.CompilerParams(
            collective_id=4, has_side_effects=True, vmem_limit_bytes=67043328
        ),
        name="feed_forward",
    )(feed_in, cot_all, gate_weight, up_weight, down_weight)


def group_of(place, seq_size):
    half = seq_size // 2
    low = place // 2
    return lax.rem(place + low, 2) * half + low


def place_of(group, seq_size):
    half = seq_size // 2
    low = lax.rem(group, half)
    return low * 2 + lax.rem(low + group // half, 2)


def remote(source, target, send, receive, to):
    return pltpu.make_async_remote_copy(
        src_ref=source, dst_ref=target, send_sem=send, recv_sem=receive,
        device_id=to, device_id_type=MESH,
    )


def same(left, right):
    return (left[0] == right[0]) & (left[1] == right[1])


class Exchange:
    def __init__(self, plan, me, source, target, local_sem, send_sem, receive_sem):
        self.me = me
        self.sends, self.receives = plan(*me)
        self.source, self.target = source, target
        self.local_sem, self.send_sem, self.receive_sem = local_sem, send_sem, receive_sem

    def greet(self, barrier):
        for origin, _, _ in self.receives:
            @pl.when(jnp.logical_not(same(origin, self.me)))
            def _():
                pl.semaphore_signal(barrier, inc=1, device_id=origin, device_id_type=MESH)

    def others(self):
        return sum(jnp.where(same(to, self.me), 0, 1) for to, _, _, _ in self.sends)

    def each_send(self, wait):
        for n, (to, source, target, at) in enumerate(self.sends):
            here = same(to, self.me)

            @pl.when(here)
            def _():
                copy = pltpu.make_async_copy(
                    self.source.at[source], self.target.at[target], self.local_sem.at[n]
                )
                copy.wait() if wait else copy.start()

            @pl.when(jnp.logical_not(here))
            def _():
                copy = remote(
                    self.source.at[source], self.target.at[target],
                    self.send_sem.at[n], self.receive_sem.at[at], to,
                )
                copy.wait_send() if wait else copy.start()

    def start(self):
        self.each_send(False)

    def wait_sends(self):
        self.each_send(True)

    def wait_receive(self, origin, target, at):
        @pl.when(jnp.logical_not(same(origin, self.me)))
        def _():
            remote(
                self.target.at[target], self.target.at[target],
                self.send_sem.at[0], self.receive_sem.at[at], origin,
            ).wait_recv()

    def wait_receives(self):
        for receive in self.receives:
            self.wait_receive(*receive)


def exchange(arrays, out_shapes, plans, number):
    count = len(arrays)

    def kernel(*refs):
        me = (lax.axis_index("seq"), lax.axis_index("tp"))
        moves = [
            Exchange(plan, me, refs[n], refs[count + n], *refs[2 * count + 3 * n :][:3])
            for n, plan in enumerate(plans)
        ]
        barrier = pltpu.get_barrier_semaphore()
        for move in moves:
            move.greet(barrier)
        pl.semaphore_wait(barrier, sum(move.others() for move in moves))
        for move in moves:
            move.start()
        for move in moves:
            move.wait_sends()
        for move in moves:
            move.wait_receives()

    semaphores = []
    for plan in plans:
        semaphores += [pltpu.SemaphoreType.DMA((len(plan(0, 0)[0]),))] * 3
    return pl.pallas_call(
        kernel,
        out_shape=[
            jax.ShapeDtypeStruct(shape, array.dtype) for shape, array in zip(out_shapes, arrays)
        ],
        in_specs=[pl.BlockSpec(memory_space=pl.ANY)] * count,
        out_specs=[pl.BlockSpec(memory_space=pl.ANY)] * count,
        scratch_shapes=semaphores,
        compiler_params=pltpu.CompilerParams(collective_id=number, has_side_effects=True),
        name=f"exchange_{number}",
    )(*arrays)


def owner_to_quarter(seq_size, tp_size, rows_each, rows_local, piece_first):
    def plan(s, t):
        sends, receives = [], []
        for slot in range(rows_local):
            row = t * rows_local + slot
            to = place_of(row // rows_each, seq_size)
            j = lax.rem(row, rows_each)
            for i in range(tp_size):
                target = (i, j, s) if piece_first else (j, s, i)
                sends.append(((to, i), (slot, i), target, j * seq_size + s))
        group = group_of(s, seq_size)
        for j in range(rows_each):
            row = group * rows_each + j
            for i in range(seq_size):
                origin = lax.rem(s + i, seq_size)
                target = (t, j, origin) if piece_first else (j, origin, t)
                receives.append(((origin, row // rows_local), target, j * seq_size + origin))
        return sends, receives

    return plan


def quarter_to_owner(seq_size, tp_size, rows_each, rows_local):
    def plan(s, t):
        sends, receives = [], []
        group = group_of(s, seq_size)
        for i in range(seq_size):
            to = lax.rem(s + i, seq_size)
            for j in range(rows_each):
                row = group * rows_each + j
                slot = lax.rem(row, rows_local)
                sends.append(((to, row // rows_local), (j, to), (slot, t), slot * tp_size + t))
        for slot in range(rows_local):
            row = t * rows_local + slot
            for i in range(tp_size):
                receives.append(
                    ((place_of(row // rows_each, seq_size), i), (slot, i), slot * tp_size + i)
                )
        return sends, receives

    return plan


def places_to_rows(seq_size, rows_each):
    def plan(s, t):
        sends, receives = [], []
        for i in range(seq_size):
            to = lax.rem(s + i, seq_size)
            rows = pl.ds(group_of(to, seq_size) * rows_each, rows_each)
            sends.append(((to, t), (rows,), (slice(None), s), s))
            origin = lax.rem(s + seq_size - i, seq_size)
            receives.append(((origin, t), (slice(None), origin), origin))
        return sends, receives

    return plan


def rows_to_places(seq_size, rows_each):
    def plan(s, t):
        sends, receives = [], []
        rows = pl.ds(group_of(s, seq_size) * rows_each, rows_each)
        for i in range(seq_size):
            to = lax.rem(s + i, seq_size)
            sends.append(((to, t), (slice(None), to), (rows,), s))
            origin = lax.rem(s + seq_size - i, seq_size)
            source_rows = pl.ds(group_of(origin, seq_size) * rows_each, rows_each)
            receives.append(((origin, t), (source_rows,), origin))
        return sends, receives

    return plan


def heads_to_tokens(tp_size):
    def plan(s, t):
        sends, receives = [], []
        for i in range(tp_size):
            to = lax.rem(t + i, tp_size)
            sends.append(((s, to), (slice(None), slice(None), to), (t,), t))
            origin = lax.rem(t + tp_size - i, tp_size)
            receives.append(((s, origin), (origin,), origin))
        return sends, receives

    return plan


def tokens_to_heads(tp_size):
    def plan(s, t):
        sends, receives = [], []
        for i in range(tp_size):
            to = lax.rem(t + i, tp_size)
            sends.append(((s, to), (to,), (slice(None), slice(None), t), t))
            origin = lax.rem(t + tp_size - i, tp_size)
            receives.append(((s, origin), (slice(None), slice(None), origin), origin))
        return sends, receives

    return plan


def spread_kernel(
    plans, sizes, x_ref, cot_ref, first_ref, x_out, cot_out, first_out,
    x_local, x_send, x_receive, cot_local, cot_send, cot_receive,
    first_local, first_send, first_receive,
    core_send, core_receive, pair_send, pair_receive, relay_send,
):
    seq_size, tp_size, rows_each, rows_local, parts = sizes
    me = (lax.axis_index("seq"), lax.axis_index("tp"))
    s, t = me
    pairs = tp_size // 2
    pair, core = t // 2, lax.rem(t, 2)
    other = pair * 2 + 1 - core
    each = seq_size // parts

    def peer(offset):
        return lax.rem(pair + offset, pairs) * 2 + core

    x_move = Exchange(plans[0], me, x_ref, x_out, x_local, x_send, x_receive)
    cot_move = Exchange(plans[1], me, cot_ref, cot_out, cot_local, cot_send, cot_receive)
    first_move = Exchange(plans[2], me, first_ref, first_out, first_local, first_send, first_receive)
    moves = (x_move, first_move, cot_move)
    barrier = pltpu.get_barrier_semaphore()
    for move in moves:
        move.greet(barrier)
    for to in [other] + [peer(offset) for offset in range(1, pairs)]:
        pl.semaphore_signal(barrier, inc=1, device_id=(s, to), device_id_type=MESH)
    pl.semaphore_wait(barrier, sum(move.others() for move in moves) + pairs)
    for move in moves:
        move.start()

    def block(out, tensor, piece, part):
        span = pl.ds(part * each, each)
        return out.at[:, span, piece] if tensor == 0 else out.at[piece, :, span]

    def number(tensor, offset, part):
        return (tensor * pairs + offset) * parts + part

    def to_core(out, tensor, part):
        view, at = block(out, tensor, t, part), number(tensor, 0, part)
        return remote(view, view, core_send.at[at], core_receive.at[at], (s, other))

    def to_pair(out, tensor, offset, part):
        view = block(out, tensor, t, part)
        return remote(
            view, view, pair_send.at[number(tensor, offset, part)],
            pair_receive.at[number(tensor, pairs - offset, part)], (s, peer(offset)),
        )

    def from_pair(out, tensor, offset, part):
        view, at = block(out, tensor, peer(offset), part), number(tensor, offset, part)
        return remote(view, view, pair_send.at[at], pair_receive.at[at], (s, peer(offset)))

    def relay(out, tensor, offset, part):
        view, at = block(out, tensor, peer(offset), part), number(tensor, offset, part)
        return remote(view, view, relay_send.at[at], core_receive.at[at], (s, other))

    def from_core(out, tensor, offset, part):
        piece = lax.rem(pair + offset, pairs) * 2 + 1 - core
        view, at = block(out, tensor, piece, part), number(tensor, offset, part)
        return remote(view, view, relay_send.at[at], core_receive.at[at], (s, other))

    def forward(move, out, tensor):
        def receive(n, carry):
            part = lax.rem(s // each + n, parts)
            for j in range(rows_each):
                for i in range(each):
                    origin = part * each + i
                    group = group_of(s, seq_size)
                    owner = (origin, (group * rows_each + j) // rows_local)
                    target = (t, j, origin) if tensor else (j, origin, t)
                    move.wait_receive(owner, target, j * seq_size + origin)
                    slot = lax.rem(group * rows_each + j, rows_local)

                    @pl.when(same(owner, me))
                    def _():
                        pltpu.make_async_copy(
                            move.source.at[slot, t], move.target.at[target],
                            move.local_sem.at[slot * tp_size + t],
                        ).wait()
            to_core(out, tensor, part).start()
            for offset in range(1, pairs):
                to_pair(out, tensor, offset, part).start()
            return carry

        def relays(n, carry):
            part = lax.rem(s // each + n, parts)
            for offset in range(1, pairs):
                from_pair(out, tensor, offset, part).wait_recv()
                relay(out, tensor, offset, part).start()
            return carry

        lax.fori_loop(0, parts, receive, 0)
        lax.fori_loop(0, parts, relays, 0)

    def finish(move, out, tensor):
        def one(part, carry):
            for offset in range(pairs):
                from_core(out, tensor, offset, part).wait_recv()
            to_core(out, tensor, part).wait_send()
            for offset in range(1, pairs):
                to_pair(out, tensor, offset, part).wait_send()
                relay(out, tensor, offset, part).wait_send()
            return carry

        lax.fori_loop(0, parts, one, 0)
        for n, (to, source, target, at) in enumerate(move.sends):
            @pl.when(jnp.logical_not(same(to, me)))
            def _():
                remote(
                    move.source.at[source], move.target.at[target],
                    move.send_sem.at[n], move.receive_sem.at[at], to,
                ).wait_send()

    forward(x_move, x_out, 0)
    forward(cot_move, cot_out, 1)
    finish(x_move, x_out, 0)
    finish(cot_move, cot_out, 1)
    first_move.wait_sends()
    first_move.wait_receives()


def spread(layer_input, cotangent, first_values, sizes):
    seq_size, tp_size, rows_each, rows_local, parts = sizes
    pieces = layer_input.shape[2:]
    plans = (
        owner_to_quarter(seq_size, tp_size, rows_each, rows_local, False),
        owner_to_quarter(seq_size, tp_size, rows_each, rows_local, True),
        places_to_rows(seq_size, rows_each),
    )
    dma = pltpu.SemaphoreType.DMA
    quarter = [
        dma((rows_local * tp_size,)), dma((rows_local * tp_size,)), dma((rows_each * seq_size,)),
    ]
    stage = tp_size // 2 * parts * 2
    return pl.pallas_call(
        functools.partial(spread_kernel, plans, sizes),
        out_shape=[
            jax.ShapeDtypeStruct((rows_each, seq_size, tp_size) + pieces, jnp.bfloat16),
            jax.ShapeDtypeStruct((tp_size, rows_each, seq_size) + pieces, jnp.bfloat16),
            jax.ShapeDtypeStruct((rows_each, seq_size) + first_values.shape[1:], jnp.bfloat16),
        ],
        in_specs=[pl.BlockSpec(memory_space=pl.ANY)] * 3,
        out_specs=[pl.BlockSpec(memory_space=pl.ANY)] * 3,
        scratch_shapes=quarter + quarter + [dma((seq_size,))] * 3 + [dma((stage,))] * 5,
        compiler_params=pltpu.CompilerParams(collective_id=5, has_side_effects=True),
        name="spread",
    )(layer_input, cotangent, first_values)


def widen(table, width):
    return jnp.concatenate([table] * (width // table.shape[1]), axis=1)


def project_kernel(
    x_ref, first_ref, cos_ref, sin_ref, gain_ref, weight_ref, swapped_ref,
    q_ref, k_ref, v_ref, square_ref,
):
    width = q_ref.shape[1]
    x = x_ref[...].astype(jnp.float32)
    inverse = lax.rsqrt(jnp.mean(x * x, axis=-1, keepdims=True) + norm_eps)
    normed = (x * inverse * gain_ref[...]).astype(jnp.bfloat16)
    straight = rows_dot(normed, weight_ref[...])
    swapped = rows_dot(normed, swapped_ref[...])
    cosine, sine = widen(cos_ref[...], width), widen(sin_ref[...], width)
    q_ref[...] = (
        (straight[:, :width] * cosine + swapped[:, :width] * sine) * (HD ** (-0.5) * LOG2E)
    ).astype(jnp.bfloat16)
    k_ref[...] = (
        straight[:, width : 2 * width] * cosine + swapped[:, width:] * sine
    ).astype(jnp.bfloat16)
    first = first_ref[0, 0].astype(jnp.float32)
    mixed = (0.5 * straight[:, 2 * width :] + 0.5 * first.T).astype(jnp.bfloat16)
    v_ref[...] = mixed
    wide = mixed.astype(jnp.float32)

    @pl.when(pl.program_id(0) == 0)
    def _():
        square_ref[...] = jnp.zeros_like(square_ref)

    square_ref[0:1, :] += jnp.sum(first * first, axis=0, keepdims=True)
    square_ref[1:2, : wide.shape[1]] += jnp.sum(wide * wide, axis=0, keepdims=True)


def project(x_rows, first_rows, cosine, sine, gain, weights, swapped):
    tokens, depth = x_rows.shape
    rows_each, seq_size, width, places = first_rows.shape
    lanes = cosine.shape[1]

    def tile(columns):
        return pl.BlockSpec((places, columns), lambda n: (n, 0))

    def fixed(array):
        return pl.BlockSpec(array.shape, lambda n: (0,) * array.ndim)

    square = jax.ShapeDtypeStruct((8, max(width, places)), jnp.float32)
    return pl.pallas_call(
        project_kernel,
        grid=(rows_each * seq_size,),
        in_specs=[
            tile(depth),
            pl.BlockSpec((1, 1, width, places), lambda n: (n // seq_size, n % seq_size, 0, 0)),
            tile(lanes),
            tile(lanes),
            fixed(gain),
            fixed(weights),
            fixed(swapped),
        ],
        out_specs=[tile(width)] * 3 + [fixed(square)],
        out_shape=[jax.ShapeDtypeStruct((tokens, width), jnp.bfloat16)] * 3 + [square],
        compiler_params=pltpu.CompilerParams(vmem_limit_bytes=67043328),
        name="project",
    )(x_rows, first_rows, cosine, sine, gain, weights, swapped)


def project_back_kernel(
    x_ref, q_ref, k_ref, v_ref, cos_ref, sin_ref, gain_ref, weight_ref, turn_ref,
    normed_g_ref, grad_ref, grad_acc,
):
    width = q_ref.shape[1]
    x = x_ref[...].astype(jnp.float32)
    inverse = lax.rsqrt(jnp.mean(x * x, axis=-1, keepdims=True) + norm_eps)
    normed = (x * inverse * gain_ref[...]).astype(jnp.bfloat16)
    cosine, sine = widen(cos_ref[...], width), widen(sin_ref[...], width)

    def unrotate(grad):
        turned = plain_dot(grad, turn_ref[...])
        return (grad.astype(jnp.float32) * cosine + turned * sine).astype(jnp.bfloat16)

    stacked = jnp.concatenate(
        [
            unrotate(q_ref[...]),
            unrotate(k_ref[...]),
            (0.5 * v_ref[...].astype(jnp.float32)).astype(jnp.bfloat16),
        ],
        axis=1,
    )
    normed_g_ref[...] = plain_dot(stacked, weight_ref[...]).astype(jnp.bfloat16).reshape(
        normed_g_ref.shape
    )

    @pl.when(pl.program_id(0) == 0)
    def _():
        grad_acc[...] = jnp.zeros_like(grad_acc)

    grad_acc[...] += columns_dot(stacked, normed)

    @pl.when(pl.program_id(0) == pl.num_programs(0) - 1)
    def _():
        grad_ref[...] = grad_acc[...].astype(jnp.bfloat16)


def project_back(x_rows, query_g, key_g, value_g, cosine, sine, gain, weights, turn, sizes):
    seq_size, tp_size, rows_each, _, _ = sizes
    tokens, depth = x_rows.shape
    places = tokens // (rows_each * seq_size)
    width, lanes = query_g.shape[1], cosine.shape[1]
    piece = places // tp_size

    def tile(columns):
        return pl.BlockSpec((places, columns), lambda n: (n, 0))

    def fixed(array):
        return pl.BlockSpec(array.shape, lambda n: (0,) * array.ndim)

    return pl.pallas_call(
        project_back_kernel,
        grid=(rows_each * seq_size,),
        in_specs=[
            tile(depth), tile(width), tile(width), tile(width), tile(lanes), tile(lanes),
            fixed(gain), fixed(weights), fixed(turn),
        ],
        out_specs=[
            pl.BlockSpec((tp_size, 1, piece, depth), lambda n: (0, n, 0, 0)),
            fixed(weights),
        ],
        out_shape=[
            jax.ShapeDtypeStruct((tp_size, rows_each * seq_size, piece, depth), jnp.bfloat16),
            jax.ShapeDtypeStruct(weights.shape, jnp.bfloat16),
        ],
        scratch_shapes=[pltpu.VMEM(weights.shape, jnp.float32)],
        compiler_params=pltpu.CompilerParams(vmem_limit_bytes=67043328),
        name="project_back",
    )(x_rows, query_g, key_g, value_g, cosine, sine, gain, weights, turn)


def total_kernel(seq_size, tp_size, in_ref, out_ref, held, sums, seq_held, send_sem, tp_sem, seq_sem):
    s, t = lax.axis_index("seq"), lax.axis_index("tp")
    barrier = pltpu.get_barrier_semaphore()
    tp_peers = [lax.rem(t + i, tp_size) for i in range(1, tp_size)]
    seq_peers = [lax.rem(s + i, seq_size) for i in range(1, seq_size)]
    for other in tp_peers:
        pl.semaphore_signal(barrier, inc=1, device_id=(s, other), device_id_type=MESH)
    for other in seq_peers:
        pl.semaphore_signal(barrier, inc=1, device_id=(other, t), device_id_type=MESH)
    pl.semaphore_wait(barrier, tp_size + seq_size - 2)

    def tp_copy(n):
        return remote(
            in_ref, held.at[tp_size - n], send_sem.at[n], tp_sem.at[tp_size - n], (s, tp_peers[n - 1])
        )

    def seq_copy(n):
        return remote(
            sums, seq_held.at[seq_size - n], send_sem.at[tp_size + n],
            seq_sem.at[seq_size - n], (seq_peers[n - 1], t),
        )

    for n in range(1, tp_size):
        tp_copy(n).start()
    for n in range(1, tp_size):
        tp_copy(n).wait()
    held[0] = in_ref[...]
    total = held[lax.rem(tp_size - t, tp_size)]
    for n in range(1, tp_size):
        total = total + held[lax.rem(n + tp_size - t, tp_size)]
    sums[...] = total
    for n in range(1, seq_size):
        seq_copy(n).start()
    seq_held[0] = total
    for n in range(1, seq_size):
        seq_copy(n).wait()
    total = seq_held[lax.rem(seq_size - s, seq_size)]
    for n in range(1, seq_size):
        total = total + seq_held[lax.rem(n + seq_size - s, seq_size)]
    out_ref[...] = total


def total_of(values, seq_size, tp_size):
    whole = pl.BlockSpec(memory_space=pltpu.VMEM)
    dma = pltpu.SemaphoreType.DMA
    return pl.pallas_call(
        functools.partial(total_kernel, seq_size, tp_size),
        out_shape=jax.ShapeDtypeStruct(values.shape, jnp.float32),
        in_specs=[whole],
        out_specs=whole,
        scratch_shapes=[
            pltpu.VMEM((tp_size,) + values.shape, jnp.float32),
            pltpu.VMEM(values.shape, jnp.float32),
            pltpu.VMEM((seq_size,) + values.shape, jnp.float32),
            dma((tp_size + seq_size,)),
            dma((tp_size,)),
            dma((seq_size,)),
        ],
        compiler_params=pltpu.CompilerParams(collective_id=6, has_side_effects=True),
        name="total",
    )(values)


def half_swap(weight):
    parts = weight.reshape(-1, 2, HD // 2, weight.shape[1])
    return jnp.stack([-parts[:, 1], parts[:, 0]], axis=1).reshape(weight.shape)


def shards(
    layer_input,
    first_values,
    doc_lengths,
    attn_gain,
    query_weight,
    key_weight,
    value_weight,
    output_weight,
    feed_gain,
    gate_weight,
    up_weight,
    down_weight,
    out_cotangent,
):
    seq_size = lax.axis_size("seq")
    tp_size = lax.axis_size("tp")
    rows_local, local_len, depth = layer_input.shape
    row_count = first_values.shape[0]
    width = query_weight.shape[0]
    rows_each = row_count // seq_size
    piece = local_len // tp_size
    tokens = rows_each * seq_size * piece
    sizes = (seq_size, tp_size, rows_each, rows_local, 4)
    me = lax.axis_index("tp")
    my_rows = group_of(lax.axis_index("seq"), seq_size) * rows_each

    _, offsets = doc_layout(doc_lengths)
    offsets = lax.dynamic_slice_in_dim(offsets, my_rows, rows_each, 0)
    starts = jnp.arange(ROW, dtype=jnp.int32)[None, :] - offsets
    low = (starts[:, ::BLOCK] // BLOCK).reshape(-1)
    starts = starts[:, None, :]
    lane = jnp.arange(min(width, 128), dtype=jnp.int32)
    frequency = rope_base ** (-(lane % (HD // 2)).astype(jnp.float32) * 2.0 / HD)
    angles = offsets.astype(jnp.float32).reshape(-1, 1) * frequency
    cosine, sine = jnp.cos(angles), jnp.sin(angles)
    attn_scale = attn_gain.astype(jnp.float32)[None, :]
    feed_scale = feed_gain.astype(jnp.float32)[None, :]
    weights = jnp.concatenate([query_weight, key_weight, value_weight], axis=0)
    swapped = jnp.concatenate([half_swap(query_weight), half_swap(key_weight)], axis=0)
    turn = half_swap(jnp.eye(width, dtype=jnp.bfloat16))

    x_rows, cot_all, first_rows = spread(
        layer_input.reshape(rows_local, tp_size, piece, depth),
        out_cotangent.reshape(rows_local, tp_size, piece, depth),
        first_values,
        sizes,
    )
    source = lax.dynamic_index_in_dim(x_rows, me, 2, keepdims=False).reshape(tokens, depth)
    source = source.astype(jnp.float32)
    cotangent = lax.dynamic_index_in_dim(cot_all, me, 0, keepdims=False).reshape(tokens, depth)
    cotangent = cotangent.astype(jnp.float32)
    x_rows = x_rows.reshape(rows_each * ROW, depth)
    queries, keys, values, squares = project(
        x_rows, first_rows, cosine, sine, attn_scale, weights, swapped
    )
    queries, keys, values = (
        part.reshape(rows_each, ROW, width) for part in (queries, keys, values)
    )
    result, logsum = attend(low, queries, keys, values, starts)
    by_piece = (rows_each, seq_size, tp_size, piece, width)
    by_head = (tp_size, rows_each, seq_size, piece, width)
    (pieces,) = exchange([result.reshape(by_piece)], [by_head], [heads_to_tokens(tp_size)], 1)
    attended = jnp.transpose(pieces.reshape(tp_size, tokens, width), (1, 0, 2)).reshape(tokens, -1)
    output_full = lax.all_gather(output_weight, "tp", axis=0, tiled=True)
    attended, output_full = lax.optimization_barrier((attended, output_full))
    middle = source + jnp.dot(attended, output_full, preferred_element_type=jnp.float32)
    unit_feed, inv_feed = norm_rows(middle)
    feed_in = (unit_feed * feed_scale).astype(jnp.bfloat16)
    feed_in_g, out_part, gate_grad, up_grad, down_grad = feed_forward(
        feed_in, cot_all.reshape(tp_size, tokens, depth), gate_weight, up_weight, down_weight
    )
    out_sum = lax.psum_scatter(out_part, "tp", scatter_dimension=0, tiled=False)
    layer_output = (middle + out_sum.astype(jnp.float32)).astype(jnp.bfloat16)
    middle_extra, feed_gain_part = norm_back(feed_in_g, unit_feed, inv_feed, feed_scale)
    middle_g = cotangent + middle_extra
    branch_g = middle_g.astype(jnp.bfloat16)
    attended_g = jnp.einsum(
        "td,ed->te", branch_g, output_full, preferred_element_type=jnp.float32
    ).astype(jnp.bfloat16)
    (attended_g,) = exchange(
        [jnp.transpose(attended_g.reshape(tokens, tp_size, width), (1, 0, 2)).reshape(by_head)],
        [by_piece],
        [tokens_to_heads(tp_size)],
        2,
    )
    query_g, key_g, value_g = attend_back(
        low, queries, keys, values, result, attended_g.reshape(result.shape), logsum, starts
    )
    normed_g, stacked_grad = project_back(
        x_rows,
        query_g.reshape(-1, width),
        key_g.reshape(-1, width),
        value_g.reshape(-1, width),
        cosine,
        sine,
        attn_scale,
        weights,
        turn,
        sizes,
    )
    output_proj_grad = lax.psum_scatter(
        jnp.einsum("te,td->ed", attended, branch_g, preferred_element_type=jnp.float32).astype(
            jnp.bfloat16
        ),
        "tp",
        scatter_dimension=0,
        tiled=True,
    )
    normed_g = lax.psum_scatter(
        normed_g.reshape(tp_size, tokens, depth), "tp", scatter_dimension=0, tiled=False
    ).astype(jnp.float32)
    unit_attn, inv_attn = norm_rows(source)
    input_extra, attn_gain_part = norm_back(normed_g, unit_attn, inv_attn, attn_scale)
    input_grad = (middle_g + input_extra).astype(jnp.bfloat16)
    quarter = (rows_each, seq_size, piece, depth)
    owned = (rows_local, tp_size, piece, depth)
    back = quarter_to_owner(seq_size, tp_size, rows_each, rows_local)
    layer_output, input_grad, value_own_g = exchange(
        [
            layer_output.reshape(quarter),
            input_grad.reshape(quarter),
            value_g.reshape(rows_each, seq_size, local_len, width),
        ],
        [owned, owned, (row_count, local_len, width)],
        [back, back, rows_to_places(seq_size, rows_each)],
        3,
    )
    first_grad = jnp.swapaxes(0.5 * value_own_g.astype(jnp.float32), 1, 2)
    feed_sums = lax.psum((gate_grad, up_grad, down_grad), "seq")
    stacked_grad, output_proj_grad, feed_sums = lax.optimization_barrier(
        (stacked_grad, output_proj_grad, feed_sums)
    )
    stacked_total, output_proj_total = lax.psum((stacked_grad, output_proj_grad), "seq")
    stacked_total = stacked_total.astype(jnp.float32)
    squares = jnp.pad(jnp.sum(squares, axis=1)[:2], (0, 126))
    small = total_of(
        jnp.concatenate([attn_gain_part, feed_gain_part, jnp.pad(squares, (0, 7 * 128))]).reshape(
            -1, 128
        ),
        seq_size,
        tp_size,
    ).reshape(-1)
    return (
        layer_output.reshape(layer_input.shape),
        input_grad.reshape(layer_input.shape),
        first_grad,
        small[:depth],
        stacked_total[:width],
        stacked_total[width : 2 * width],
        stacked_total[2 * width :],
        output_proj_total.astype(jnp.float32),
        small[depth : 2 * depth],
        feed_sums[0].astype(jnp.float32),
        feed_sums[1].astype(jnp.float32),
        feed_sums[2].astype(jnp.float32),
        jnp.sqrt(small[2 * depth : 2 * depth + 2]),
    )


def solution(mesh):
    placed = (
        P("tp", "seq", None),
        P(None, "tp", "seq"),
        P(),
        P(),
        P("tp", None),
        P("tp", None),
        P("tp", None),
        P("tp", None),
        P(),
        P(None, "tp"),
        P(None, "tp"),
        P("tp", None),
        P("tp", "seq", None),
    )
    return jax.shard_map(
        shards,
        mesh=mesh,
        in_specs=placed,
        out_specs=(
            P("tp", "seq", None),
            P("tp", "seq", None),
            P(None, "tp", "seq"),
            P(),
            P("tp", None),
            P("tp", None),
            P("tp", None),
            P("tp", None),
            P(),
            P(None, "tp"),
            P(None, "tp"),
            P("tp", None),
            P(),
        ),
        check_vma=False,
    )
```

time: 887 us -> 763 us (0.86)
  Pallas kernels: 269 us -> 366 us
  waiting for transfers between devices: 387 us -> 312 us
  matrix products: 81.1 us -> 8.8 us
  blocking collectives: 43.6 us -> 0 us
  other arithmetic: 46.2 us -> 32.4 us
  local copies, waits for them, and re-layouts: 36.9 us -> 27.5 us
    pallas_call x4 -> x8, Pallas kernels: 197 us -> 295 us  [the longest x3 93.3 us: exchange(): pl.pallas_call(kernel, out_shape=[jax.ShapeDtypeStruct(shape, array.dtype...]
    all_gather x3 -> x0, waiting for transfers between devices: 94.9 us -> none  [the longest x1 42.4 us: shards(): feed_all = lax.all_gather(feed_in, 'tp', axis=0, tiled=True)]
    dot_general x15 -> x3, matrix products: 81.1 us -> 8.8 us  [the longest x1 3.25 us: shards(): jnp.einsum('td,ed->te', branch_g, output_full, preferred_element_type=jnp...]
    psum x1 -> x0, blocking collectives: 43.6 us -> none  [shards(): small = lax.psum((attn_gain_part, feed_gain_part, squares), ('seq', 'tp'))]
    psum x1 -> x2, waiting for transfers between devices: 173 us -> 191 us  [the longest x1 97.6 us: shards(): lax.psum((stacked_grad, output_proj_grad), 'seq')]
    convert_element_type x5 -> x0, local copies, waits for them, and re-layouts: 9.55 us -> none  [the longest x1 2.26 us: shards(): keys_rot = rotate(projected[..., width_local:2 * width_local].reshape(row...]
    reduce_scatter x4 -> x3, waiting for transfers between devices: 118 us -> 119 us  [the longest x1 43.9 us: shards(): out_sum = lax.psum_scatter(out_part, 'tp', scatter_dimension=0, tiled=False)]
  transfers between devices with their start and end apart: 9 -> 6, of which waited for: 7 -> 5; matrix products, arithmetic and copies ran while one was open for 13% -> 6% of each run, Pallas kernels for 31% -> 28%
where the time goes in v2:
time: 763 us; the launch traced here: 762 us
  Pallas kernels  366 us (48%)
  waiting for transfers between devices  312 us (41%)
  other arithmetic  32.4 us (4%)
  local copies, waits for them, and re-layouts  27.5 us (4%)
  between operations  14.6 us (2%)
  matrix products  8.8 us (1%)
    psum x1, waiting for transfers between devices, shards(): lax.psum((stacked_grad, output_proj_grad), 'seq')  97.6 us
    pallas_call x3, Pallas kernels, exchange(): pl.pallas_call(kernel, out_shape=[jax.ShapeDtypeStruct(shape, array.dtype...  93.3 us
    psum x1, waiting for transfers between devices, shards(): feed_sums = lax.psum((gate_grad, up_grad, down_grad), 'seq')  93 us
    pallas_call x1, Pallas kernels, spread(): pl.pallas_call(functools.partial(spread_kernel, plans, sizes), out_shape=...  91.6 us
    pallas_call x1, Pallas kernels, feed_forward(): pl.pallas_call(functools.partial(feed_kernel, chunk), out_shape=[jax.Shap...  65 us
    reduce_scatter x1, waiting for transfers between devices, shards(): out_sum = lax.psum_scatter(out_part, 'tp', scatter_dimension=0, tiled=False)  43.9 us
    reduce_scatter x1, waiting for transfers between devices, shards(): lax.psum_scatter(normed_g.reshape(tp_size, tokens, depth), 'tp', scatter_...  42.3 us
    pallas_call x1, Pallas kernels, attend_back(): pl.pallas_call(attend_back_kernel, grid_spec=pltpu.PrefetchScalarGridSpec...  36.5 us
  transfers between devices with their start and end apart: 6, of which 5 were waited for; matrix products, arithmetic and copies ran while one was open for 6% of the time, Pallas kernels for 28%

profile of v2, /device:TPU:0, one launch (start us, length us, event | category | flops | bytes accessed | tf_op | source)
XLA Modules:
  0.0 761.6 jit_solution(17150879380911658277)
XLA Ops:
  11.2 91.6 %spread.1 = (bf16[1,8,4,64,1024]{4,3,2,1,0:T(8,128)(2,1)}, bf16[4,1,8,64,1024]{4,3,2,1,0:T(8,128)(2,1)}, bf16[1,8,256,256]{3,2,1,0:T(8,128)(2,1)}) custom-call(bf16[2,4,64,1024]{3,2,1,0:T(8,128)(2,1)} %bitcast.101, bf16[2,4,64,1024]{3,2,1,0:T(8,128)(2,1)} %bitcast.102, bf16[8,256,256]{2,1,0:T(8,128)(2,1)} %first_ref.1), custom_call_target="tpu_custom_call" | custom-call | tf_op jit(solution)/shard_map/spread/pallas_call | solution.py:770
  105.1 5.5 multiply_sine_fusion
  110.6 11.8 %project.1 = (bf16[2048,256]{1,0:T(8,128)(2,1)}, bf16[2048,256]{1,0:T(8,128)(2,1)}, bf16[2048,256]{1,0:T(8,128)(2,1)}, f32[8,256]{1,0:T(8,128)}) custom-call(bf16[2048,1024]{1,0:T(8,128)(2,1)} %bitcast.77, bf16[1,8,256,256]{3,2,1,0:T(8,128)(2,1)} %get-tuple-element.43.first_ref, f32[2048,128]{1,0:T(8,128)} %get-tuple-element.135.cos_ref, ...), custom_call_target="tpu_custom_call" | custom-call | tf_op jit(solution)/shard_map/project/pallas_call | solution.py:831
  123.7 35.1 %attend.1 = (bf16[1,2048,256]{2,1,0:T(8,128)(2,1)}, f32[1,2,2,2048]{3,2,1,0:T(2,128)}) custom-call(s32[8]{0:T(128)} %fusion.17.low_ref, bf16[1,2048,256]{2,1,0:T(8,128)(2,1)} %bitcast.86, bf16[1,2048,256]{2,1,0:T(8,128)(2,1)} %bitcast.88, bf16[1,2048,256]{2,1,0:T(8,128)(2,1)} %bitcast.90, s32[1,1,2048]{2,1,0:T(1,128)} %bitcast.111), custom_call_target="tpu_custom_call" | custom-call | tf_op jit(solution)/shard_map/attend/pallas_call | solution.py:119
  158.7 12.7 %exchange_1.1 = bf16[4,1,8,64,256]{4,3,2,1,0:T(8,128)(2,1)} custom-call(bf16[1,8,4,64,256]{4,3,2,1,0:T(8,128)(2,1)} %bitcast.92), custom_call_target="tpu_custom_call" | custom-call | tf_op jit(solution)/shard_map/exchange_1/pallas_call | solution.py:525
  173.0 1.6 copy.40.gate_w
  174.5 2.6 copy.41.up_w
  178.5 3.0 multiply_reduce_fusion.2
  184.0 65.0 %feed_forward.1 = (f32[512,1024]{1,0:T(8,128)}, bf16[4,512,1024]{2,1,0:T(8,128)(2,1)}, bf16[1024,704]{1,0:T(8,128)(2,1)}, bf16[1024,704]{1,0:T(8,128)(2,1)}, bf16[704,1024]{1,0:T(8,128)(2,1)}) custom-call(bf16[512,1024]{1,0:T(8,128)(2,1)} %multiply_convert_fusion.feed_ref, bf16[4,512,1024]{2,1,0:T(8,128)(2,1)} %bitcast.79, bf16[1024,704]{1,0:T(8,128)(2,1)} %copy.40.gate_w, ...), custom_call_target="tpu_custom_call" | custom-call | tf_op jit(solution)/shard_map/feed_forward/pallas_call | solution.py:397
  249.8 2.4 constant_dynamic-slice_fusion
  252.2 2.8 multiply_reduce_fusion
  255.0 43.9 %reduce-scatter.4.cloned.1.call-done = bf16[1,512,1024]{2,1,0:T(8,128)(2,1)} async-done(((bf16[4,512,1024]{2,1,0:T(8,128)(2,1)}), bf16[1,512,1024]{2,1,0:T(8,128)(2,1)}) %reduce-scatter.4.cloned.1.call-update) | async-done | bytes 1048592 | tf_op jit(solution)/shard_map/reduce_scatter | solution.py:1061
  298.9 3.8 convert_add_fusion
  304.0 2.6 convolution_convert_fusion
  308.3 3.3 convolution_convert_fusion.1
  312.6 12.6 %exchange_2.1 = bf16[1,8,4,64,256]{4,3,2,1,0:T(8,128)(2,1)} custom-call(bf16[4,1,8,64,256]{4,3,2,1,0:T(8,128)(2,1)} %bitcast.84), custom_call_target="tpu_custom_call" | custom-call | tf_op jit(solution)/shard_map/exchange_2/pallas_call | solution.py:525
  325.1 36.5 %attend_back.1 = (bf16[1,2048,256]{2,1,0:T(8,128)(2,1)}, bf16[1,2048,256]{2,1,0:T(8,128)(2,1)}, bf16[1,2048,256]{2,1,0:T(8,128)(2,1)}) custom-call(s32[8]{0:T(128)} %fusion.17.low_ref, bf16[1,2048,256]{2,1,0:T(8,128)(2,1)} %bitcast.87, bf16[1,2048,256]{2,1,0:T(8,128)(2,1)} %bitcast.89, bf16[1,2048,256]{2,1,0:T(8,128)(2,1)} %bitcast.91, ...), custom_call_target="tpu_custom_call" | custom-call | tf_op jit(solution)/shard_map/attend_back/pallas_call | solution.py:211
  361.6 15.0 %project_back.1 = (bf16[4,8,64,1024]{3,2,1,0:T(8,128)(2,1)}, bf16[768,1024]{1,0:T(8,128)(2,1)}) custom-call(bf16[2048,1024]{1,0:T(8,128)(2,1)} %bitcast.78, bf16[2048,256]{1,0:T(8,128)(2,1)} %bitcast.103, bf16[2048,256]{1,0:T(8,128)(2,1)} %bitcast.104, bf16[2048,256]{1,0:T(8,128)(2,1)} %bitcast.80, f32[2048,128]{1,0:T(8,128)} %get-tuple-element.135.cos_ref, ...), custom_call_target="tpu_custom_call" | custom-call | tf_op jit(solution)/shard_map/project_back/pallas_call | solution.py:900
  376.6 93.0 %all-reduce.9.cloned.1.call-done = (bf16[1024,704]{1,0:T(8,128)(2,1)}, bf16[1024,704]{1,0:T(8,128)(2,1)}, bf16[704,1024]{1,0:T(8,128)(2,1)}) async-done(((bf16[1024,704]{1,0:T(8,128)(2,1)}, bf16[1024,704]{1,0:T(8,128)(2,1)}, bf16[704,1024]{1,0:T(8,128)(2,1)}), (bf16[1024,704]{1,0:T(8,128)(2,1)}, bf16[1024,704]{1,0:T(8,128)(2,1)}, bf16[704,1024]{1,0:T(8,128)(2,1)})) %all-reduce.9.cloned.1.call-update) | async-done | bytes 4325392 | tf_op jit(solution)/shard_map/psum | solution.py:1118
  469.6 33.2 %reduce-scatter.8.cloned.1.call-done = bf16[256,1024]{1,0:T(8,128)(2,1)} async-done(((bf16[1024,1024]{1,0:T(8,128)(2,1)}), bf16[256,1024]{1,0:T(8,128)(2,1)}) %reduce-scatter.8.cloned.1.call-update) | async-done | bytes 524304 | tf_op jit(solution)/shard_map/reduce_scatter | solution.py:1090
  505.1 2.0 copy.44
  507.0 2.0 copy.45
  509.0 1.9 convert_element_type.114
  510.9 97.6 %all-reduce.7.cloned.1.call-done = (bf16[768,1024]{1,0:T(8,128)(2,1)}, bf16[256,1024]{1,0:T(8,128)(2,1)}) async-done(((bf16[768,1024]{1,0:T(8,128)(2,1)}, bf16[256,1024]{1,0:T(8,128)(2,1)}), (bf16[768,1024]{1,0:T(8,128)(2,1)}, bf16[256,1024]{1,0:T(8,128)(2,1)})) %all-reduce.7.cloned.1.call-update) | async-done | bytes 2097168 | tf_op jit(solution)/shard_map/psum | solution.py:1122
  608.6 2.2 convert_element_type.111
  610.8 1.8 fusion.19
  612.6 42.3 %reduce-scatter.6.cloned.1.call-done = bf16[1,512,1024]{2,1,0:T(8,128)(2,1)} async-done(((bf16[4,512,1024]{2,1,0:T(8,128)(2,1)}), bf16[1,512,1024]{2,1,0:T(8,128)(2,1)}) %reduce-scatter.6.cloned.1.call-update) | async-done | bytes 1048592 | tf_op jit(solution)/shard_map/reduce_scatter | solution.py:1098
  654.9 2.3 fusion.6
  657.2 3.1 fusion.5
  660.4 68.0 %exchange_3.1 = (bf16[2,4,64,1024]{3,2,1,0:T(8,128)(2,1)}, bf16[2,4,64,1024]{3,2,1,0:T(8,128)(2,1)}, bf16[8,256,256]{2,1,0:T(8,128)(2,1)}) custom-call(bf16[1,8,64,1024]{3,2,1,0:T(8,128)(2,1)} %bitcast.96, bf16[1,8,64,1024]{3,2,1,0:T(8,128)(2,1)} %bitcast.83, bf16[1,8,256,256]{3,2,1,0:T(8,128)(2,1)} %bitcast.81), custom_call_target="tpu_custom_call" | custom-call | tf_op jit(solution)/shard_map/exchange_3/pallas_call | solution.py:525
  729.8 1.8 copy.43
  732.3 18.0 %total.1 = f32[24,128]{1,0:T(8,128)} custom-call(f32[24,128]{1,0:T(8,128)} %pad_maximum_fusion.4.in_ref), custom_call_target="tpu_custom_call" | custom-call | tf_op jit(solution)/shard_map/total/pallas_call | solution.py:966
  (105 shorter events, 26.3 us)
Async XLA Ops:
  7.2 95.6 %copy-start.10 = (bf16[256,1024]{1,0:T(8,128)(2,1)S(1)}, bf16[256,1024]{1,0:T(8,128)(2,1)}, u32[]{:S(2)}) copy-start(bf16[256,1024]{1,0:T(8,128)(2,1)} %param.17) | copy-start | bytes 1572868
  7.2 171.3 %all-gather.2.cloned.1.call-start = ((), (), s32[]{:S(2)}) async-start(), calls=%async_computation.3 | async-start | bytes 2621440 | tf_op jit(solution)/shard_map/all_gather | solution.py:1053
  7.9 290.9 %reduce-scatter.4.cloned.1.call-start = ((), (), s32[]{:S(2)}) async-start(), calls=%async_computation.4 | async-start | bytes 5242880 | tf_op jit(solution)/shard_map/reduce_scatter | solution.py:1061
  9.3 1.9 copy-start.19
  11.1 91.7 %copy-start.9 = (bf16[256,1024]{1,0:T(8,128)(2,1)S(1)}, bf16[256,1024]{1,0:T(8,128)(2,1)}, u32[]{:S(2)}) copy-start(bf16[256,1024]{1,0:T(8,128)(2,1)} %param.18) | copy-start | bytes 1572868
  11.2 91.8 %copy-start.17 = (bf16[256,1024]{1,0:T(8,128)(2,1)S(1)}, bf16[256,1024]{1,0:T(8,128)(2,1)}, u32[]{:S(2)}) copy-start(bf16[256,1024]{1,0:T(8,128)(2,1)} %param.19) | copy-start | bytes 1572868
  158.7 14.2 %copy-start.26 = (bf16[1024]{0:T(1024)(128)(2,1)S(1)}, bf16[1024]{0:T(1024)(128)(2,1)}, u32[]{:S(2)}) copy-start(bf16[1024]{0:T(1024)(128)(2,1)} %param.21) | copy-start | bytes 6148
  158.7 14.2 %copy-start.13 = (bf16[1024,704]{0,1:T(8,128)(2,1)S(1)}, bf16[1024,704]{0,1:T(8,128)(2,1)}, u32[]{:S(2)}) copy-start(bf16[1024,704]{0,1:T(8,128)(2,1)} %param.22) | copy-start | bytes 4325380
  172.9 5.5 copy-start.7
  173.0 8.5 %copy-start.20 = (f32[1024]{0:T(1024)}, f32[1024]{0:T(1024)S(1)}, u32[]{:S(2)}) copy-start(f32[1024]{0:T(1024)S(1)} %convert_element_type.94) | copy-start | bytes 12292
  181.4 1.3 copy-start
  181.4 2.5 copy-start.22
  249.0 220.6 %all-reduce.9.cloned.1.call-start = ((), (), s32[]{:S(2)}) async-start(), calls=%async_computation.8 | async-start | bytes 9175040 | tf_op jit(solution)/shard_map/psum | solution.py:1118
  249.0 3.2 copy-start.21
  249.7 2.5 copy-start.1
  249.7 2.5 copy-start.23
  249.7 253.0 %reduce-scatter.8.cloned.1.call-start = ((), (), s32[]{:S(2)}) async-start(), calls=%async_computation.6 | async-start | bytes 2621440 | tf_op jit(solution)/shard_map/reduce_scatter | solution.py:1090
  255.0 49.1 %copy-start.8 = (bf16[4,512,256]{1,2,0:T(8,128)(2,1)S(1)}, bf16[4,512,256]{1,2,0:T(8,128)(2,1)}, u32[]{:S(2)}) copy-start(bf16[4,512,256]{1,2,0:T(8,128)(2,1)} %copy-done.7) | copy-start | bytes 3145732
  302.7 1.3 copy-start.3
  306.6 1.6 copy-start.4
  306.6 301.9 %all-reduce.7.cloned.1.call-start = ((), (), s32[]{:S(2)}) async-start(), calls=%async_computation.7 | async-start | bytes 4194304 | tf_op jit(solution)/shard_map/psum | solution.py:1122
  502.7 152.1 %reduce-scatter.6.cloned.1.call-start = ((), (), s32[]{:S(2)}) async-start(), calls=%async_computation.5 | async-start | bytes 5242880 | tf_op jit(solution)/shard_map/reduce_scatter | solution.py:1098
  502.8 2.1 copy-start.25
  502.8 2.2 copy-start.12
  505.0 2.0 copy-start.11
  507.0 2.0 copy-start.14
  608.6 2.2 copy-start.6
  610.8 44.0 %copy-start.18 = (f32[1024]{0:T(1024)S(1)}, f32[1024]{0:T(1024)}, u32[]{:S(2)}) copy-start(f32[1024]{0:T(1024)} %convert_element_type.93) | copy-start | bytes 12292
  612.6 44.6 %copy-start.5 = (f32[512,1024]{1,0:T(8,128)S(1)}, f32[512,1024]{1,0:T(8,128)}, u32[]{:S(2)}) copy-start(f32[512,1024]{1,0:T(8,128)} %copy-done.3) | copy-start | bytes 6291460
  729.8 1.8 copy-start.24
  729.8 23.0 %copy-start.16 = (bf16[2,4,64,1024]{3,2,1,0:T(8,128)(2,1)S(1)}, bf16[2,4,64,1024]{3,2,1,0:T(8,128)(2,1)}, u32[]{:S(2)}) copy-start(bf16[2,4,64,1024]{3,2,1,0:T(8,128)(2,1)} %get-tuple-element.58) | copy-start | bytes 3145732
  731.7 22.1 %copy-start.15 = (bf16[2,4,64,1024]{3,2,1,0:T(8,128)(2,1)S(1)}, bf16[2,4,64,1024]{3,2,1,0:T(8,128)(2,1)}, u32[]{:S(2)}) copy-start(bf16[2,4,64,1024]{3,2,1,0:T(8,128)(2,1)} %get-tuple-element.59) | copy-start | bytes 3145732
  (1 other events, 1.1 us)
Sparse Core Ops, SparseCore 0:
  9.6 43.3 all-gather.1
  249.1 49.7 reduce-scatter.3
  302.9 166.6 all-reduce.8
  472.5 30.1 reduce-scatter.7
  506.2 102.2 all-reduce.6
  610.9 43.8 reduce-scatter.5

commit v3 on v2

--- a/solution.py
+++ b/solution.py
@@ -918,67 +918,472 @@
     )(x_rows, query_g, key_g, value_g, cosine, sine, gain, weights, turn)
 
 
-def total_kernel(seq_size, tp_size, in_ref, out_ref, held, sums, seq_held, send_sem, tp_sem, seq_sem):
+class Reduce:
+    def __init__(self, place, hbm, part, core_in, pair_in, chunks, sems):
+        self.seq, self.tp, self.pairs = place
+        self.pair, self.core = self.tp // 2, lax.rem(self.tp, 2)
+        self.other = self.pair * 2 + 1 - self.core
+        self.hbm, self.part, self.core_in, self.pair_in = hbm, part, core_in, pair_in
+        self.chunks = chunks
+        self.load_sem, self.core_send, self.core_recv, self.pair_send, self.pair_recv = sems
+
+    def peer(self, offset):
+        return lax.rem(self.pair + offset, self.pairs) * 2 + self.core
+
+    def cut(self, ref, lead, c):
+        return ref.at[lead, :, c]
+
+    def load(self, offset):
+        return pltpu.make_async_copy(
+            self.hbm.at[self.peer(offset)], self.part.at[offset], self.load_sem.at[offset]
+        )
+
+    def to_core(self, offset, c):
+        lead = lax.rem(self.pair + offset, self.pairs) * 2 + 1 - self.core
+        at = offset * self.chunks + c
+        return remote(
+            self.cut(self.hbm, lead, c), self.cut(self.core_in, offset, c),
+            self.core_send.at[at], self.core_recv.at[at], (self.seq, self.other),
+        )
+
+    def to_pair(self, offset, c):
+        back = self.pairs - offset
+        return remote(
+            self.cut(self.part, offset, c), self.cut(self.pair_in, back, c),
+            self.pair_send.at[offset * self.chunks + c],
+            self.pair_recv.at[back * self.chunks + c], (self.seq, self.peer(offset)),
+        )
+
+    def from_pair(self, offset, c):
+        view, at = self.cut(self.pair_in, offset, c), offset * self.chunks + c
+        return remote(
+            view, view, self.pair_send.at[at], self.pair_recv.at[at], (self.seq, self.peer(offset))
+        )
+
+    def start(self):
+        for offset in list(range(1, self.pairs)) + [0]:
+            self.load(offset).start()
+        for c in range(self.chunks):
+            for offset in list(range(1, self.pairs)) + [0]:
+                self.to_core(offset, c).start()
+
+    def wait_loads(self):
+        for offset in range(self.pairs):
+            self.load(offset).wait()
+
+    def pass_on(self, c):
+        for offset in range(1, self.pairs):
+            self.to_core(offset, c).wait_recv()
+
+            def add(b, carry):
+                self.part[offset, b, c] = (
+                    self.part[offset, b, c].astype(jnp.float32)
+                    + self.core_in[offset, b, c].astype(jnp.float32)
+                ).astype(jnp.bfloat16)
+                return carry
+
+            lax.fori_loop(0, self.part.shape[1], add, 0)
+            self.to_pair(offset, c).start()
+
+    def arrive(self, c):
+        self.to_core(0, c).wait_recv()
+        for offset in range(1, self.pairs):
+            self.from_pair(offset, c).wait_recv()
+
+    def total(self, b, c):
+        value = self.part[0, b, c].astype(jnp.float32) + self.core_in[0, b, c].astype(jnp.float32)
+        for offset in range(1, self.pairs):
+            value = value + self.pair_in[offset, b, c].astype(jnp.float32)
+        return value
+
+    def finish(self):
+        for c in range(self.chunks):
+            for offset in range(self.pairs):
+                self.to_core(offset, c).wait_send()
+            for offset in range(1, self.pairs):
+                self.to_pair(offset, c).wait_send()
+
+
+class SeqSum:
+    def __init__(self, place, color, bits, blocks, held, sums, send_sem, recv_sem):
+        self.seq, self.tp = place
+        self.sums = sums
+        self.bits, self.blocks, self.held, self.color = bits, blocks, held, color
+        self.size = 1 << len(bits)
+        self.send_sem, self.recv_sem = send_sem, recv_sem
+        low, self.lows = color * self.size, []
+        self.flags = []
+        for n, bit in enumerate(bits):
+            flag = lax.rem(self.seq // (1 << bit), 2)
+            self.flags.append(flag)
+            self.lows.append(low)
+            low = low + flag * (self.size >> (n + 1))
+        self.lows.append(low)
+
+    def partner(self, n):
+        return (self.seq + (1 - 2 * self.flags[n]) * (1 << self.bits[n]), self.tp)
+
+    def span(self, n):
+        return pl.ds(self.lows[n + 1], self.size >> (n + 1))
+
+    def give(self, n):
+        half = self.size >> (n + 1)
+        begin = self.size - (self.size >> n)
+        source = self.blocks.at[pl.ds(self.lows[n] + (1 - self.flags[n]) * half, half)]
+        steps = len(self.bits)
+        return remote(
+            source, self.held.at[self.color, pl.ds(begin, half)],
+            self.send_sem.at[self.color * 2 * steps + n],
+            self.recv_sem.at[self.color * 2 * steps + n], self.partner(n),
+        )
+
+    def take(self, n):
+        copy = self.give(n)
+        copy.wait_recv()
+        copy.wait_send()
+        half = self.size >> (n + 1)
+        begin = self.size - (self.size >> n)
+
+        target = self.sums if n + 1 == len(self.bits) else self.blocks
+
+        def add(b, carry):
+            at = self.lows[n + 1] + b
+            target[at] = (
+                self.blocks[at].astype(jnp.float32)
+                + self.held[self.color, begin + b].astype(jnp.float32)
+            ).astype(jnp.bfloat16)
+            return carry
+
+        lax.fori_loop(0, half, add, 0)
+
+    def spread(self, n):
+        view = self.sums.at[self.span(n)]
+        at = self.color * 2 * len(self.bits) + len(self.bits) + n
+        return remote(view, view, self.send_sem.at[at], self.recv_sem.at[at], self.partner(n))
+
+    def collect(self, n):
+        half = self.size >> (n + 1)
+        view = self.sums.at[pl.ds(self.lows[n] + (1 - self.flags[n]) * half, half)]
+        at = self.color * 2 * len(self.bits) + len(self.bits) + n
+        remote(view, view, self.send_sem.at[at], self.recv_sem.at[at], self.partner(n)).wait_recv()
+
+    def steps(self):
+        count = len(self.bits)
+        self.give(0).start()
+        yield
+        for n in range(count):
+            self.take(n)
+            if n + 1 < count:
+                self.give(n + 1).start()
+            else:
+                self.spread(n).start()
+            yield
+        for n in range(count - 1, -1, -1):
+            self.collect(n)
+            if n > 0:
+                self.spread(n - 1).start()
+            yield
+        for n in range(count):
+            self.spread(n).wait_send()
+
+
+def tail_kernel(
+    sizes, dv_plan, normed_hbm, proj_hbm, out_hbm, grad_hbm, source_hbm, middle_hbm,
+    middle_g_hbm, dv_hbm, gain_ref, small_ref,
+    out_ref, input_g_ref, dv_ref, sums_ref, total_ref,
+    normed_part, normed_core, normed_pair, proj_part, proj_core, proj_pair,
+    out_part, out_core, out_pair, source, middle, middle_g, input_g, result,
+    blocks, held, sums, small, tp_held, tp_sum, seq_held,
+    *sems,
+):
+    seq_size, tp_size, rows_each, rows_local, _ = sizes
     s, t = lax.axis_index("seq"), lax.axis_index("tp")
-    barrier = pltpu.get_barrier_semaphore()
+    me = (s, t)
+    pairs = tp_size // 2
+    normed_sems, proj_sems, out_sems = sems[:5], sems[5:10], sems[10:15]
+    dv_sems, back_sems, lo_sems = sems[15:18], sems[18:21], sems[21:24]
+    load_sem, grad_send, grad_recv, small_send, tp_sem, seq_sem = sems[24:]
+    place = (s, t, pairs)
+    normed = Reduce(place, normed_hbm, normed_part, normed_core, normed_pair, 2, normed_sems)
+    proj = Reduce(place, proj_hbm, proj_part, proj_core, proj_pair, 1, proj_sems)
+    out = Reduce(place, out_hbm, out_part, out_core, out_pair, 2, out_sems)
+    dv_move = Exchange(dv_plan, me, dv_hbm, dv_ref, *dv_sems)
+    half = source.shape[0]
+    piece = source.shape[2]
+
+    group = group_of(s, seq_size)
+    origins = []
+    for slot in range(rows_local):
+        row = t * rows_local + slot
+        for i in range(tp_size):
+            origins.append(((place_of(row // rows_each, seq_size), i), (slot, i), slot * tp_size + i))
+
     tp_peers = [lax.rem(t + i, tp_size) for i in range(1, tp_size)]
     seq_peers = [lax.rem(s + i, seq_size) for i in range(1, seq_size)]
-    for other in tp_peers:
-        pl.semaphore_signal(barrier, inc=1, device_id=(s, other), device_id_type=MESH)
-    for other in seq_peers:
-        pl.semaphore_signal(barrier, inc=1, device_id=(other, t), device_id_type=MESH)
-    pl.semaphore_wait(barrier, tp_size + seq_size - 2)
+    barrier = pltpu.get_barrier_semaphore()
+    dv_move.greet(barrier)
+    for origin, _, _ in origins:
+        @pl.when(jnp.logical_not(same(origin, me)))
+        def _():
+            pl.semaphore_signal(barrier, inc=1, device_id=origin, device_id_type=MESH)
+    for to in tp_peers:
+        pl.semaphore_signal(barrier, inc=1, device_id=(s, to), device_id_type=MESH)
+    for to in seq_peers:
+        pl.semaphore_signal(barrier, inc=1, device_id=(to, t), device_id_type=MESH)
+    back_others = sum(
+        jnp.where(
+            same((to, (group * rows_each + j) // rows_local), me), 0, 1
+        )
+        for j in range(rows_each)
+        for to in range(seq_size)
+    )
+    pl.semaphore_wait(barrier, dv_move.others() + back_others + tp_size + seq_size - 2)
+
+    loads = [
+        pltpu.make_async_copy(grad_hbm, blocks.at[pl.ds(0, grad_hbm.shape[0])], load_sem.at[0]),
+        pltpu.make_async_copy(source_hbm, source, load_sem.at[1]),
+        pltpu.make_async_copy(middle_g_hbm, middle_g, load_sem.at[2]),
+        pltpu.make_async_copy(middle_hbm, middle, load_sem.at[3]),
+    ]
+    loads[0].start()
+    proj.start()
+    normed.start()
+    loads[1].start()
+    loads[2].start()
+    dv_move.start()
+    out.start()
+    loads[3].start()
+
+    order = list(range(seq_size.bit_length() - 1))
+    first = SeqSum(me, 0, order, blocks, held, sums, grad_send, grad_recv).steps()
+    second = SeqSum(me, 1, order[1:] + order[:1], blocks, held, sums, grad_send, grad_recv).steps()
+
+    loads[0].wait()
+    next(first)
+    proj.wait_loads()
+    proj.pass_on(0)
+    normed.wait_loads()
+    normed.pass_on(0)
+    normed.pass_on(1)
+    proj.arrive(0)
+
+    def put(b, carry):
+        at = grad_hbm.shape[0] + b
+        blocks[at] = proj.total(b, 0).astype(jnp.bfloat16)
+        return carry
+
+    lax.fori_loop(0, blocks.shape[0] - grad_hbm.shape[0], put, 0)
+    next(second)
+    next(first)
+    out.wait_loads()
+    out.pass_on(0)
+    out.pass_on(1)
+
+    def send_back(source_ref, target, trio, b, c, wait):
+        local_sem, send_sem, recv_sem = trio
+        flat = 2 * b + c
+        j, to = flat // seq_size, lax.rem(flat, seq_size)
+        row = group * rows_each + j
+        slot = lax.rem(row, rows_local)
+        place = (to, row // rows_local)
+        here = same(place, me)
+        view = target.at[slot, t]
+
+        @pl.when(here)
+        def _():
+            copy = pltpu.make_async_copy(source_ref.at[b, c], view, local_sem.at[flat])
+            copy.wait() if wait else copy.start()
+
+        @pl.when(jnp.logical_not(here))
+        def _():
+            copy = remote(
+                source_ref.at[b, c], view, send_sem.at[flat], recv_sem.at[slot * tp_size + t], place
+            )
+            copy.wait_send() if wait else copy.start()
+
+    gain = gain_ref[...]
+    small[...] = small_ref[...]
+
+    def back(c):
+        normed.arrive(c)
+
+        def one(n, carry):
+            b = lax.rem(n + s // 2, half)
+            grads = normed.total(b, c)
+            x = source[b, c].astype(jnp.float32)
+            inverse = lax.rsqrt(jnp.mean(x * x, axis=-1, keepdims=True) + norm_eps)
+            unit = x * inverse
+            scaled = grads * gain
+            extra = inverse * (scaled - unit * jnp.mean(scaled * unit, axis=-1, keepdims=True))
+            input_g[b, c] = (middle_g[b, c] + extra).astype(jnp.bfloat16)
+            small[0:1, :] += jnp.sum(grads * unit, axis=0, keepdims=True)
+            send_back(input_g, input_g_ref, back_sems, b, c, False)
+            return carry
+
+        lax.fori_loop(0, half, one, 0)
+
+    def forward(c):
+        out.arrive(c)
+
+        def one(n, carry):
+            b = lax.rem(n + s // 2, half)
+            result[b, c] = (middle[b, c] + out.total(b, c)).astype(jnp.bfloat16)
+            send_back(result, out_ref, lo_sems, b, c, False)
+            return carry
+
+        lax.fori_loop(0, half, one, 0)
 
     def tp_copy(n):
         return remote(
-            in_ref, held.at[tp_size - n], send_sem.at[n], tp_sem.at[tp_size - n], (s, tp_peers[n - 1])
+            small, tp_held.at[tp_size - n], small_send.at[n],
+            tp_sem.at[tp_size - n], (s, tp_peers[n - 1]),
         )
 
     def seq_copy(n):
         return remote(
-            sums, seq_held.at[seq_size - n], send_sem.at[tp_size + n],
+            tp_sum, seq_held.at[seq_size - n], small_send.at[tp_size + n],
             seq_sem.at[seq_size - n], (seq_peers[n - 1], t),
         )
 
+    next(first)
+    next(second)
+    loads[1].wait()
+    loads[2].wait()
+    back(0)
+    next(first)
+    next(second)
+    back(1)
     for n in range(1, tp_size):
         tp_copy(n).start()
+    next(first)
+    next(second)
+    loads[3].wait()
+    forward(0)
     for n in range(1, tp_size):
         tp_copy(n).wait()
-    held[0] = in_ref[...]
-    total = held[lax.rem(tp_size - t, tp_size)]
+    tp_held[0] = small[...]
+    total = tp_held[lax.rem(tp_size - t, tp_size)]
     for n in range(1, tp_size):
-        total = total + held[lax.rem(n + tp_size - t, tp_size)]
-    sums[...] = total
+        total = total + tp_held[lax.rem(n + tp_size - t, tp_size)]
+    tp_sum[...] = total
     for n in range(1, seq_size):
         seq_copy(n).start()
     seq_held[0] = total
+    next(first)
+    next(second)
+    forward(1)
+    for _ in first:
+        pass
+    for _ in second:
+        pass
     for n in range(1, seq_size):
         seq_copy(n).wait()
     total = seq_held[lax.rem(seq_size - s, seq_size)]
     for n in range(1, seq_size):
         total = total + seq_held[lax.rem(n + seq_size - s, seq_size)]
-    out_ref[...] = total
-
-
-def total_of(values, seq_size, tp_size):
-    whole = pl.BlockSpec(memory_space=pltpu.VMEM)
+    total_ref[...] = total
+    store = pltpu.make_async_copy(sums, sums_ref, load_sem.at[0])
+    store.start()
+
+    for reduce in (normed, proj, out):
+        reduce.finish()
+    for c in range(2):
+        def done(b, carry):
+            send_back(input_g, input_g_ref, back_sems, b, c, True)
+            send_back(result, out_ref, lo_sems, b, c, True)
+            return carry
+
+        lax.fori_loop(0, half, done, 0)
+    dv_move.wait_sends()
+    dv_move.wait_receives()
+    for origin, target, at in origins:
+        @pl.when(jnp.logical_not(same(origin, me)))
+        def _():
+            for ref, trio in ((input_g_ref, back_sems), (out_ref, lo_sems)):
+                view = ref.at[target]
+                remote(view, view, trio[1].at[0], trio[2].at[at], origin).wait_recv()
+    store.wait()
+
+
+def tail(normed_g, proj_grad, out_part, grads, source, middle, middle_g, value_g, gain, small, sizes):
+    seq_size, tp_size, rows_each, rows_local, _ = sizes
+    pairs = tp_size // 2
+    blocks = rows_each * seq_size
+    tokens, depth = source.shape
+    piece = tokens // blocks
+    width = proj_grad.shape[0] // tp_size
+    fine = 2 * width // seq_size
+    places = value_g.shape[2]
+    bf16, f32 = jnp.bfloat16, jnp.float32
+    shape = (blocks // 2, 2, piece, depth)
+    proj_shape = (width // fine, 1, fine, depth)
+    anywhere = pl.BlockSpec(memory_space=pl.ANY)
+    vmem = pl.BlockSpec(memory_space=pltpu.VMEM)
     dma = pltpu.SemaphoreType.DMA
+    plan = rows_to_places(seq_size, rows_each)
+    steps = seq_size.bit_length() - 1
+    owned = jax.ShapeDtypeStruct((rows_local, tp_size, piece, depth), bf16)
+
+    def reduce_sems(chunks):
+        return [dma((pairs,))] + [dma((pairs * chunks,))] * 4
+
     return pl.pallas_call(
-        functools.partial(total_kernel, seq_size, tp_size),
-        out_shape=jax.ShapeDtypeStruct(values.shape, jnp.float32),
-        in_specs=[whole],
-        out_specs=whole,
-        scratch_shapes=[
-            pltpu.VMEM((tp_size,) + values.shape, jnp.float32),
-            pltpu.VMEM(values.shape, jnp.float32),
-            pltpu.VMEM((seq_size,) + values.shape, jnp.float32),
+        functools.partial(tail_kernel, sizes, plan),
+        out_shape=[
+            owned,
+            owned,
+            jax.ShapeDtypeStruct((rows_each * seq_size, places, width), bf16),
+            jax.ShapeDtypeStruct((2 * seq_size, fine, depth), bf16),
+            jax.ShapeDtypeStruct(small.shape, f32),
+        ],
+        in_specs=[anywhere] * 8 + [vmem] * 2,
+        out_specs=[anywhere] * 4 + [vmem],
+        scratch_shapes=[pltpu.VMEM((pairs,) + shape, bf16)] * 3
+        + [pltpu.VMEM((pairs,) + proj_shape, bf16)] * 3
+        + [pltpu.VMEM((pairs,) + shape, bf16)] * 3
+        + [
+            pltpu.VMEM(shape, bf16),
+            pltpu.VMEM(shape, f32),
+            pltpu.VMEM(shape, f32),
+            pltpu.VMEM(shape, bf16),
+            pltpu.VMEM(shape, bf16),
+            pltpu.VMEM((2 * seq_size, fine, depth), bf16),
+            pltpu.VMEM((2, seq_size, fine, depth), bf16),
+            pltpu.VMEM((2 * seq_size, fine, depth), bf16),
+            pltpu.VMEM(small.shape, f32),
+            pltpu.VMEM((tp_size,) + small.shape, f32),
+            pltpu.VMEM(small.shape, f32),
+            pltpu.VMEM((seq_size,) + small.shape, f32),
+        ]
+        + reduce_sems(2)
+        + reduce_sems(1)
+        + reduce_sems(2)
+        + [dma((seq_size,))] * 3
+        + ([dma((blocks,))] * 2 + [dma((rows_local * tp_size,))]) * 2
+        + [
+            dma((4,)),
+            dma((4 * steps,)),
+            dma((4 * steps,)),
             dma((tp_size + seq_size,)),
             dma((tp_size,)),
             dma((seq_size,)),
         ],
-        compiler_params=pltpu.CompilerParams(collective_id=6, has_side_effects=True),
-        name="total",
-    )(values)
+        compiler_params=pltpu.CompilerParams(
+            collective_id=6, has_side_effects=True, vmem_limit_bytes=67043328
+        ),
+        name="tail",
+    )(
+        normed_g.reshape((tp_size,) + shape),
+        proj_grad.reshape((tp_size,) + proj_shape),
+        out_part.reshape((tp_size,) + shape),
+        grads.reshape(-1, fine, depth),
+        source.reshape(shape),
+        middle.reshape(shape),
+        middle_g.reshape(shape),
+        value_g,
+        gain,
+        small,
+    )
 
 
 def half_swap(weight):
@@ -1034,8 +1439,8 @@
         first_values,
         sizes,
     )
-    source = lax.dynamic_index_in_dim(x_rows, me, 2, keepdims=False).reshape(tokens, depth)
-    source = source.astype(jnp.float32)
+    source_low = lax.dynamic_index_in_dim(x_rows, me, 2, keepdims=False).reshape(tokens, depth)
+    source = source_low.astype(jnp.float32)
     cotangent = lax.dynamic_index_in_dim(cot_all, me, 0, keepdims=False).reshape(tokens, depth)
     cotangent = cotangent.astype(jnp.float32)
     x_rows = x_rows.reshape(rows_each * ROW, depth)
@@ -1058,8 +1463,7 @@
     feed_in_g, out_part, gate_grad, up_grad, down_grad = feed_forward(
         feed_in, cot_all.reshape(tp_size, tokens, depth), gate_weight, up_weight, down_weight
     )
-    out_sum = lax.psum_scatter(out_part, "tp", scatter_dimension=0, tiled=False)
-    layer_output = (middle + out_sum.astype(jnp.float32)).astype(jnp.bfloat16)
+    feed_sums = lax.psum((gate_grad, up_grad, down_grad), "seq")
     middle_extra, feed_gain_part = norm_back(feed_in_g, unit_feed, inv_feed, feed_scale)
     middle_g = cotangent + middle_extra
     branch_g = middle_g.astype(jnp.bfloat16)
@@ -1087,62 +1491,40 @@
         turn,
         sizes,
     )
-    output_proj_grad = lax.psum_scatter(
-        jnp.einsum("te,td->ed", attended, branch_g, preferred_element_type=jnp.float32).astype(
-            jnp.bfloat16
-        ),
-        "tp",
-        scatter_dimension=0,
-        tiled=True,
-    )
-    normed_g = lax.psum_scatter(
-        normed_g.reshape(tp_size, tokens, depth), "tp", scatter_dimension=0, tiled=False
-    ).astype(jnp.float32)
-    unit_attn, inv_attn = norm_rows(source)
-    input_extra, attn_gain_part = norm_back(normed_g, unit_attn, inv_attn, attn_scale)
-    input_grad = (middle_g + input_extra).astype(jnp.bfloat16)
-    quarter = (rows_each, seq_size, piece, depth)
-    owned = (rows_local, tp_size, piece, depth)
-    back = quarter_to_owner(seq_size, tp_size, rows_each, rows_local)
-    layer_output, input_grad, value_own_g = exchange(
-        [
-            layer_output.reshape(quarter),
-            input_grad.reshape(quarter),
-            value_g.reshape(rows_each, seq_size, local_len, width),
-        ],
-        [owned, owned, (row_count, local_len, width)],
-        [back, back, rows_to_places(seq_size, rows_each)],
-        3,
+    output_proj_grad = jnp.einsum(
+        "te,td->ed", attended, branch_g, preferred_element_type=jnp.float32
+    ).astype(jnp.bfloat16)
+    squares = jnp.pad(jnp.sum(squares, axis=1)[:2], (0, depth - 2))
+    small = jnp.stack([jnp.zeros_like(squares), feed_gain_part, squares])
+    layer_output, input_grad, value_own_g, grad_sums, small = tail(
+        normed_g,
+        output_proj_grad,
+        out_part,
+        stacked_grad,
+        source_low,
+        middle,
+        middle_g,
+        value_g.reshape(rows_each, seq_size, local_len, width),
+        attn_scale,
+        jnp.pad(small, ((0, 5), (0, 0))),
+        sizes,
     )
     first_grad = jnp.swapaxes(0.5 * value_own_g.astype(jnp.float32), 1, 2)
-    feed_sums = lax.psum((gate_grad, up_grad, down_grad), "seq")
-    stacked_grad, output_proj_grad, feed_sums = lax.optimization_barrier(
-        (stacked_grad, output_proj_grad, feed_sums)
-    )
-    stacked_total, output_proj_total = lax.psum((stacked_grad, output_proj_grad), "seq")
-    stacked_total = stacked_total.astype(jnp.float32)
-    squares = jnp.pad(jnp.sum(squares, axis=1)[:2], (0, 126))
-    small = total_of(
-        jnp.concatenate([attn_gain_part, feed_gain_part, jnp.pad(squares, (0, 7 * 128))]).reshape(
-            -1, 128
-        ),
-        seq_size,
-        tp_size,
-    ).reshape(-1)
+    grad_sums = grad_sums.reshape(4 * width, depth).astype(jnp.float32)
     return (
         layer_output.reshape(layer_input.shape),
         input_grad.reshape(layer_input.shape),
         first_grad,
-        small[:depth],
-        stacked_total[:width],
-        stacked_total[width : 2 * width],
-        stacked_total[2 * width :],
-        output_proj_total.astype(jnp.float32),
-        small[depth : 2 * depth],
+        small[0],
+        grad_sums[:width],
+        grad_sums[width : 2 * width],
+        grad_sums[2 * width : 3 * width],
+        grad_sums[3 * width :],
+        small[1],
         feed_sums[0].astype(jnp.float32),
         feed_sums[1].astype(jnp.float32),
         feed_sums[2].astype(jnp.float32),
-        jnp.sqrt(small[2 * depth : 2 * depth + 2]),
+        jnp.sqrt(small[2, :2]),
     )
 
 

time: 763 us -> 561 us (0.74)
  waiting for transfers between devices: 312 us -> 0.72 us
  Pallas kernels: 366 us -> 484 us
  other arithmetic: 32.4 us -> 20.3 us
    pallas_call x1, Pallas kernels: 18 us -> 203 us  [tail(): pl.pallas_call(functools.partial(tail_kernel, sizes, plan), out_shape=[ow...]
    reduce_scatter x3 -> x0, waiting for transfers between devices: 119 us -> none  [the longest x1 43.9 us: shards(): out_sum = lax.psum_scatter(out_part, 'tp', scatter_dimension=0, tiled=False)]
    psum x1 -> x0, waiting for transfers between devices: 97.6 us -> none  [shards(): lax.psum((stacked_grad, output_proj_grad), 'seq')]
    psum x1, waiting for transfers between devices: 93 us -> 0.01 us  [shards(): feed_sums = lax.psum((gate_grad, up_grad, down_grad), 'seq')]
    pallas_call x3 -> x2, Pallas kernels: 93.3 us -> 25.4 us  [exchange(): pl.pallas_call(kernel, out_shape=[jax.ShapeDtypeStruct(shape, array.dtype...]
    unnamed x63 -> x57, local copies, waits for them, and re-layouts: 16.3 us -> 18.8 us
  transfers between devices with their start and end apart: 6 -> 2, of which waited for: 5 -> 0; matrix products, arithmetic and copies ran while one was open for 6% -> 7% of each run, Pallas kernels for 28% -> 75%
where the time goes in v3:
time: 561 us; the launch traced here: 558 us
  Pallas kernels  484 us (86%)
  local copies, waits for them, and re-layouts  30 us (5%)
  other arithmetic  20.3 us (4%)
  between operations  14.5 us (3%)
  matrix products  9.1 us (2%)
    pallas_call x1, Pallas kernels, tail(): pl.pallas_call(functools.partial(tail_kernel, sizes, plan), out_shape=[ow...  203 us
    pallas_call x1, Pallas kernels, spread(): pl.pallas_call(functools.partial(spread_kernel, plans, sizes), out_shape=...  91.6 us
    pallas_call x1, Pallas kernels, feed_forward(): pl.pallas_call(functools.partial(feed_kernel, chunk), out_shape=[jax.Shap...  64.9 us
    pallas_call x1, Pallas kernels, attend_back(): pl.pallas_call(attend_back_kernel, grid_spec=pltpu.PrefetchScalarGridSpec...  36.7 us
    pallas_call x1, Pallas kernels, attend(): pl.pallas_call(attend_kernel, grid_spec=pltpu.PrefetchScalarGridSpec(num_...  35 us
    pallas_call x2, Pallas kernels, exchange(): pl.pallas_call(kernel, out_shape=[jax.ShapeDtypeStruct(shape, array.dtype...  25.4 us
    unnamed x57, local copies, waits for them, and re-layouts  18.8 us
    pallas_call x1, Pallas kernels, project_back(): pl.pallas_call(project_back_kernel, grid=(rows_each * seq_size,), in_spec...  15 us
  transfers between devices with their start and end apart: 2, of which 0 were waited for; matrix products, arithmetic and copies ran while one was open for 7% of the time, Pallas kernels for 75%

profile of v3, /device:TPU:0, one launch (start us, length us, event | category | flops | bytes accessed | tf_op | source)
XLA Modules:
  0.0 558.3 jit_solution(8324778252221882359)
XLA Ops:
  9.9 1.3 broadcast_in_dim.31
  11.2 91.6 %spread.1 = (bf16[1,8,4,64,1024]{4,3,2,1,0:T(8,128)(2,1)}, bf16[4,1,8,64,1024]{4,3,2,1,0:T(8,128)(2,1)}, bf16[1,8,256,256]{3,2,1,0:T(8,128)(2,1)}) custom-call(bf16[2,4,64,1024]{3,2,1,0:T(8,128)(2,1)} %bitcast.95, bf16[2,4,64,1024]{3,2,1,0:T(8,128)(2,1)} %bitcast.96, bf16[8,256,256]{2,1,0:T(8,128)(2,1)} %first_ref.1), custom_call_target="tpu_custom_call" | custom-call | tf_op jit(solution)/shard_map/spread/pallas_call | solution.py:770
  104.1 1.0 pad_maximum_fusion.swapped_ref
  105.1 5.5 multiply_sine_fusion
  110.6 11.8 %project.1 = (bf16[2048,256]{1,0:T(8,128)(2,1)}, bf16[2048,256]{1,0:T(8,128)(2,1)}, bf16[2048,256]{1,0:T(8,128)(2,1)}, f32[8,256]{1,0:T(8,128)}) custom-call(bf16[2048,1024]{1,0:T(8,128)(2,1)} %bitcast.67, bf16[1,8,256,256]{3,2,1,0:T(8,128)(2,1)} %get-tuple-element.40.first_ref, f32[2048,128]{1,0:T(8,128)} %get-tuple-element.124.cos_ref, ...), custom_call_target="tpu_custom_call" | custom-call | tf_op jit(solution)/shard_map/project/pallas_call | solution.py:831
  122.4 1.2 fusion.7.low_ref
  123.7 35.0 %attend.1 = (bf16[1,2048,256]{2,1,0:T(8,128)(2,1)}, f32[1,2,2,2048]{3,2,1,0:T(2,128)}) custom-call(s32[8]{0:T(128)} %fusion.7.low_ref, bf16[1,2048,256]{2,1,0:T(8,128)(2,1)} %bitcast.81, bf16[1,2048,256]{2,1,0:T(8,128)(2,1)} %bitcast.83, bf16[1,2048,256]{2,1,0:T(8,128)(2,1)} %bitcast.85, s32[1,1,2048]{2,1,0:T(1,128)} %bitcast.107), custom_call_target="tpu_custom_call" | custom-call | tf_op jit(solution)/shard_map/attend/pallas_call | solution.py:119
  158.7 12.7 %exchange_1.1 = bf16[4,1,8,64,256]{4,3,2,1,0:T(8,128)(2,1)} custom-call(bf16[1,8,4,64,256]{4,3,2,1,0:T(8,128)(2,1)} %bitcast.87), custom_call_target="tpu_custom_call" | custom-call | tf_op jit(solution)/shard_map/exchange_1/pallas_call | solution.py:525
  171.4 1.5 copy.39
  172.9 1.6 copy.40.gate_w
  174.5 2.6 copy.41.up_w
  177.0 1.3 constant_dynamic-slice_fusion
  178.4 3.3 multiply_reduce_fusion.2
  181.8 1.3 copy-done
  183.0 1.2 multiply_convert_fusion.feed_ref
  184.3 64.9 %feed_forward.1 = (f32[512,1024]{1,0:T(8,128)}, bf16[4,512,1024]{2,1,0:T(8,128)(2,1)}, bf16[1024,704]{1,0:T(8,128)(2,1)}, bf16[1024,704]{1,0:T(8,128)(2,1)}, bf16[704,1024]{1,0:T(8,128)(2,1)}) custom-call(bf16[512,1024]{1,0:T(8,128)(2,1)} %multiply_convert_fusion.feed_ref, bf16[4,512,1024]{2,1,0:T(8,128)(2,1)} %bitcast.72, bf16[1024,704]{1,0:T(8,128)(2,1)} %copy.40.gate_w, ...), custom_call_target="tpu_custom_call" | custom-call | tf_op jit(solution)/shard_map/feed_forward/pallas_call | solution.py:397
  250.8 1.3 constant_dynamic-slice_fusion.1
  252.1 2.3 multiply_reduce_fusion
  256.1 1.3 convolution_convert_fusion.1
  258.4 12.7 %exchange_2.1 = bf16[1,8,4,64,256]{4,3,2,1,0:T(8,128)(2,1)} custom-call(bf16[4,1,8,64,256]{4,3,2,1,0:T(8,128)(2,1)} %bitcast.77), custom_call_target="tpu_custom_call" | custom-call | tf_op jit(solution)/shard_map/exchange_2/pallas_call | solution.py:525
  271.8 36.7 %attend_back.1 = (bf16[1,2048,256]{2,1,0:T(8,128)(2,1)}, bf16[1,2048,256]{2,1,0:T(8,128)(2,1)}, bf16[1,2048,256]{2,1,0:T(8,128)(2,1)}) custom-call(s32[8]{0:T(128)} %fusion.7.low_ref, bf16[1,2048,256]{2,1,0:T(8,128)(2,1)} %bitcast.82, bf16[1,2048,256]{2,1,0:T(8,128)(2,1)} %bitcast.84, bf16[1,2048,256]{2,1,0:T(8,128)(2,1)} %bitcast.86, ...), custom_call_target="tpu_custom_call" | custom-call | tf_op jit(solution)/shard_map/attend_back/pallas_call | solution.py:211
  308.4 15.0 %project_back.1 = (bf16[4,8,64,1024]{3,2,1,0:T(8,128)(2,1)}, bf16[768,1024]{1,0:T(8,128)(2,1)}) custom-call(bf16[2048,1024]{1,0:T(8,128)(2,1)} %bitcast.68, bf16[2048,256]{1,0:T(8,128)(2,1)} %bitcast.97, bf16[2048,256]{1,0:T(8,128)(2,1)} %bitcast.98, bf16[2048,256]{1,0:T(8,128)(2,1)} %bitcast.75, f32[2048,128]{1,0:T(8,128)} %get-tuple-element.124.cos_ref, ...), custom_call_target="tpu_custom_call" | custom-call | tf_op jit(solution)/shard_map/project_back/pallas_call | solution.py:900
  323.4 4.5 convolution_convert_fusion
  327.9 203.3 %tail.1 = (bf16[2,4,64,1024]{3,2,1,0:T(8,128)(2,1)}, bf16[2,4,64,1024]{3,2,1,0:T(8,128)(2,1)}, bf16[8,256,256]{2,1,0:T(8,128)(2,1)}, bf16[16,64,1024]{2,1,0:T(8,128)(2,1)}, f32[8,1024]{1,0:T(8,128)}) custom-call(bf16[4,4,2,64,1024]{4,3,2,1,0:T(8,128)(2,1)} %bitcast.74, bf16[4,4,1,64,1024]{4,3,2,1,0:T(8,128)(2,1)} %bitcast.89, ...), custom_call_target="tpu_custom_call" | custom-call | tf_op jit(solution)/shard_map/tail/pallas_call | solution.py:1330
  531.2 2.7 multiply_bitcast_fusion
  534.0 3.0 copy.43
  537.0 1.2 sqrt_bitcast_fusion
  538.2 1.4 fusion.10
  539.6 2.2 fusion.9
  541.9 3.1 copy.44
  545.0 2.0 copy.45
  546.9 1.9 convert_element_type.80
  (81 shorter events, 11.4 us)
Async XLA Ops:
  7.2 95.6 %copy-start.10 = (bf16[256,1024]{1,0:T(8,128)(2,1)S(1)}, bf16[256,1024]{1,0:T(8,128)(2,1)}, u32[]{:S(2)}) copy-start(bf16[256,1024]{1,0:T(8,128)(2,1)} %param.17) | copy-start | bytes 1572868
  7.2 171.2 %all-gather.2.cloned.1.call-start = ((), (), s32[]{:S(2)}) async-start(), calls=%async_computation | async-start | bytes 2621440 | tf_op jit(solution)/shard_map/all_gather | solution.py:1458
  7.9 533.9 %all-reduce.5.cloned.1.call-start = ((), (), s32[]{:S(2)}) async-start(), calls=%async_computation.1 | async-start | bytes 9175040 | tf_op jit(solution)/shard_map/psum | solution.py:1466
  9.3 1.9 copy-start.17
  11.1 91.7 %copy-start.9 = (bf16[256,1024]{1,0:T(8,128)(2,1)S(1)}, bf16[256,1024]{1,0:T(8,128)(2,1)}, u32[]{:S(2)}) copy-start(bf16[256,1024]{1,0:T(8,128)(2,1)} %param.18) | copy-start | bytes 1572868
  11.2 91.8 %copy-start.16 = (bf16[256,1024]{1,0:T(8,128)(2,1)S(1)}, bf16[256,1024]{1,0:T(8,128)(2,1)}, u32[]{:S(2)}) copy-start(bf16[256,1024]{1,0:T(8,128)(2,1)} %param.19) | copy-start | bytes 1572868
  103.0 1.1 copy-start.3
  158.6 14.2 %copy-start.23 = (bf16[1024]{0:T(1024)(128)(2,1)S(1)}, bf16[1024]{0:T(1024)(128)(2,1)}, u32[]{:S(2)}) copy-start(bf16[1024]{0:T(1024)(128)(2,1)} %param.21) | copy-start | bytes 6148
  158.7 14.2 %copy-start.12 = (bf16[1024,704]{0,1:T(8,128)(2,1)S(1)}, bf16[1024,704]{0,1:T(8,128)(2,1)}, u32[]{:S(2)}) copy-start(bf16[1024,704]{0,1:T(8,128)(2,1)} %param.22) | copy-start | bytes 4325380
  172.9 5.5 copy-start.7
  172.9 8.9 %copy-start.18 = (f32[1024]{0:T(1024)}, f32[1024]{0:T(1024)S(1)}, u32[]{:S(2)}) copy-start(f32[1024]{0:T(1024)S(1)} %convert_element_type.70) | copy-start | bytes 12292
  178.4 3.4 copy-start.2
  181.7 1.3 copy-start
  181.7 2.5 copy-start.20
  249.2 0.7 copy-start.22
  249.2 2.9 copy-start.1
  249.2 2.9 copy-start.19
  249.2 2.9 copy-start.21
  252.1 2.3 copy-start.5
  254.5 1.6 copy-start.8
  256.1 1.3 copy-start.4
  534.0 5.7 %copy-start.6 = (bf16[16,64,1024]{2,1,0:T(8,128)(2,1)S(1)}, bf16[16,64,1024]{2,1,0:T(8,128)(2,1)}, u32[]{:S(2)}) copy-start(bf16[16,64,1024]{2,1,0:T(8,128)(2,1)} %get-tuple-element.61) | copy-start | bytes 6291460
  541.9 3.1 copy-start.11
  545.0 2.0 copy-start.13
  546.9 1.9 copy-start.15
  548.9 1.6 copy-start.14
Sparse Core Ops, SparseCore 0:
  9.6 43.3 all-gather.1
  249.3 253.5 all-reduce.4

commit v4 on v3

--- a/solution.py
+++ b/solution.py
@@ -56,32 +56,43 @@
     return jnp.where(lanes // HD == head, block, jnp.zeros_like(block))
 
 
+def lane_group(head, width):
+    lanes = min(width, 128)
+    return slice(head * HD // lanes * lanes, head * HD // lanes * lanes + lanes), head % (lanes // HD)
+
+
 def attend_kernel(low_ref, q_ref, k_ref, v_ref, start_ref, o_ref, lse_ref, v_cols):
     row = pl.program_id(0)
-    length, lanes = q_ref.shape[1:]
-    heads = lanes // HD
+    length, width = q_ref.shape[1:]
+    heads = width // HD
+    together = min(width, 128) // HD
     blocks = length // BLOCK
     for j in range(blocks):
         v_cols[:, j * BLOCK : (j + 1) * BLOCK] = v_ref[0, j * BLOCK : (j + 1) * BLOCK, :].T
 
     def query_block(i, carry):
         first = pl.multiple_of(i * BLOCK, BLOCK)
-        q_block = q_ref[0, pl.ds(first, BLOCK), :]
-        q_heads = [head_masked(q_block, h, heads) for h in range(heads)]
+        q_heads = []
+        for h in range(heads):
+            lanes, at = lane_group(h, width)
+            q_heads.append(head_masked(q_ref[0, pl.ds(first, BLOCK), lanes], at, together))
         start = start_ref[0, :, pl.ds(first, BLOCK)]
         places = first + lax.broadcasted_iota(jnp.int32, (1, BLOCK), 1)
 
         def key_block(j, state):
             at = pl.multiple_of(j * BLOCK, BLOCK)
-            k_block = k_ref[0, pl.ds(at, BLOCK), :]
             keys = at + lax.broadcasted_iota(jnp.int32, (BLOCK, BLOCK), 0)
             allowed = (keys >= start) & (keys <= places)
+            scores = [
+                rows_dot(k_ref[0, pl.ds(at, BLOCK), lane_group(h, width)[0]], q_heads[h])
+                for h in range(heads)
+            ]
             out = []
             for h in range(heads):
                 top, total, acc = state[h]
-                scores = jnp.where(allowed, rows_dot(k_block, q_heads[h]), masked_score)
-                new_top = jnp.maximum(top, jnp.max(scores, axis=0, keepdims=True))
-                weights = jnp.exp2(scores - new_top)
+                masked = jnp.where(allowed, scores[h], masked_score)
+                new_top = jnp.maximum(top, jnp.max(masked, axis=0, keepdims=True))
+                weights = jnp.exp2(masked - new_top)
                 shrink = jnp.exp2(top - new_top)
                 total = total * shrink + jnp.sum(weights, axis=0, keepdims=True)
                 acc = acc * shrink + plain_dot(
@@ -104,7 +115,7 @@
         o_ref[0, pl.ds(first, BLOCK), :] = columns.T.astype(jnp.bfloat16)
         for h in range(heads):
             top, total, _ = state[h]
-            lse_ref[0, 0, pl.ds(h, 1), pl.ds(first, BLOCK)] = top + jnp.log2(total)
+            lse_ref[0, pl.ds(h, 1), pl.ds(first, BLOCK)] = top + jnp.log2(total)
         return carry
 
     lax.fori_loop(0, blocks, query_block, 0)
@@ -112,26 +123,22 @@
 
 def attend(low, queries, keys, values, starts):
     rows, length, width = queries.shape
-    lanes = min(width, 128)
-    groups = width // lanes
-    heads = lanes // HD
-    wide = pl.BlockSpec((1, length, lanes), lambda r, g, low: (r, 0, g))
+    heads = width // HD
+    wide = pl.BlockSpec((1, length, width), lambda r, low: (r, 0, 0))
     return pl.pallas_call(
         attend_kernel,
         grid_spec=pltpu.PrefetchScalarGridSpec(
             num_scalar_prefetch=1,
-            grid=(rows, groups),
-            in_specs=[wide, wide, wide, pl.BlockSpec((1, 1, length), lambda r, g, low: (r, 0, 0))],
-            out_specs=[
-                wide,
-                pl.BlockSpec((1, 1, heads, length), lambda r, g, low: (r, g, 0, 0)),
-            ],
-            scratch_shapes=[pltpu.VMEM((lanes, length), jnp.bfloat16)],
+            grid=(rows,),
+            in_specs=[wide, wide, wide, pl.BlockSpec((1, 1, length), lambda r, low: (r, 0, 0))],
+            out_specs=[wide, pl.BlockSpec((1, heads, length), lambda r, low: (r, 0, 0))],
+            scratch_shapes=[pltpu.VMEM((width, length), jnp.bfloat16)],
         ),
         out_shape=[
             jax.ShapeDtypeStruct(queries.shape, jnp.bfloat16),
-            jax.ShapeDtypeStruct((rows, groups, heads, length), jnp.float32),
+            jax.ShapeDtypeStruct((rows, heads, length), jnp.float32),
         ],
+        compiler_params=pltpu.CompilerParams(vmem_limit_bytes=67043328),
         name="attend",
     )(low, queries, keys, values, starts)
 
@@ -141,54 +148,56 @@
     qg_ref, kg_ref, vg_ref, k_cols, k_acc, v_acc,
 ):
     row = pl.program_id(0)
-    length, lanes = q_ref.shape[1:]
-    heads = lanes // HD
+    length, width = q_ref.shape[1:]
+    heads = width // HD
+    together = min(width, 128) // HD
     blocks = length // BLOCK
     for j in range(blocks):
         k_cols[:, j * BLOCK : (j + 1) * BLOCK] = k_ref[0, j * BLOCK : (j + 1) * BLOCK, :].T
     k_acc[...] = jnp.zeros_like(k_acc)
     v_acc[...] = jnp.zeros_like(v_acc)
     select = (
-        lax.broadcasted_iota(jnp.int32, (8, lanes), 1) // HD
-        == lax.broadcasted_iota(jnp.int32, (8, lanes), 0)
+        lax.broadcasted_iota(jnp.int32, (8, width), 1) // HD
+        == lax.broadcasted_iota(jnp.int32, (8, width), 0)
     ).astype(jnp.float32)
 
     def query_block(i, carry):
         first = pl.multiple_of(i * BLOCK, BLOCK)
-        q_block = q_ref[0, pl.ds(first, BLOCK), :]
-        g_block = g_ref[0, pl.ds(first, BLOCK), :]
-        q_heads = [head_masked(q_block, h, heads) for h in range(heads)]
-        g_heads = [head_masked(g_block, h, heads) for h in range(heads)]
-        product = g_block.astype(jnp.float32) * o_ref[0, pl.ds(first, BLOCK), :].astype(jnp.float32)
+        q_heads, g_heads = [], []
+        for h in range(heads):
+            lanes, at = lane_group(h, width)
+            q_heads.append(head_masked(q_ref[0, pl.ds(first, BLOCK), lanes], at, together))
+            g_heads.append(head_masked(g_ref[0, pl.ds(first, BLOCK), lanes], at, together))
+        product = g_ref[0, pl.ds(first, BLOCK), :].astype(jnp.float32) * o_ref[
+            0, pl.ds(first, BLOCK), :
+        ].astype(jnp.float32)
         centre = lax.dot_general(
             select, product, (((1,), (1,)), ((), ())),
             precision=lax.Precision.HIGHEST, preferred_element_type=jnp.float32,
         )
-        lse = lse_ref[0, 0, :, pl.ds(first, BLOCK)]
+        lse = lse_ref[0, :, pl.ds(first, BLOCK)]
         start = start_ref[0, :, pl.ds(first, BLOCK)]
         places = first + lax.broadcasted_iota(jnp.int32, (1, BLOCK), 1)
 
         def key_block(j, state):
             at = pl.multiple_of(j * BLOCK, BLOCK)
-            k_block = k_ref[0, pl.ds(at, BLOCK), :]
-            v_block = v_ref[0, pl.ds(at, BLOCK), :]
             keys = at + lax.broadcasted_iota(jnp.int32, (BLOCK, BLOCK), 0)
             allowed = (keys >= start) & (keys <= places)
-            k_add = jnp.zeros((BLOCK, lanes), jnp.float32)
-            v_add = jnp.zeros((BLOCK, lanes), jnp.float32)
+            scores, prob_gs = [], []
+            for h in range(heads):
+                lanes, _ = lane_group(h, width)
+                scores.append(rows_dot(k_ref[0, pl.ds(at, BLOCK), lanes], q_heads[h]))
+                prob_gs.append(rows_dot(v_ref[0, pl.ds(at, BLOCK), lanes], g_heads[h]))
             out = []
             for h in range(heads):
-                scores = jnp.where(allowed, rows_dot(k_block, q_heads[h]), masked_score)
-                probs = jnp.exp2(scores - lse[h : h + 1, :])
-                prob_g = rows_dot(v_block, g_heads[h])
-                score_g = (probs * (prob_g - centre[h : h + 1, :])).astype(jnp.bfloat16)
-                v_add = v_add + plain_dot(probs.astype(jnp.bfloat16), g_heads[h])
-                k_add = k_add + plain_dot(score_g, q_heads[h])
+                lanes, _ = lane_group(h, width)
+                probs = jnp.exp2(jnp.where(allowed, scores[h], masked_score) - lse[h : h + 1, :])
+                score_g = (probs * (prob_gs[h] - centre[h : h + 1, :])).astype(jnp.bfloat16)
+                v_acc[pl.ds(at, BLOCK), lanes] += plain_dot(probs.astype(jnp.bfloat16), g_heads[h])
+                k_acc[pl.ds(at, BLOCK), lanes] += plain_dot(score_g, q_heads[h])
                 out.append(
                     state[h] + plain_dot(k_cols[h * HD : (h + 1) * HD, pl.ds(at, BLOCK)], score_g)
                 )
-            k_acc[pl.ds(at, BLOCK), :] += k_add
-            v_acc[pl.ds(at, BLOCK), :] += v_add
             return tuple(out)
 
         begin = tuple(jnp.zeros((HD, BLOCK), jnp.float32) for _ in range(heads))
@@ -204,28 +213,27 @@
 
 def attend_back(low, queries, keys, values, attended, grads, lse, starts):
     rows, length, width = queries.shape
-    lanes = min(width, 128)
-    groups = width // lanes
-    heads = lanes // HD
-    wide = pl.BlockSpec((1, length, lanes), lambda r, g, low: (r, 0, g))
+    heads = width // HD
+    wide = pl.BlockSpec((1, length, width), lambda r, low: (r, 0, 0))
     return pl.pallas_call(
         attend_back_kernel,
         grid_spec=pltpu.PrefetchScalarGridSpec(
             num_scalar_prefetch=1,
-            grid=(rows, groups),
+            grid=(rows,),
             in_specs=[wide] * 5
             + [
-                pl.BlockSpec((1, 1, heads, length), lambda r, g, low: (r, g, 0, 0)),
-                pl.BlockSpec((1, 1, length), lambda r, g, low: (r, 0, 0)),
+                pl.BlockSpec((1, heads, length), lambda r, low: (r, 0, 0)),
+                pl.BlockSpec((1, 1, length), lambda r, low: (r, 0, 0)),
             ],
             out_specs=[wide] * 3,
             scratch_shapes=[
-                pltpu.VMEM((lanes, length), jnp.bfloat16),
-                pltpu.VMEM((length, lanes), jnp.float32),
-                pltpu.VMEM((length, lanes), jnp.float32),
+                pltpu.VMEM((width, length), jnp.bfloat16),
+                pltpu.VMEM((length, width), jnp.float32),
+                pltpu.VMEM((length, width), jnp.float32),
             ],
         ),
         out_shape=[jax.ShapeDtypeStruct(queries.shape, jnp.bfloat16)] * 3,
+        compiler_params=pltpu.CompilerParams(vmem_limit_bytes=67043328),
         name="attend_back",
     )(low, queries, keys, values, attended, grads, lse, starts)
 
@@ -236,8 +244,8 @@
 
 def feed_kernel(
     chunk, feed_ref, cot_ref, gate_w, up_w, down_w,
-    feed_g_ref, out_ref, gate_grad_ref, up_grad_ref, down_grad_ref,
-    feed_all, part, core_in, pair_in, gate_acc, up_acc, down_acc,
+    feed_g_ref, out_ref, keep_ref, give_ref,
+    feed_all, part, core_in, pair_in, acc,
     feed_send, feed_core, feed_pair, relay_send, part_send, part_core, sum_send, sum_pair,
 ):
     tokens = feed_ref.shape[0]
@@ -309,9 +317,7 @@
         for offset in range(1, pairs):
             feed_to_pair(offset, c).start()
     feed_all[me] = feed_ref[...]
-    gate_acc[...] = jnp.zeros_like(gate_acc)
-    up_acc[...] = jnp.zeros_like(up_acc)
-    down_acc[...] = jnp.zeros_like(down_acc)
+    acc[...] = jnp.zeros_like(acc)
 
     def step(n, carry):
         which = lax.rem(n, 2)
@@ -330,8 +336,8 @@
 
         feed = feed_all[owner, rows(c), :]
         cot = cot_ref[owner, rows(c), :]
-        gate = plain_dot(feed, gate_w[...])
-        up = plain_dot(feed, up_w[...])
+        gate = rows_dot(feed, gate_w[...])
+        up = rows_dot(feed, up_w[...])
         sigmoid = jax.nn.sigmoid(gate)
         activated = gate * sigmoid
         hidden = (activated * up).astype(jnp.bfloat16)
@@ -339,7 +345,7 @@
         up_g = (hidden_g * activated).astype(jnp.bfloat16)
         gate_g = (hidden_g * up * sigmoid * (1.0 + gate * (1.0 - sigmoid))).astype(jnp.bfloat16)
         part[owner, rows(c), :] = (
-            rows_dot(gate_g, gate_w[...]) + rows_dot(up_g, up_w[...])
+            plain_dot(gate_g, gate_w[...]) + plain_dot(up_g, up_w[...])
         ).astype(jnp.bfloat16)
 
         @pl.when(which == 1)
@@ -347,9 +353,9 @@
             part_to_core(offset, c).start()
 
         out_ref[owner, rows(c), :] = plain_dot(hidden, down_w[...]).astype(jnp.bfloat16)
-        gate_acc[...] += columns_dot(feed, gate_g)
-        up_acc[...] += columns_dot(feed, up_g)
-        down_acc[...] += columns_dot(hidden, cot)
+        acc[0] += columns_dot(gate_g, feed)
+        acc[1] += columns_dot(up_g, feed)
+        acc[2] += columns_dot(hidden, cot)
 
         @pl.when((which == 1) & (offset > 0))
         def _():
@@ -364,9 +370,13 @@
         return carry
 
     lax.fori_loop(0, 2 * chunks * pairs, step, 0)
-    gate_grad_ref[...] = gate_acc[...].astype(jnp.bfloat16)
-    up_grad_ref[...] = up_acc[...].astype(jnp.bfloat16)
-    down_grad_ref[...] = down_acc[...].astype(jnp.bfloat16)
+    half = acc.shape[1] // 2
+    flag = lax.rem(seq, 2)
+    for n in range(3):
+        keep_ref[n] = acc[n, pl.ds(pl.multiple_of(flag * half, 8), half), :].astype(jnp.bfloat16)
+        give_ref[n] = acc[n, pl.ds(pl.multiple_of((1 - flag) * half, 8), half), :].astype(
+            jnp.bfloat16
+        )
     for c in range(chunks):
         part_to_core(0, c).wait_recv()
         for offset in range(1, pairs):
@@ -391,7 +401,7 @@
     pairs = tp_size // 2
     chunk = min(tokens, 256)
     chunks = tokens // chunk
-    hidden = gate_weight.shape[1]
+    hidden = gate_weight.shape[0]
     whole = pl.BlockSpec(memory_space=pltpu.VMEM)
     dma = pltpu.SemaphoreType.DMA
     return pl.pallas_call(
@@ -399,20 +409,17 @@
         out_shape=[
             jax.ShapeDtypeStruct((tokens, width), jnp.float32),
             jax.ShapeDtypeStruct(cot_all.shape, jnp.bfloat16),
-            jax.ShapeDtypeStruct((width, hidden), jnp.bfloat16),
-            jax.ShapeDtypeStruct((width, hidden), jnp.bfloat16),
-            jax.ShapeDtypeStruct((hidden, width), jnp.bfloat16),
+            jax.ShapeDtypeStruct((3, hidden // 2, width), jnp.bfloat16),
+            jax.ShapeDtypeStruct((3, hidden // 2, width), jnp.bfloat16),
         ],
         in_specs=[whole] * 5,
-        out_specs=[whole] * 5,
+        out_specs=[whole] * 4,
         scratch_shapes=[
             pltpu.VMEM(cot_all.shape, jnp.bfloat16),
             pltpu.VMEM(cot_all.shape, jnp.bfloat16),
             pltpu.VMEM((pairs, tokens, width), jnp.bfloat16),
             pltpu.VMEM((pairs, tokens, width), jnp.bfloat16),
-            pltpu.VMEM((width, hidden), jnp.float32),
-            pltpu.VMEM((width, hidden), jnp.float32),
-            pltpu.VMEM((hidden, width), jnp.float32),
+            pltpu.VMEM((3, hidden, width), jnp.float32),
         ]
         + [dma((pairs * chunks,))] * 8,
         compiler_params=pltpu.CompilerParams(
@@ -634,10 +641,13 @@
 
 
 def spread_kernel(
-    plans, sizes, x_ref, cot_ref, first_ref, x_out, cot_out, first_out,
+    plans, sizes, x_ref, cot_ref, first_ref, output_ref, q_w, k_w, v_w, offset_ref, frequency_ref,
+    gain_ref,
+    x_out, cot_out, first_out, output_out, q_ref, k_ref, v_ref, cos_ref, sin_ref, square_ref,
+    x_rows, first_rows, q_turned, k_turned,
     x_local, x_send, x_receive, cot_local, cot_send, cot_receive,
     first_local, first_send, first_receive,
-    core_send, core_receive, pair_send, pair_receive, relay_send,
+    core_send, core_receive, pair_send, pair_receive, relay_send, load_sem, output_sem,
 ):
     seq_size, tp_size, rows_each, rows_local, parts = sizes
     me = (lax.axis_index("seq"), lax.axis_index("tp"))
@@ -664,20 +674,25 @@
         move.start()
 
     def block(out, tensor, piece, part):
+        if tensor == 2:
+            return out.at[piece]
         span = pl.ds(part * each, each)
         return out.at[:, span, piece] if tensor == 0 else out.at[piece, :, span]
 
     def number(tensor, offset, part):
         return (tensor * pairs + offset) * parts + part
 
+    def own(out, tensor, part):
+        return output_ref if tensor == 2 else block(out, tensor, t, part)
+
     def to_core(out, tensor, part):
         view, at = block(out, tensor, t, part), number(tensor, 0, part)
-        return remote(view, view, core_send.at[at], core_receive.at[at], (s, other))
+        return remote(own(out, tensor, part), view, core_send.at[at], core_receive.at[at], (s, other))
 
     def to_pair(out, tensor, offset, part):
         view = block(out, tensor, t, part)
         return remote(
-            view, view, pair_send.at[number(tensor, offset, part)],
+            own(out, tensor, part), view, pair_send.at[number(tensor, offset, part)],
             pair_receive.at[number(tensor, pairs - offset, part)], (s, peer(offset)),
         )
 
@@ -727,10 +742,16 @@
         lax.fori_loop(0, parts, receive, 0)
         lax.fori_loop(0, parts, relays, 0)
 
-    def finish(move, out, tensor):
+    def arrive(out, tensor):
         def one(part, carry):
             for offset in range(pairs):
                 from_core(out, tensor, offset, part).wait_recv()
+            return carry
+
+        lax.fori_loop(0, parts, one, 0)
+
+    def finish(move, out, tensor):
+        def one(part, carry):
             to_core(out, tensor, part).wait_send()
             for offset in range(1, pairs):
                 to_pair(out, tensor, offset, part).wait_send()
@@ -746,17 +767,113 @@
                     move.send_sem.at[n], move.receive_sem.at[at], to,
                 ).wait_send()
 
+    blocks, _, piece, depth = x_rows.shape
+    places = tp_size * piece
+    width = q_w.shape[0]
+    lanes = cos_ref.shape[2]
+    output_copy = pltpu.make_async_copy(output_ref, output_out.at[t], output_sem)
+    output_copy.start()
+    turn = half_turn(width)
+    q_turned[...] = plain_dot(turn, q_w[...]).astype(jnp.bfloat16)
+    k_turned[...] = plain_dot(turn, k_w[...]).astype(jnp.bfloat16)
+    square_ref[...] = jnp.zeros_like(square_ref)
+
+    def tables(n, carry):
+        angles = frequency_ref[...] * offset_ref[n]
+        cos_ref[n] = jnp.concatenate([jnp.cos(angles)] * (2 * lanes // HD), axis=0).T
+        sin_ref[n] = jnp.concatenate([jnp.sin(angles)] * (2 * lanes // HD), axis=0).T
+        return carry
+
+    lax.fori_loop(0, blocks, tables, 0)
+
+    def x_load(n):
+        source = x_out.at[n // seq_size, lax.rem(n, seq_size)]
+        return pltpu.make_async_copy(source, x_rows.at[n], load_sem.at[n])
+
+    def first_load(n):
+        source = first_out.at[n // seq_size, lax.rem(n, seq_size)]
+        return pltpu.make_async_copy(source, first_rows.at[n], load_sem.at[n])
+
+    def start_loads(load):
+        def one(n, carry):
+            load(n).start()
+            return carry
+
+        lax.fori_loop(0, blocks, one, 0)
+
+    def query_key(n, carry):
+        x_load(n).wait()
+        x = x_rows[n].reshape(places, depth).astype(jnp.float32)
+        inverse = lax.rsqrt(jnp.mean(x * x, axis=-1, keepdims=True) + norm_eps)
+        normed = (x * inverse * gain_ref[...]).astype(jnp.bfloat16)
+        cosine, sine = widen(cos_ref[n], width), widen(sin_ref[n], width)
+        q_ref[n] = (
+            (rows_dot(normed, q_w[...]) * cosine + rows_dot(normed, q_turned[...]) * sine)
+            * (HD ** (-0.5) * LOG2E)
+        ).astype(jnp.bfloat16)
+        k_ref[n] = (
+            rows_dot(normed, k_w[...]) * cosine + rows_dot(normed, k_turned[...]) * sine
+        ).astype(jnp.bfloat16)
+        x_rows[n] = normed.reshape(x_rows.shape[1:])
+        return carry
+
+    def mix(n, carry):
+        first_load(n).wait()
+        first = first_rows[n].astype(jnp.float32)
+        value = rows_dot(x_rows[n].reshape(places, depth), v_w[...])
+        mixed = (0.5 * value + 0.5 * first.T).astype(jnp.bfloat16)
+        v_ref[n] = mixed
+        wide = mixed.astype(jnp.float32)
+        square_ref[0:1, : first.shape[1]] += jnp.sum(first * first, axis=0, keepdims=True)
+        square_ref[1:2, : wide.shape[1]] += jnp.sum(wide * wide, axis=0, keepdims=True)
+        return carry
+
     forward(x_move, x_out, 0)
+    to_core(output_out, 2, 0).start()
+    for offset in range(1, pairs):
+        to_pair(output_out, 2, offset, 0).start()
+    arrive(x_out, 0)
+    start_loads(x_load)
+    lax.fori_loop(0, blocks, query_key, 0)
+    first_move.wait_sends()
+    first_move.wait_receives()
+    start_loads(first_load)
+    lax.fori_loop(0, blocks, mix, 0)
+    for offset in range(1, pairs):
+        from_pair(output_out, 2, offset, 0).wait_recv()
+        relay(output_out, 2, offset, 0).start()
     forward(cot_move, cot_out, 1)
+    arrive(cot_out, 1)
+    for offset in range(pairs):
+        from_core(output_out, 2, offset, 0).wait_recv()
+    to_core(output_out, 2, 0).wait_send()
+    for offset in range(1, pairs):
+        to_pair(output_out, 2, offset, 0).wait_send()
+        relay(output_out, 2, offset, 0).wait_send()
     finish(x_move, x_out, 0)
     finish(cot_move, cot_out, 1)
-    first_move.wait_sends()
-    first_move.wait_receives()
-
-
-def spread(layer_input, cotangent, first_values, sizes):
+    output_copy.wait()
+
+
+def half_turn(width):
+    row = lax.broadcasted_iota(jnp.int32, (width, width), 0)
+    column = lax.broadcasted_iota(jnp.int32, (width, width), 1)
+    low = lax.rem(row, HD) < HD // 2
+    minus = low & (column == row + HD // 2)
+    plus = jnp.logical_not(low) & (column == row - HD // 2)
+    return jnp.where(plus, 1.0, jnp.where(minus, -1.0, 0.0)).astype(jnp.bfloat16)
+
+
+def spread(
+    layer_input, cotangent, first_values, output_weight, query_weight, key_weight, value_weight,
+    offsets, frequency, gain, sizes,
+):
     seq_size, tp_size, rows_each, rows_local, parts = sizes
     pieces = layer_input.shape[2:]
+    width, depth = query_weight.shape
+    features, places = first_values.shape[1:]
+    blocks = rows_each * seq_size
+    lanes = min(width, 128)
     plans = (
         owner_to_quarter(seq_size, tp_size, rows_each, rows_local, False),
         owner_to_quarter(seq_size, tp_size, rows_each, rows_local, True),
@@ -766,223 +883,107 @@
     quarter = [
         dma((rows_local * tp_size,)), dma((rows_local * tp_size,)), dma((rows_each * seq_size,)),
     ]
-    stage = tp_size // 2 * parts * 2
+    stage = tp_size // 2 * parts * 3
+    bf16, f32 = jnp.bfloat16, jnp.float32
+    anywhere = pl.BlockSpec(memory_space=pl.ANY)
+    vmem = pl.BlockSpec(memory_space=pltpu.VMEM)
+    part = jax.ShapeDtypeStruct((blocks, places, width), bf16)
+    table = jax.ShapeDtypeStruct((blocks, places, lanes), f32)
     return pl.pallas_call(
         functools.partial(spread_kernel, plans, sizes),
         out_shape=[
-            jax.ShapeDtypeStruct((rows_each, seq_size, tp_size) + pieces, jnp.bfloat16),
-            jax.ShapeDtypeStruct((tp_size, rows_each, seq_size) + pieces, jnp.bfloat16),
-            jax.ShapeDtypeStruct((rows_each, seq_size) + first_values.shape[1:], jnp.bfloat16),
+            jax.ShapeDtypeStruct((rows_each, seq_size, tp_size) + pieces, bf16),
+            jax.ShapeDtypeStruct((tp_size, rows_each, seq_size) + pieces, bf16),
+            jax.ShapeDtypeStruct((rows_each, seq_size, features, places), bf16),
+            jax.ShapeDtypeStruct((tp_size,) + output_weight.shape, bf16),
+            part,
+            part,
+            part,
+            table,
+            table,
+            jax.ShapeDtypeStruct((8, max(width, places)), f32),
         ],
-        in_specs=[pl.BlockSpec(memory_space=pl.ANY)] * 3,
-        out_specs=[pl.BlockSpec(memory_space=pl.ANY)] * 3,
-        scratch_shapes=quarter + quarter + [dma((seq_size,))] * 3 + [dma((stage,))] * 5,
-        compiler_params=pltpu.CompilerParams(collective_id=5, has_side_effects=True),
+        in_specs=[anywhere] * 3 + [vmem] * 7,
+        out_specs=[anywhere] * 4 + [vmem] * 6,
+        scratch_shapes=[
+            pltpu.VMEM((blocks, tp_size) + pieces, bf16),
+            pltpu.VMEM((blocks, features, places), bf16),
+            pltpu.VMEM((width, depth), bf16),
+            pltpu.VMEM((width, depth), bf16),
+        ]
+        + quarter
+        + quarter
+        + [dma((seq_size,))] * 3
+        + [dma((stage,))] * 5
+        + [dma((blocks,)), dma],
+        compiler_params=pltpu.CompilerParams(
+            collective_id=5, has_side_effects=True, vmem_limit_bytes=67043328
+        ),
         name="spread",
-    )(layer_input, cotangent, first_values)
+    )(
+        layer_input, cotangent, first_values, output_weight, query_weight, key_weight,
+        value_weight, offsets, frequency, gain,
+    )
 
 
 def widen(table, width):
     return jnp.concatenate([table] * (width // table.shape[1]), axis=1)
 
 
-def project_kernel(
-    x_ref, first_ref, cos_ref, sin_ref, gain_ref, weight_ref, swapped_ref,
-    q_ref, k_ref, v_ref, square_ref,
-):
-    width = q_ref.shape[1]
-    x = x_ref[...].astype(jnp.float32)
-    inverse = lax.rsqrt(jnp.mean(x * x, axis=-1, keepdims=True) + norm_eps)
-    normed = (x * inverse * gain_ref[...]).astype(jnp.bfloat16)
-    straight = rows_dot(normed, weight_ref[...])
-    swapped = rows_dot(normed, swapped_ref[...])
-    cosine, sine = widen(cos_ref[...], width), widen(sin_ref[...], width)
-    q_ref[...] = (
-        (straight[:, :width] * cosine + swapped[:, :width] * sine) * (HD ** (-0.5) * LOG2E)
-    ).astype(jnp.bfloat16)
-    k_ref[...] = (
-        straight[:, width : 2 * width] * cosine + swapped[:, width:] * sine
-    ).astype(jnp.bfloat16)
-    first = first_ref[0, 0].astype(jnp.float32)
-    mixed = (0.5 * straight[:, 2 * width :] + 0.5 * first.T).astype(jnp.bfloat16)
-    v_ref[...] = mixed
-    wide = mixed.astype(jnp.float32)
-
-    @pl.when(pl.program_id(0) == 0)
-    def _():
-        square_ref[...] = jnp.zeros_like(square_ref)
-
-    square_ref[0:1, :] += jnp.sum(first * first, axis=0, keepdims=True)
-    square_ref[1:2, : wide.shape[1]] += jnp.sum(wide * wide, axis=0, keepdims=True)
-
-
-def project(x_rows, first_rows, cosine, sine, gain, weights, swapped):
-    tokens, depth = x_rows.shape
-    rows_each, seq_size, width, places = first_rows.shape
-    lanes = cosine.shape[1]
-
-    def tile(columns):
-        return pl.BlockSpec((places, columns), lambda n: (n, 0))
-
-    def fixed(array):
-        return pl.BlockSpec(array.shape, lambda n: (0,) * array.ndim)
-
-    square = jax.ShapeDtypeStruct((8, max(width, places)), jnp.float32)
-    return pl.pallas_call(
-        project_kernel,
-        grid=(rows_each * seq_size,),
-        in_specs=[
-            tile(depth),
-            pl.BlockSpec((1, 1, width, places), lambda n: (n // seq_size, n % seq_size, 0, 0)),
-            tile(lanes),
-            tile(lanes),
-            fixed(gain),
-            fixed(weights),
-            fixed(swapped),
-        ],
-        out_specs=[tile(width)] * 3 + [fixed(square)],
-        out_shape=[jax.ShapeDtypeStruct((tokens, width), jnp.bfloat16)] * 3 + [square],
-        compiler_params=pltpu.CompilerParams(vmem_limit_bytes=67043328),
-        name="project",
-    )(x_rows, first_rows, cosine, sine, gain, weights, swapped)
-
-
-def project_back_kernel(
-    x_ref, q_ref, k_ref, v_ref, cos_ref, sin_ref, gain_ref, weight_ref, turn_ref,
-    normed_g_ref, grad_ref, grad_acc,
-):
-    width = q_ref.shape[1]
-    x = x_ref[...].astype(jnp.float32)
-    inverse = lax.rsqrt(jnp.mean(x * x, axis=-1, keepdims=True) + norm_eps)
-    normed = (x * inverse * gain_ref[...]).astype(jnp.bfloat16)
-    cosine, sine = widen(cos_ref[...], width), widen(sin_ref[...], width)
-
-    def unrotate(grad):
-        turned = plain_dot(grad, turn_ref[...])
-        return (grad.astype(jnp.float32) * cosine + turned * sine).astype(jnp.bfloat16)
-
-    stacked = jnp.concatenate(
-        [
-            unrotate(q_ref[...]),
-            unrotate(k_ref[...]),
-            (0.5 * v_ref[...].astype(jnp.float32)).astype(jnp.bfloat16),
-        ],
-        axis=1,
-    )
-    normed_g_ref[...] = plain_dot(stacked, weight_ref[...]).astype(jnp.bfloat16).reshape(
-        normed_g_ref.shape
-    )
-
-    @pl.when(pl.program_id(0) == 0)
-    def _():
-        grad_acc[...] = jnp.zeros_like(grad_acc)
-
-    grad_acc[...] += columns_dot(stacked, normed)
-
-    @pl.when(pl.program_id(0) == pl.num_programs(0) - 1)
-    def _():
-        grad_ref[...] = grad_acc[...].astype(jnp.bfloat16)
-
-
-def project_back(x_rows, query_g, key_g, value_g, cosine, sine, gain, weights, turn, sizes):
-    seq_size, tp_size, rows_each, _, _ = sizes
-    tokens, depth = x_rows.shape
-    places = tokens // (rows_each * seq_size)
-    width, lanes = query_g.shape[1], cosine.shape[1]
-    piece = places // tp_size
-
-    def tile(columns):
-        return pl.BlockSpec((places, columns), lambda n: (n, 0))
-
-    def fixed(array):
-        return pl.BlockSpec(array.shape, lambda n: (0,) * array.ndim)
-
-    return pl.pallas_call(
-        project_back_kernel,
-        grid=(rows_each * seq_size,),
-        in_specs=[
-            tile(depth), tile(width), tile(width), tile(width), tile(lanes), tile(lanes),
-            fixed(gain), fixed(weights), fixed(turn),
-        ],
-        out_specs=[
-            pl.BlockSpec((tp_size, 1, piece, depth), lambda n: (0, n, 0, 0)),
-            fixed(weights),
-        ],
-        out_shape=[
-            jax.ShapeDtypeStruct((tp_size, rows_each * seq_size, piece, depth), jnp.bfloat16),
-            jax.ShapeDtypeStruct(weights.shape, jnp.bfloat16),
-        ],
-        scratch_shapes=[pltpu.VMEM(weights.shape, jnp.float32)],
-        compiler_params=pltpu.CompilerParams(vmem_limit_bytes=67043328),
-        name="project_back",
-    )(x_rows, query_g, key_g, value_g, cosine, sine, gain, weights, turn)
-
-
 class Reduce:
-    def __init__(self, place, hbm, part, core_in, pair_in, chunks, sems):
+    def __init__(self, place, full, core_in, pair_in, chunks, sems):
         self.seq, self.tp, self.pairs = place
         self.pair, self.core = self.tp // 2, lax.rem(self.tp, 2)
         self.other = self.pair * 2 + 1 - self.core
-        self.hbm, self.part, self.core_in, self.pair_in = hbm, part, core_in, pair_in
+        self.full, self.core_in, self.pair_in = full, core_in, pair_in
         self.chunks = chunks
-        self.load_sem, self.core_send, self.core_recv, self.pair_send, self.pair_recv = sems
+        self.core_send, self.core_recv, self.pair_send, self.pair_recv = sems
 
     def peer(self, offset):
         return lax.rem(self.pair + offset, self.pairs) * 2 + self.core
 
     def cut(self, ref, lead, c):
         return ref.at[lead, :, c]
-
-    def load(self, offset):
-        return pltpu.make_async_copy(
-            self.hbm.at[self.peer(offset)], self.part.at[offset], self.load_sem.at[offset]
-        )
 
     def to_core(self, offset, c):
         lead = lax.rem(self.pair + offset, self.pairs) * 2 + 1 - self.core
         at = offset * self.chunks + c
         return remote(
-            self.cut(self.hbm, lead, c), self.cut(self.core_in, offset, c),
+            self.cut(self.full, lead, c), self.cut(self.core_in, offset, c),
             self.core_send.at[at], self.core_recv.at[at], (self.seq, self.other),
         )
 
     def to_pair(self, offset, c):
         back = self.pairs - offset
         return remote(
-            self.cut(self.part, offset, c), self.cut(self.pair_in, back, c),
+            self.cut(self.full, self.peer(offset), c), self.cut(self.pair_in, back - 1, c),
             self.pair_send.at[offset * self.chunks + c],
             self.pair_recv.at[back * self.chunks + c], (self.seq, self.peer(offset)),
         )
 
     def from_pair(self, offset, c):
-        view, at = self.cut(self.pair_in, offset, c), offset * self.chunks + c
+        view, at = self.cut(self.pair_in, offset - 1, c), offset * self.chunks + c
         return remote(
             view, view, self.pair_send.at[at], self.pair_recv.at[at], (self.seq, self.peer(offset))
         )
 
-    def start(self):
+    def start(self, c):
         for offset in list(range(1, self.pairs)) + [0]:
-            self.load(offset).start()
-        for c in range(self.chunks):
-            for offset in list(range(1, self.pairs)) + [0]:
-                self.to_core(offset, c).start()
-
-    def wait_loads(self):
-        for offset in range(self.pairs):
-            self.load(offset).wait()
+            self.to_core(offset, c).start()
 
     def pass_on(self, c):
         for offset in range(1, self.pairs):
             self.to_core(offset, c).wait_recv()
+            to = self.peer(offset)
 
             def add(b, carry):
-                self.part[offset, b, c] = (
-                    self.part[offset, b, c].astype(jnp.float32)
+                self.full[to, b, c] = (
+                    self.full[to, b, c].astype(jnp.float32)
                     + self.core_in[offset, b, c].astype(jnp.float32)
                 ).astype(jnp.bfloat16)
                 return carry
 
-            lax.fori_loop(0, self.part.shape[1], add, 0)
+            lax.fori_loop(0, self.full.shape[1], add, 0)
             self.to_pair(offset, c).start()
 
     def arrive(self, c):
@@ -991,9 +992,10 @@
             self.from_pair(offset, c).wait_recv()
 
     def total(self, b, c):
-        value = self.part[0, b, c].astype(jnp.float32) + self.core_in[0, b, c].astype(jnp.float32)
+        value = self.full[self.tp, b, c].astype(jnp.float32)
+        value = value + self.core_in[0, b, c].astype(jnp.float32)
         for offset in range(1, self.pairs):
-            value = value + self.pair_in[offset, b, c].astype(jnp.float32)
+            value = value + self.pair_in[offset - 1, b, c].astype(jnp.float32)
         return value
 
     def finish(self):
@@ -1005,111 +1007,121 @@
 
 
 class SeqSum:
-    def __init__(self, place, color, bits, blocks, held, sums, send_sem, recv_sem):
+    def __init__(self, place, steps, done, blocks, held, mine, sums, local_sem, send_sem, recv_sem):
         self.seq, self.tp = place
-        self.sums = sums
-        self.bits, self.blocks, self.held, self.color = bits, blocks, held, color
-        self.size = 1 << len(bits)
-        self.send_sem, self.recv_sem = send_sem, recv_sem
-        low, self.lows = color * self.size, []
-        self.flags = []
-        for n, bit in enumerate(bits):
-            flag = lax.rem(self.seq // (1 << bit), 2)
-            self.flags.append(flag)
+        self.count, self.done, self.size = steps, done, 1 << steps
+        self.blocks, self.held, self.mine, self.sums = blocks, held, mine, sums
+        self.local_sem, self.send_sem, self.recv_sem = local_sem, send_sem, recv_sem
+        self.flags = [lax.rem(self.seq // (1 << n), 2) for n in range(steps)]
+        low, self.lows = 0, [0]
+        for n in range(steps):
+            low = low + self.flags[n] * (self.size >> (n + 1))
             self.lows.append(low)
-            low = low + flag * (self.size >> (n + 1))
-        self.lows.append(low)
 
     def partner(self, n):
-        return (self.seq + (1 - 2 * self.flags[n]) * (1 << self.bits[n]), self.tp)
-
-    def span(self, n):
-        return pl.ds(self.lows[n + 1], self.size >> (n + 1))
+        return (self.seq + (1 - 2 * self.flags[n]) * (1 << n), self.tp)
+
+    def half(self, n):
+        return self.size >> (n + 1)
+
+    def begin(self, n):
+        return (self.size >> self.done) - (self.size >> n)
 
     def give(self, n):
-        half = self.size >> (n + 1)
-        begin = self.size - (self.size >> n)
-        source = self.blocks.at[pl.ds(self.lows[n] + (1 - self.flags[n]) * half, half)]
-        steps = len(self.bits)
+        half = self.half(n)
+        low = self.lows[n] - self.lows[self.done] + (1 - self.flags[n]) * half
         return remote(
-            source, self.held.at[self.color, pl.ds(begin, half)],
-            self.send_sem.at[self.color * 2 * steps + n],
-            self.recv_sem.at[self.color * 2 * steps + n], self.partner(n),
+            self.blocks.at[pl.ds(low, half)], self.held.at[pl.ds(self.begin(n), half)],
+            self.send_sem.at[n], self.recv_sem.at[n], self.partner(n),
         )
 
     def take(self, n):
         copy = self.give(n)
         copy.wait_recv()
         copy.wait_send()
-        half = self.size >> (n + 1)
-        begin = self.size - (self.size >> n)
-
-        target = self.sums if n + 1 == len(self.bits) else self.blocks
+        last = n + 1 == self.count
 
         def add(b, carry):
-            at = self.lows[n + 1] + b
-            target[at] = (
+            at = self.lows[n + 1] - self.lows[self.done] + b
+            value = (
                 self.blocks[at].astype(jnp.float32)
-                + self.held[self.color, begin + b].astype(jnp.float32)
+                + self.held[self.begin(n) + b].astype(jnp.float32)
             ).astype(jnp.bfloat16)
+            if last:
+                self.mine[b] = value
+            else:
+                self.blocks[at] = value
             return carry
 
-        lax.fori_loop(0, half, add, 0)
+        lax.fori_loop(0, self.half(n), add, 0)
+
+    def store(self):
+        return pltpu.make_async_copy(
+            self.mine, self.sums.at[pl.ds(self.lows[self.count], 1)], self.local_sem
+        )
 
     def spread(self, n):
-        view = self.sums.at[self.span(n)]
-        at = self.color * 2 * len(self.bits) + len(self.bits) + n
-        return remote(view, view, self.send_sem.at[at], self.recv_sem.at[at], self.partner(n))
+        target = self.sums.at[pl.ds(self.lows[n + 1], self.half(n))]
+        source = self.mine if n + 1 == self.count else target
+        at = self.count + n
+        return remote(source, target, self.send_sem.at[at], self.recv_sem.at[at], self.partner(n))
 
     def collect(self, n):
-        half = self.size >> (n + 1)
+        half = self.half(n)
         view = self.sums.at[pl.ds(self.lows[n] + (1 - self.flags[n]) * half, half)]
-        at = self.color * 2 * len(self.bits) + len(self.bits) + n
+        at = self.count + n
         remote(view, view, self.send_sem.at[at], self.recv_sem.at[at], self.partner(n)).wait_recv()
 
     def steps(self):
-        count = len(self.bits)
-        self.give(0).start()
+        self.give(self.done).start()
         yield
-        for n in range(count):
+        for n in range(self.done, self.count):
             self.take(n)
-            if n + 1 < count:
+            if n + 1 < self.count:
                 self.give(n + 1).start()
             else:
                 self.spread(n).start()
+                self.store().start()
             yield
-        for n in range(count - 1, -1, -1):
+        for n in range(self.count - 1, -1, -1):
             self.collect(n)
+            if n + 1 == self.count:
+                self.store().wait()
             if n > 0:
                 self.spread(n - 1).start()
             yield
-        for n in range(count):
+        for n in range(self.count):
             self.spread(n).wait_send()
 
 
 def tail_kernel(
-    sizes, dv_plan, normed_hbm, proj_hbm, out_hbm, grad_hbm, source_hbm, middle_hbm,
-    middle_g_hbm, dv_hbm, gain_ref, small_ref,
-    out_ref, input_g_ref, dv_ref, sums_ref, total_ref,
-    normed_part, normed_core, normed_pair, proj_part, proj_core, proj_pair,
-    out_part, out_core, out_pair, source, middle, middle_g, input_g, result,
-    blocks, held, sums, small, tp_held, tp_sum, seq_held,
+    sizes, dv_plan, out_hbm, keep_hbm, got_hbm, x_hbm, q_hbm, k_hbm, v_hbm, cos_hbm, sin_hbm,
+    qw_hbm, kw_hbm, vw_hbm, attended_hbm, source_hbm, middle_hbm, middle_g_hbm, dv_hbm, gain_ref, small_ref,
+    out_ref, input_g_ref, dv_ref, sums_ref, feed_ref, total_ref,
+    x_rows, q_rows, k_rows, v_rows, cos_rows, sin_rows, weights, attended, grad_acc,
+    normed_full, normed_core, normed_pair, proj_full, proj_core, proj_pair,
+    out_full, out_core, out_pair, source, middle, middle_g, input_g, result,
+    blocks, held, mine, feed_blocks, feed_got, feed_held, feed_mine,
+    small, tp_held, tp_sum, seq_held,
     *sems,
 ):
     seq_size, tp_size, rows_each, rows_local, _ = sizes
     s, t = lax.axis_index("seq"), lax.axis_index("tp")
     me = (s, t)
     pairs = tp_size // 2
-    normed_sems, proj_sems, out_sems = sems[:5], sems[5:10], sems[10:15]
-    dv_sems, back_sems, lo_sems = sems[15:18], sems[18:21], sems[21:24]
-    load_sem, grad_send, grad_recv, small_send, tp_sem, seq_sem = sems[24:]
+    count = seq_size.bit_length() - 1
+    normed_sems, proj_sems, out_sems = sems[:4], sems[4:8], sems[8:12]
+    dv_sems, back_sems, lo_sems = sems[12:15], sems[15:18], sems[18:21]
+    load_sem, x_sem, feed_sem, store_sem, grad_send, grad_recv = sems[21:27]
+    feed_send, feed_recv, small_send, tp_sem, seq_sem = sems[27:]
     place = (s, t, pairs)
-    normed = Reduce(place, normed_hbm, normed_part, normed_core, normed_pair, 2, normed_sems)
-    proj = Reduce(place, proj_hbm, proj_part, proj_core, proj_pair, 1, proj_sems)
-    out = Reduce(place, out_hbm, out_part, out_core, out_pair, 2, out_sems)
+    normed = Reduce(place, normed_full, normed_core, normed_pair, 2, normed_sems)
+    proj = Reduce(place, proj_full, proj_core, proj_pair, 1, proj_sems)
+    out = Reduce(place, out_full, out_core, out_pair, 2, out_sems)
     dv_move = Exchange(dv_plan, me, dv_hbm, dv_ref, *dv_sems)
     half = source.shape[0]
-    piece = source.shape[2]
+    places, depth = x_rows.shape[1:]
+    width = q_rows.shape[2]
 
     group = group_of(s, seq_size)
     origins = []
@@ -1120,6 +1132,43 @@
 
     tp_peers = [lax.rem(t + i, tp_size) for i in range(1, tp_size)]
     seq_peers = [lax.rem(s + i, seq_size) for i in range(1, seq_size)]
+
+    names = (
+        (q_hbm, q_rows), (k_hbm, k_rows), (v_hbm, v_rows), (cos_hbm, cos_rows),
+        (sin_hbm, sin_rows), (qw_hbm, weights.at[pl.ds(0, width)]),
+        (kw_hbm, weights.at[pl.ds(width, width)]), (vw_hbm, weights.at[pl.ds(2 * width, width)]),
+        (out_hbm, out_full), (attended_hbm, attended),
+        (middle_g_hbm, middle_g), (source_hbm, source), (middle_hbm, middle),
+    )
+    loads = [
+        pltpu.make_async_copy(origin, target, load_sem.at[n])
+        for n, (origin, target) in enumerate(names)
+    ]
+    feed_loads = [
+        (
+            pltpu.make_async_copy(keep_hbm.at[n], feed_blocks.at[n], feed_sem.at[2 * n]),
+            pltpu.make_async_copy(got_hbm.at[n], feed_got.at[n], feed_sem.at[2 * n + 1]),
+        )
+        for n in range(3)
+    ]
+
+    def x_load(n):
+        return pltpu.make_async_copy(x_hbm.at[n], x_rows.at[n], x_sem.at[n])
+
+    def ordered(n):
+        return 2 * lax.rem(n, half) + n // half
+
+    for pair in feed_loads:
+        for copy in pair:
+            copy.start()
+    loads[8].start()
+    for copy in loads[:8]:
+        copy.start()
+    for n in range(2 * half):
+        x_load(ordered(n)).start()
+    for copy in loads[9:]:
+        copy.start()
+
     barrier = pltpu.get_barrier_semaphore()
     dv_move.greet(barrier)
     for origin, _, _ in origins:
@@ -1131,53 +1180,115 @@
     for to in seq_peers:
         pl.semaphore_signal(barrier, inc=1, device_id=(to, t), device_id_type=MESH)
     back_others = sum(
-        jnp.where(
-            same((to, (group * rows_each + j) // rows_local), me), 0, 1
-        )
+        jnp.where(same((to, (group * rows_each + j) // rows_local), me), 0, 1)
         for j in range(rows_each)
         for to in range(seq_size)
     )
     pl.semaphore_wait(barrier, dv_move.others() + back_others + tp_size + seq_size - 2)
 
-    loads = [
-        pltpu.make_async_copy(grad_hbm, blocks.at[pl.ds(0, grad_hbm.shape[0])], load_sem.at[0]),
-        pltpu.make_async_copy(source_hbm, source, load_sem.at[1]),
-        pltpu.make_async_copy(middle_g_hbm, middle_g, load_sem.at[2]),
-        pltpu.make_async_copy(middle_hbm, middle, load_sem.at[3]),
+    def seq_sum(n, done, *refs):
+        return SeqSum(
+            me, count, done, *refs, store_sem.at[n],
+            (grad_send if done == 0 else feed_send).at[n if done == 0 else n - 2],
+            (grad_recv if done == 0 else feed_recv).at[n if done == 0 else n - 2],
+        ).steps()
+
+    sums = [
+        seq_sum(n, 0, blocks.at[n], held.at[n], mine.at[n], sums_ref.at[n]) for n in range(2)
     ]
-    loads[0].start()
-    proj.start()
-    normed.start()
-    loads[1].start()
-    loads[2].start()
+    feeds = [
+        seq_sum(
+            n + 2, 1, feed_blocks.at[n], feed_held.at[n], feed_mine.at[n], feed_ref.at[n]
+        )
+        for n in range(3)
+    ]
+
+    for n in range(3):
+        for copy in feed_loads[n]:
+            copy.wait()
+
+        def join(b, carry):
+            feed_blocks[n, b] = (
+                feed_blocks[n, b].astype(jnp.float32) + feed_got[n, b].astype(jnp.float32)
+            ).astype(jnp.bfloat16)
+            return carry
+
+        lax.fori_loop(0, feed_blocks.shape[1], join, 0)
+        next(feeds[n])
+    loads[8].wait()
+    out.start(0)
+    out.start(1)
     dv_move.start()
-    out.start()
-    loads[3].start()
-
-    order = list(range(seq_size.bit_length() - 1))
-    first = SeqSum(me, 0, order, blocks, held, sums, grad_send, grad_recv).steps()
-    second = SeqSum(me, 1, order[1:] + order[:1], blocks, held, sums, grad_send, grad_recv).steps()
-
-    loads[0].wait()
-    next(first)
-    proj.wait_loads()
-    proj.pass_on(0)
-    normed.wait_loads()
-    normed.pass_on(0)
-    normed.pass_on(1)
-    proj.arrive(0)
-
-    def put(b, carry):
-        at = grad_hbm.shape[0] + b
-        blocks[at] = proj.total(b, 0).astype(jnp.bfloat16)
-        return carry
-
-    lax.fori_loop(0, blocks.shape[0] - grad_hbm.shape[0], put, 0)
-    next(second)
-    next(first)
-    out.wait_loads()
+    for copy in loads[:8]:
+        copy.wait()
+    turn = half_turn(width)
+    grad_acc[...] = jnp.zeros_like(grad_acc)
+    gain = gain_ref[...]
+
+    def project_back(first, last):
+        def one(n, carry):
+            at = ordered(n)
+            x_load(at).wait()
+            x = x_rows[at].astype(jnp.float32)
+            inverse = lax.rsqrt(jnp.mean(x * x, axis=-1, keepdims=True) + norm_eps)
+            rows = (x * inverse * gain).astype(jnp.bfloat16)
+            cosine, sine = widen(cos_rows[at], width), widen(sin_rows[at], width)
+
+            def unrotate(grad):
+                turned = plain_dot(grad, turn)
+                return (grad.astype(jnp.float32) * cosine + turned * sine).astype(jnp.bfloat16)
+
+            stacked = jnp.concatenate(
+                [
+                    unrotate(q_rows[at]),
+                    unrotate(k_rows[at]),
+                    (0.5 * v_rows[at].astype(jnp.float32)).astype(jnp.bfloat16),
+                ],
+                axis=1,
+            )
+            b, c = at // 2, lax.rem(at, 2)
+            product = plain_dot(stacked, weights[...])
+            for i in range(tp_size):
+                piece = places // tp_size
+                normed_full[i, b, c] = product[i * piece : (i + 1) * piece].astype(jnp.bfloat16)
+            grad_acc[...] += columns_dot(stacked, rows)
+            return carry
+
+        lax.fori_loop(first, last, one, 0)
+
+    quarter = half // 2
+    project_back(0, quarter)
     out.pass_on(0)
     out.pass_on(1)
+    next(feeds[0])
+    project_back(quarter, half)
+    normed.start(0)
+    next(feeds[1])
+    project_back(half, half + quarter)
+    normed.pass_on(0)
+    next(feeds[2])
+    next(feeds[0])
+    project_back(half + quarter, 2 * half)
+    normed.start(1)
+    fine = blocks.shape[2]
+    for n in range(3 * seq_size // 2):
+        blocks[n // seq_size, n % seq_size] = grad_acc[n * fine : (n + 1) * fine].astype(
+            jnp.bfloat16
+        )
+    next(sums[0])
+    next(feeds[1])
+    loads[9].wait()
+    loads[10].wait()
+    branch = middle_g[...].reshape(2 * half * middle_g.shape[2], depth).astype(jnp.bfloat16)
+    for i in range(tp_size):
+        product = columns_dot(attended[i], branch)
+        for n in range(seq_size // 2):
+            proj_full[i, n, 0] = product[n * fine : (n + 1) * fine].astype(jnp.bfloat16)
+    proj.start(0)
+    normed.pass_on(1)
+    proj.pass_on(0)
+    next(feeds[2])
+    next(feeds[0])
 
     def send_back(source_ref, target, trio, b, c, wait):
         local_sem, send_sem, recv_sem = trio
@@ -1201,7 +1312,6 @@
             )
             copy.wait_send() if wait else copy.start()
 
-    gain = gain_ref[...]
     small[...] = small_ref[...]
 
     def back(c):
@@ -1245,20 +1355,30 @@
             seq_sem.at[seq_size - n], (seq_peers[n - 1], t),
         )
 
-    next(first)
-    next(second)
-    loads[1].wait()
-    loads[2].wait()
+    def all_steps(generators):
+        for generator in generators:
+            next(generator, None)
+
+    loads[12].wait()
+    forward(0)
+    forward(1)
+    next(feeds[1])
+    loads[11].wait()
     back(0)
-    next(first)
-    next(second)
+    proj.arrive(0)
+
+    def put(b, carry):
+        blocks[1, seq_size // 2 + b] = proj.total(b, 0).astype(jnp.bfloat16)
+        return carry
+
+    lax.fori_loop(0, seq_size // 2, put, 0)
+    next(sums[1])
+    next(sums[0])
+    next(feeds[2])
     back(1)
     for n in range(1, tp_size):
         tp_copy(n).start()
-    next(first)
-    next(second)
-    loads[3].wait()
-    forward(0)
+    all_steps([feeds[0], sums[0], sums[1]])
     for n in range(1, tp_size):
         tp_copy(n).wait()
     tp_held[0] = small[...]
@@ -1269,21 +1389,17 @@
     for n in range(1, seq_size):
         seq_copy(n).start()
     seq_held[0] = total
-    next(first)
-    next(second)
-    forward(1)
-    for _ in first:
-        pass
-    for _ in second:
-        pass
+    for _ in range(2 * count):
+        all_steps([feeds[1], sums[0], feeds[2], sums[1], feeds[0]])
+    for generator in sums + feeds:
+        for _ in generator:
+            pass
     for n in range(1, seq_size):
         seq_copy(n).wait()
     total = seq_held[lax.rem(seq_size - s, seq_size)]
     for n in range(1, seq_size):
         total = total + seq_held[lax.rem(n + seq_size - s, seq_size)]
     total_ref[...] = total
-    store = pltpu.make_async_copy(sums, sums_ref, load_sem.at[0])
-    store.start()
 
     for reduce in (normed, proj, out):
         reduce.finish()
@@ -1302,21 +1418,26 @@
             for ref, trio in ((input_g_ref, back_sems), (out_ref, lo_sems)):
                 view = ref.at[target]
                 remote(view, view, trio[1].at[0], trio[2].at[at], origin).wait_recv()
-    store.wait()
-
-
-def tail(normed_g, proj_grad, out_part, grads, source, middle, middle_g, value_g, gain, small, sizes):
+
+
+def tail(
+    out_part, keep, got, x_rows, query_g, key_g, value_g, cosine, sine, query_weight, key_weight, value_weight,
+    attended, source, middle, middle_g, gain, small, sizes,
+):
     seq_size, tp_size, rows_each, rows_local, _ = sizes
     pairs = tp_size // 2
     blocks = rows_each * seq_size
     tokens, depth = source.shape
     piece = tokens // blocks
-    width = proj_grad.shape[0] // tp_size
+    width = query_g.shape[-1]
+    places = x_rows.shape[0] // blocks
+    lanes = cosine.shape[2]
     fine = 2 * width // seq_size
-    places = value_g.shape[2]
     bf16, f32 = jnp.bfloat16, jnp.float32
     shape = (blocks // 2, 2, piece, depth)
     proj_shape = (width // fine, 1, fine, depth)
+    hidden = 2 * keep.shape[1] // seq_size
+    feed_shape = (3, seq_size // 2, hidden, depth)
     anywhere = pl.BlockSpec(memory_space=pl.ANY)
     vmem = pl.BlockSpec(memory_space=pltpu.VMEM)
     dma = pltpu.SemaphoreType.DMA
@@ -1324,8 +1445,15 @@
     steps = seq_size.bit_length() - 1
     owned = jax.ShapeDtypeStruct((rows_local, tp_size, piece, depth), bf16)
 
+    def reduce_shapes(part):
+        return [
+            pltpu.VMEM((tp_size,) + part, bf16),
+            pltpu.VMEM((pairs,) + part, bf16),
+            pltpu.VMEM((pairs - 1,) + part, bf16),
+        ]
+
     def reduce_sems(chunks):
-        return [dma((pairs,))] + [dma((pairs * chunks,))] * 4
+        return [dma((pairs * chunks,))] * 4
 
     return pl.pallas_call(
         functools.partial(tail_kernel, sizes, plan),
@@ -1333,23 +1461,39 @@
             owned,
             owned,
             jax.ShapeDtypeStruct((rows_each * seq_size, places, width), bf16),
-            jax.ShapeDtypeStruct((2 * seq_size, fine, depth), bf16),
+            jax.ShapeDtypeStruct((2, seq_size, fine, depth), bf16),
+            jax.ShapeDtypeStruct((3, seq_size, hidden, depth), bf16),
             jax.ShapeDtypeStruct(small.shape, f32),
         ],
-        in_specs=[anywhere] * 8 + [vmem] * 2,
-        out_specs=[anywhere] * 4 + [vmem],
-        scratch_shapes=[pltpu.VMEM((pairs,) + shape, bf16)] * 3
-        + [pltpu.VMEM((pairs,) + proj_shape, bf16)] * 3
-        + [pltpu.VMEM((pairs,) + shape, bf16)] * 3
+        in_specs=[anywhere] * 17 + [vmem] * 2,
+        out_specs=[anywhere] * 5 + [vmem],
+        scratch_shapes=[
+            pltpu.VMEM((blocks, places, depth), bf16),
+            pltpu.VMEM((blocks, places, width), bf16),
+            pltpu.VMEM((blocks, places, width), bf16),
+            pltpu.VMEM((blocks, places, width), bf16),
+            pltpu.VMEM((blocks, places, lanes), f32),
+            pltpu.VMEM((blocks, places, lanes), f32),
+            pltpu.VMEM((3 * width, depth), bf16),
+            pltpu.VMEM(attended.shape, bf16),
+            pltpu.VMEM((3 * width, depth), f32),
+        ]
+        + reduce_shapes(shape)
+        + reduce_shapes(proj_shape)
+        + reduce_shapes(shape)
         + [
             pltpu.VMEM(shape, bf16),
             pltpu.VMEM(shape, f32),
             pltpu.VMEM(shape, f32),
             pltpu.VMEM(shape, bf16),
             pltpu.VMEM(shape, bf16),
-            pltpu.VMEM((2 * seq_size, fine, depth), bf16),
             pltpu.VMEM((2, seq_size, fine, depth), bf16),
-            pltpu.VMEM((2 * seq_size, fine, depth), bf16),
+            pltpu.VMEM((2, seq_size, fine, depth), bf16),
+            pltpu.VMEM((2, 1, fine, depth), bf16),
+            pltpu.VMEM(feed_shape, bf16),
+            pltpu.VMEM(feed_shape, bf16),
+            pltpu.VMEM(feed_shape, bf16),
+            pltpu.VMEM((3, 1, hidden, depth), bf16),
             pltpu.VMEM(small.shape, f32),
             pltpu.VMEM((tp_size,) + small.shape, f32),
             pltpu.VMEM(small.shape, f32),
@@ -1361,9 +1505,14 @@
         + [dma((seq_size,))] * 3
         + ([dma((blocks,))] * 2 + [dma((rows_local * tp_size,))]) * 2
         + [
-            dma((4,)),
-            dma((4 * steps,)),
-            dma((4 * steps,)),
+            dma((13,)),
+            dma((blocks,)),
+            dma((6,)),
+            dma((5,)),
+            dma((2, 2 * steps)),
+            dma((2, 2 * steps)),
+            dma((3, 2 * steps)),
+            dma((3, 2 * steps)),
             dma((tp_size + seq_size,)),
             dma((tp_size,)),
             dma((seq_size,)),
@@ -1373,22 +1522,26 @@
         ),
         name="tail",
     )(
-        normed_g.reshape((tp_size,) + shape),
-        proj_grad.reshape((tp_size,) + proj_shape),
         out_part.reshape((tp_size,) + shape),
-        grads.reshape(-1, fine, depth),
+        keep.reshape(feed_shape),
+        got.reshape(feed_shape),
+        x_rows.reshape(blocks, places, depth),
+        query_g.reshape(blocks, places, width),
+        key_g.reshape(blocks, places, width),
+        value_g.reshape(blocks, places, width),
+        cosine,
+        sine,
+        query_weight,
+        key_weight,
+        value_weight,
+        attended,
         source.reshape(shape),
         middle.reshape(shape),
         middle_g.reshape(shape),
-        value_g,
+        value_g.reshape(rows_each, seq_size, places, width),
         gain,
         small,
     )
-
-
-def half_swap(weight):
-    parts = weight.reshape(-1, 2, HD // 2, weight.shape[1])
-    return jnp.stack([-parts[:, 1], parts[:, 0]], axis=1).reshape(weight.shape)
 
 
 def shards(
@@ -1423,30 +1576,31 @@
     starts = jnp.arange(ROW, dtype=jnp.int32)[None, :] - offsets
     low = (starts[:, ::BLOCK] // BLOCK).reshape(-1)
     starts = starts[:, None, :]
-    lane = jnp.arange(min(width, 128), dtype=jnp.int32)
-    frequency = rope_base ** (-(lane % (HD // 2)).astype(jnp.float32) * 2.0 / HD)
-    angles = offsets.astype(jnp.float32).reshape(-1, 1) * frequency
-    cosine, sine = jnp.cos(angles), jnp.sin(angles)
+    half_dim = HD // 2
+    frequency = rope_base ** (-jnp.arange(half_dim, dtype=jnp.float32) * 2.0 / HD)
     attn_scale = attn_gain.astype(jnp.float32)[None, :]
     feed_scale = feed_gain.astype(jnp.float32)[None, :]
-    weights = jnp.concatenate([query_weight, key_weight, value_weight], axis=0)
-    swapped = jnp.concatenate([half_swap(query_weight), half_swap(key_weight)], axis=0)
-    turn = half_swap(jnp.eye(width, dtype=jnp.bfloat16))
-
-    x_rows, cot_all, first_rows = spread(
+    (
+        x_rows, cot_all, _, output_full, queries, keys, values, cosine, sine, squares,
+    ) = spread(
         layer_input.reshape(rows_local, tp_size, piece, depth),
         out_cotangent.reshape(rows_local, tp_size, piece, depth),
         first_values,
+        output_weight,
+        query_weight,
+        key_weight,
+        value_weight,
+        offsets.astype(jnp.float32).reshape(rows_each * seq_size, 1, local_len),
+        frequency[:, None],
+        attn_scale,
         sizes,
     )
+    output_full = output_full.reshape(tp_size * width, depth)
     source_low = lax.dynamic_index_in_dim(x_rows, me, 2, keepdims=False).reshape(tokens, depth)
     source = source_low.astype(jnp.float32)
     cotangent = lax.dynamic_index_in_dim(cot_all, me, 0, keepdims=False).reshape(tokens, depth)
     cotangent = cotangent.astype(jnp.float32)
     x_rows = x_rows.reshape(rows_each * ROW, depth)
-    queries, keys, values, squares = project(
-        x_rows, first_rows, cosine, sine, attn_scale, weights, swapped
-    )
     queries, keys, values = (
         part.reshape(rows_each, ROW, width) for part in (queries, keys, values)
     )
@@ -1455,15 +1609,13 @@
     by_head = (tp_size, rows_each, seq_size, piece, width)
     (pieces,) = exchange([result.reshape(by_piece)], [by_head], [heads_to_tokens(tp_size)], 1)
     attended = jnp.transpose(pieces.reshape(tp_size, tokens, width), (1, 0, 2)).reshape(tokens, -1)
-    output_full = lax.all_gather(output_weight, "tp", axis=0, tiled=True)
-    attended, output_full = lax.optimization_barrier((attended, output_full))
     middle = source + jnp.dot(attended, output_full, preferred_element_type=jnp.float32)
     unit_feed, inv_feed = norm_rows(middle)
     feed_in = (unit_feed * feed_scale).astype(jnp.bfloat16)
-    feed_in_g, out_part, gate_grad, up_grad, down_grad = feed_forward(
-        feed_in, cot_all.reshape(tp_size, tokens, depth), gate_weight, up_weight, down_weight
+    feed_in_g, out_part, keep, give = feed_forward(
+        feed_in, cot_all.reshape(tp_size, tokens, depth), gate_weight.T, up_weight.T, down_weight
     )
-    feed_sums = lax.psum((gate_grad, up_grad, down_grad), "seq")
+    got = lax.ppermute(give, "seq", [(n, n + 1 - 2 * (n % 2)) for n in range(seq_size)])
     middle_extra, feed_gain_part = norm_back(feed_in_g, unit_feed, inv_feed, feed_scale)
     middle_g = cotangent + middle_extra
     branch_g = middle_g.astype(jnp.bfloat16)
@@ -1479,38 +1631,32 @@
     query_g, key_g, value_g = attend_back(
         low, queries, keys, values, result, attended_g.reshape(result.shape), logsum, starts
     )
-    normed_g, stacked_grad = project_back(
+    squares = jnp.pad(jnp.sum(squares, axis=1)[:2], (0, depth - 2))
+    small = jnp.stack([jnp.zeros_like(squares), feed_gain_part, squares])
+    layer_output, input_grad, value_own_g, grad_sums, feed_sums, small = tail(
+        out_part,
+        keep,
+        got,
         x_rows,
-        query_g.reshape(-1, width),
-        key_g.reshape(-1, width),
-        value_g.reshape(-1, width),
+        query_g,
+        key_g,
+        value_g,
         cosine,
         sine,
-        attn_scale,
-        weights,
-        turn,
-        sizes,
-    )
-    output_proj_grad = jnp.einsum(
-        "te,td->ed", attended, branch_g, preferred_element_type=jnp.float32
-    ).astype(jnp.bfloat16)
-    squares = jnp.pad(jnp.sum(squares, axis=1)[:2], (0, depth - 2))
-    small = jnp.stack([jnp.zeros_like(squares), feed_gain_part, squares])
-    layer_output, input_grad, value_own_g, grad_sums, small = tail(
-        normed_g,
-        output_proj_grad,
-        out_part,
-        stacked_grad,
+        query_weight,
+        key_weight,
+        value_weight,
+        pieces.reshape(tp_size, tokens, width),
         source_low,
         middle,
         middle_g,
-        value_g.reshape(rows_each, seq_size, local_len, width),
         attn_scale,
         jnp.pad(small, ((0, 5), (0, 0))),
         sizes,
     )
     first_grad = jnp.swapaxes(0.5 * value_own_g.astype(jnp.float32), 1, 2)
     grad_sums = grad_sums.reshape(4 * width, depth).astype(jnp.float32)
+    feed_sums = feed_sums.reshape(3, -1, depth).astype(jnp.float32)
     return (
         layer_output.reshape(layer_input.shape),
         input_grad.reshape(layer_input.shape),
@@ -1521,9 +1667,9 @@
         grad_sums[2 * width : 3 * width],
         grad_sums[3 * width :],
         small[1],
-        feed_sums[0].astype(jnp.float32),
-        feed_sums[1].astype(jnp.float32),
-        feed_sums[2].astype(jnp.float32),
+        feed_sums[0].T,
+        feed_sums[1].T,
+        feed_sums[2],
         jnp.sqrt(small[2, :2]),
     )
 

time: 561 us -> 505 us (0.900)
  Pallas kernels: 484 us -> 463 us
  between operations: 14.5 us -> 0.93 us
  local copies, waits for them, and re-layouts: 30 us -> 20.4 us
  matrix products: 9.1 us -> 2.67 us
  other arithmetic: 20.3 us -> 14.2 us
    pallas_call x2 -> x0, Pallas kernels: 26.8 us -> none  [the longest x1 15 us: project_back(): pl.pallas_call(project_back_kernel, grid=(rows_each * seq_size,), in_spec...]
    pallas_call x1, Pallas kernels: 203 us -> 224 us  [tail(): pl.pallas_call(functools.partial(tail_kernel, sizes, plan), out_shape=[ow...]
    pallas_call x1, Pallas kernels: 35 us -> 18.1 us  [attend(): pl.pallas_call(attend_kernel, grid_spec=pltpu.PrefetchScalarGridSpec(num_...]
    unnamed x57 -> x37, local copies, waits for them, and re-layouts: 18.8 us -> 7.4 us
    pallas_call x1, Pallas kernels: 36.7 us -> 25.9 us  [attend_back(): pl.pallas_call(attend_back_kernel, grid_spec=pltpu.PrefetchScalarGridSpec...]
    pallas_call x1, Pallas kernels: 91.6 us -> 102 us  [spread(): pl.pallas_call(functools.partial(spread_kernel, plans, sizes), out_shape=...]
  transfers between devices with their start and end apart: 2 -> 1, of which waited for: 0 -> 0; matrix products, arithmetic and copies ran while one was open for 7% -> 2% of each run, Pallas kernels for 75% -> 8%
where the time goes in v4:
time: 505 us; the launch traced here: 502 us
  Pallas kernels  463 us (92%)
  local copies, waits for them, and re-layouts  20.4 us (4%)
  other arithmetic  14.2 us (3%)
    pallas_call x1, Pallas kernels, tail(): pl.pallas_call(functools.partial(tail_kernel, sizes, plan), out_shape=[ow...  224 us
    pallas_call x1, Pallas kernels, spread(): pl.pallas_call(functools.partial(spread_kernel, plans, sizes), out_shape=...  102 us
    pallas_call x1, Pallas kernels, feed_forward(): pl.pallas_call(functools.partial(feed_kernel, chunk), out_shape=[jax.Shap...  63.4 us
    pallas_call x2, Pallas kernels, exchange(): pl.pallas_call(kernel, out_shape=[jax.ShapeDtypeStruct(shape, array.dtype...  29.1 us
    pallas_call x1, Pallas kernels, attend_back(): pl.pallas_call(attend_back_kernel, grid_spec=pltpu.PrefetchScalarGridSpec...  25.9 us
    pallas_call x1, Pallas kernels, attend(): pl.pallas_call(attend_kernel, grid_spec=pltpu.PrefetchScalarGridSpec(num_...  18.1 us
  transfers between devices with their start and end apart: 1, of which 0 were waited for; matrix products, arithmetic and copies ran while one was open for 2% of the time, Pallas kernels for 8%

profile of v4, /device:TPU:0, one launch (start us, length us, event | category | flops | bytes accessed | tf_op | source)
XLA Modules:
  0.0 502.1 jit_solution(16944321498953977005)
XLA Ops:
  0.7 0.6 multiply_power_fusion.frequency_ref
  1.3 1.3 convert_element_type.48
  2.6 0.9 reduce_window_sum.11
  3.4 1.3 broadcast_in_dim.31
  6.9 102.0 %spread.1 = (bf16[1,8,4,64,1024]{4,3,2,1,0:T(8,128)(2,1)}, bf16[4,1,8,64,1024]{4,3,2,1,0:T(8,128)(2,1)}, bf16[1,8,256,256]{3,2,1,0:T(8,128)(2,1)}, bf16[4,256,10...) custom-call(bf16[2,4,64,1024]{3,2,1,0:T(8,128)(2,1)} %bitcast.102, ...), custom_call_target="tpu_custom_call" | custom-call | tf_op jit(solution)/shard_map/spread/pallas_call | solution.py:892
  108.9 18.1 %attend.1 = (bf16[1,2048,256]{2,1,0:T(8,128)(2,1)}, f32[1,4,2048]{2,1,0:T(4,128)}) custom-call(s32[8]{0:T(128)} %fusion.1.low_ref, bf16[1,2048,256]{2,1,0:T(8,128)(2,1)} %bitcast.82, bf16[1,2048,256]{2,1,0:T(8,128)(2,1)} %bitcast.84, bf16[1,2048,256]{2,1,0:T(8,128)(2,1)} %bitcast.86, s32[1,1,2048]{2,1,0:T(1,128)} %bitcast.104), custom_call_target="tpu_custom_call" | custom-call | tf_op jit(solution)/shard_map/attend/pallas_call | solution.py:128
  127.1 15.5 %exchange_1.1 = bf16[4,1,8,64,256]{4,3,2,1,0:T(8,128)(2,1)} custom-call(bf16[1,8,4,64,256]{4,3,2,1,0:T(8,128)(2,1)} %bitcast.88), custom_call_target="tpu_custom_call" | custom-call | tf_op jit(solution)/shard_map/exchange_1/pallas_call | solution.py:532
  142.6 1.4 constant_dynamic-slice_fusion.1
  144.1 1.4 multiply_reduce_fusion.2
  145.5 1.3 copy-done
  146.8 1.2 multiply_convert_fusion.feed_ref
  148.0 63.4 %feed_forward.1 = (f32[512,1024]{1,0:T(8,128)}, bf16[4,512,1024]{2,1,0:T(8,128)(2,1)}, bf16[3,352,1024]{2,1,0:T(8,128)(2,1)}, bf16[3,352,1024]{2,1,0:T(8,128)(2,1)}) custom-call(bf16[512,1024]{1,0:T(8,128)(2,1)} %multiply_convert_fusion.feed_ref, bf16[4,512,1024]{2,1,0:T(8,128)(2,1)} %bitcast.73, bf16[704,1024]{1,0:T(8,128)(2,1)} %bitcast.95, ...), custom_call_target="tpu_custom_call" | custom-call | tf_op jit(solution)/shard_map/feed_forward/pallas_call | solution.py:407
  211.5 0.9 collective-permute-start
  212.4 0.8 reduce_sum.39
  213.2 1.3 constant_dynamic-slice_fusion
  214.6 2.3 multiply_reduce_fusion
  217.6 1.0 copy-done.14
  218.5 1.3 convolution_convert_fusion
  219.9 1.0 copy.32
  220.9 13.6 %exchange_2.1 = bf16[1,8,4,64,256]{4,3,2,1,0:T(8,128)(2,1)} custom-call(bf16[4,1,8,64,256]{4,3,2,1,0:T(8,128)(2,1)} %bitcast.81), custom_call_target="tpu_custom_call" | custom-call | tf_op jit(solution)/shard_map/exchange_2/pallas_call | solution.py:532
  235.2 25.9 %attend_back.1 = (bf16[1,2048,256]{2,1,0:T(8,128)(2,1)}, bf16[1,2048,256]{2,1,0:T(8,128)(2,1)}, bf16[1,2048,256]{2,1,0:T(8,128)(2,1)}) custom-call(s32[8]{0:T(128)} %fusion.1.low_ref, bf16[1,2048,256]{2,1,0:T(8,128)(2,1)} %bitcast.83, bf16[1,2048,256]{2,1,0:T(8,128)(2,1)} %bitcast.85, bf16[1,2048,256]{2,1,0:T(8,128)(2,1)} %bitcast.87, ...), custom_call_target="tpu_custom_call" | custom-call | tf_op jit(solution)/shard_map/attend_back/pallas_call | solution.py:218
  261.1 224.4 %tail.1 = (bf16[2,4,64,1024]{3,2,1,0:T(8,128)(2,1)}, bf16[2,4,64,1024]{3,2,1,0:T(8,128)(2,1)}, bf16[8,256,256]{2,1,0:T(8,128)(2,1)}, bf16[2,8,64,1024]{3,2,1,0:T...) custom-call(bf16[4,4,2,64,1024]{4,3,2,1,0:T(8,128)(2,1)} %bitcast.90, ...), custom_call_target="tpu_custom_call" | custom-call | tf_op jit(solution)/shard_map/tail/pallas_call | solution.py:1458
  485.5 1.2 sqrt_bitcast_fusion
  486.7 1.4 fusion.5
  488.2 1.4 multiply_bitcast_fusion
  489.6 1.8 copy.29
  491.4 2.2 bitcast_convert_fusion
  493.6 2.1 fusion.4
  495.7 3.9 fusion.3
  499.6 1.0 copy.35
  500.5 0.6 copy-done.6
  501.2 1.0 copy.36
  (44 shorter events, 3.7 us)
Async XLA Ops:
  5.7 0.6 copy-start.8
  127.1 16.9 %copy-start.13 = (bf16[4,256,1024]{2,1,0:T(8,128)(2,1)S(1)}, bf16[4,256,1024]{2,1,0:T(8,128)(2,1)}, u32[]{:S(2)}) copy-start(bf16[4,256,1024]{2,1,0:T(8,128)(2,1)} %get-tuple-element.42) | copy-start | bytes 6291460
  142.6 1.5 copy-start.5
  144.0 1.5 copy-start.4
  144.1 2.7 copy-start.9
  145.5 1.3 copy-start
  145.5 2.5 copy-start.11
  211.5 3.1 copy-start.1
  211.5 3.1 copy-start.10
  211.5 3.1 copy-start.12
  211.5 49.6 %collective-permute-start = (bf16[3,352,1024]{2,1,0:T(8,128)(2,1)}, bf16[3,352,1024]{2,1,0:T(8,128)(2,1)}, u32[]{:S(2)}, u32[]{:S(2)}) collective-permute-start(bf16[3,352,1024]{2,1,0:T(8,128)(2,1)} %get-tuple-element.46), channel_id=1, source_target_pairs={{0,4},{4,0},{8,12},{12,8},{16,20},{20,16},{24,28},{28,24},{1,5},{5... | collective-permute-start | bytes 6488072 | tf_op jit(solution)/shard_map/ppermute | solution.py:1618
  214.6 2.3 copy-start.2
  216.9 1.6 copy-start.14
  217.5 2.3 copy-start.3
  491.4 4.3 slice-start
  493.6 2.1 slice-start.1
  495.7 3.9 copy-start.7
  499.6 1.6 copy-start.6

commit v5 on v4

--- a/solution.py
+++ b/solution.py
@@ -319,10 +319,16 @@
     feed_all[me] = feed_ref[...]
     acc[...] = jnp.zeros_like(acc)
 
+    count = chunks * pairs
+    early = chunks - 1
+
     def step(n, carry):
         which = lax.rem(n, 2)
-        c = lax.rem(n // 2, chunks)
-        offset = n // (2 * chunks)
+        at = n // 2
+        if early:
+            at = at + (at + count - early) // count - (at + 1) // count * (count - early)
+        c = lax.rem(at, chunks)
+        offset = at // chunks
         owner = lax.rem(pair + offset, pairs) * 2 + lax.rem(core + which, 2)
 
         @pl.when((which == 0) & (offset > 0))
@@ -1097,12 +1103,12 @@
 def tail_kernel(
     sizes, dv_plan, out_hbm, keep_hbm, got_hbm, x_hbm, q_hbm, k_hbm, v_hbm, cos_hbm, sin_hbm,
     qw_hbm, kw_hbm, vw_hbm, attended_hbm, source_hbm, middle_hbm, middle_g_hbm, dv_hbm, gain_ref, small_ref,
-    out_ref, input_g_ref, dv_ref, sums_ref, feed_ref, total_ref,
+    out_ref, input_g_ref, first_g_ref, sums_ref, feed_ref, gain_g_ref, feed_gain_g_ref, norms_ref,
     x_rows, q_rows, k_rows, v_rows, cos_rows, sin_rows, weights, attended, grad_acc,
     normed_full, normed_core, normed_pair, proj_full, proj_core, proj_pair,
     out_full, out_core, out_pair, source, middle, middle_g, input_g, result,
     blocks, held, mine, feed_blocks, feed_got, feed_held, feed_mine,
-    small, tp_held, tp_sum, seq_held,
+    small, tp_held, tp_sum, seq_held, dv_rows, dv_cols,
     *sems,
 ):
     seq_size, tp_size, rows_each, rows_local, _ = sizes
@@ -1113,12 +1119,12 @@
     normed_sems, proj_sems, out_sems = sems[:4], sems[4:8], sems[8:12]
     dv_sems, back_sems, lo_sems = sems[12:15], sems[15:18], sems[18:21]
     load_sem, x_sem, feed_sem, store_sem, grad_send, grad_recv = sems[21:27]
-    feed_send, feed_recv, small_send, tp_sem, seq_sem = sems[27:]
+    feed_send, feed_recv, small_send, tp_sem, seq_sem, first_sem = sems[27:]
     place = (s, t, pairs)
     normed = Reduce(place, normed_full, normed_core, normed_pair, 2, normed_sems)
     proj = Reduce(place, proj_full, proj_core, proj_pair, 1, proj_sems)
     out = Reduce(place, out_full, out_core, out_pair, 2, out_sems)
-    dv_move = Exchange(dv_plan, me, dv_hbm, dv_ref, *dv_sems)
+    dv_move = Exchange(dv_plan, me, dv_hbm, dv_rows, *dv_sems)
     half = source.shape[0]
     places, depth = x_rows.shape[1:]
     width = q_rows.shape[2]
@@ -1128,7 +1134,7 @@
     for slot in range(rows_local):
         row = t * rows_local + slot
         for i in range(tp_size):
-            origins.append(((place_of(row // rows_each, seq_size), i), (slot, i), slot * tp_size + i))
+            origins.append(((place_of(row // rows_each, seq_size), i), slot, i))
 
     tp_peers = [lax.rem(t + i, tp_size) for i in range(1, tp_size)]
     seq_peers = [lax.rem(s + i, seq_size) for i in range(1, seq_size)]
@@ -1290,6 +1296,10 @@
     next(feeds[2])
     next(feeds[0])
 
+    def own_part(target, slot, i):
+        piece = source.shape[2]
+        return target.at[slot, pl.ds(pl.multiple_of(i * piece, piece), piece)]
+
     def send_back(source_ref, target, trio, b, c, wait):
         local_sem, send_sem, recv_sem = trio
         flat = 2 * b + c
@@ -1298,7 +1308,7 @@
         slot = lax.rem(row, rows_local)
         place = (to, row // rows_local)
         here = same(place, me)
-        view = target.at[slot, t]
+        view = own_part(target, slot, t)
 
         @pl.when(here)
         def _():
@@ -1389,6 +1399,16 @@
     for n in range(1, seq_size):
         seq_copy(n).start()
     seq_held[0] = total
+    dv_move.wait_sends()
+    dv_move.wait_receives()
+
+    def first_back(n, carry):
+        dv_cols[n] = (0.5 * dv_rows[n].astype(jnp.float32)).T
+        return carry
+
+    lax.fori_loop(0, dv_rows.shape[0], first_back, 0)
+    first_store = pltpu.make_async_copy(dv_cols, first_g_ref, first_sem)
+    first_store.start()
     for _ in range(2 * count):
         all_steps([feeds[1], sums[0], feeds[2], sums[1], feeds[0]])
     for generator in sums + feeds:
@@ -1399,7 +1419,9 @@
     total = seq_held[lax.rem(seq_size - s, seq_size)]
     for n in range(1, seq_size):
         total = total + seq_held[lax.rem(n + seq_size - s, seq_size)]
-    total_ref[...] = total
+    gain_g_ref[...] = total[0:1]
+    feed_gain_g_ref[...] = total[1:2]
+    norms_ref[...] = jnp.sqrt(total[2:3, :2])
 
     for reduce in (normed, proj, out):
         reduce.finish()
@@ -1410,13 +1432,13 @@
             return carry
 
         lax.fori_loop(0, half, done, 0)
-    dv_move.wait_sends()
-    dv_move.wait_receives()
-    for origin, target, at in origins:
+    first_store.wait()
+    for origin, slot, i in origins:
         @pl.when(jnp.logical_not(same(origin, me)))
         def _():
             for ref, trio in ((input_g_ref, back_sems), (out_ref, lo_sems)):
-                view = ref.at[target]
+                view = own_part(ref, slot, i)
+                at = slot * tp_size + i
                 remote(view, view, trio[1].at[0], trio[2].at[at], origin).wait_recv()
 
 
@@ -1443,7 +1465,7 @@
     dma = pltpu.SemaphoreType.DMA
     plan = rows_to_places(seq_size, rows_each)
     steps = seq_size.bit_length() - 1
-    owned = jax.ShapeDtypeStruct((rows_local, tp_size, piece, depth), bf16)
+    owned = jax.ShapeDtypeStruct((rows_local, tp_size * piece, depth), bf16)
 
     def reduce_shapes(part):
         return [
@@ -1460,13 +1482,15 @@
         out_shape=[
             owned,
             owned,
-            jax.ShapeDtypeStruct((rows_each * seq_size, places, width), bf16),
+            jax.ShapeDtypeStruct((blocks, width, places), f32),
             jax.ShapeDtypeStruct((2, seq_size, fine, depth), bf16),
             jax.ShapeDtypeStruct((3, seq_size, hidden, depth), bf16),
-            jax.ShapeDtypeStruct(small.shape, f32),
+            jax.ShapeDtypeStruct((1, depth), f32),
+            jax.ShapeDtypeStruct((1, depth), f32),
+            jax.ShapeDtypeStruct((1, 2), f32),
         ],
         in_specs=[anywhere] * 17 + [vmem] * 2,
-        out_specs=[anywhere] * 5 + [vmem],
+        out_specs=[anywhere] * 5 + [vmem] * 3,
         scratch_shapes=[
             pltpu.VMEM((blocks, places, depth), bf16),
             pltpu.VMEM((blocks, places, width), bf16),
@@ -1498,6 +1522,8 @@
             pltpu.VMEM((tp_size,) + small.shape, f32),
             pltpu.VMEM(small.shape, f32),
             pltpu.VMEM((seq_size,) + small.shape, f32),
+            pltpu.VMEM((blocks, places, width), bf16),
+            pltpu.VMEM((blocks, width, places), f32),
         ]
         + reduce_sems(2)
         + reduce_sems(1)
@@ -1516,6 +1542,7 @@
             dma((tp_size + seq_size,)),
             dma((tp_size,)),
             dma((seq_size,)),
+            dma,
         ],
         compiler_params=pltpu.CompilerParams(
             collective_id=6, has_side_effects=True, vmem_limit_bytes=67043328
@@ -1633,7 +1660,10 @@
     )
     squares = jnp.pad(jnp.sum(squares, axis=1)[:2], (0, depth - 2))
     small = jnp.stack([jnp.zeros_like(squares), feed_gain_part, squares])
-    layer_output, input_grad, value_own_g, grad_sums, feed_sums, small = tail(
+    (
+        layer_output, input_grad, first_grad, grad_sums, feed_sums,
+        gain_grad, feed_gain_grad, norms,
+    ) = tail(
         out_part,
         keep,
         got,
@@ -1654,23 +1684,20 @@
         jnp.pad(small, ((0, 5), (0, 0))),
         sizes,
     )
-    first_grad = jnp.swapaxes(0.5 * value_own_g.astype(jnp.float32), 1, 2)
-    grad_sums = grad_sums.reshape(4 * width, depth).astype(jnp.float32)
+    grad_sums = grad_sums.reshape(4, width, depth)
+    projections = [grad_sums[n].astype(jnp.float32) for n in range(4)]
     feed_sums = feed_sums.reshape(3, -1, depth).astype(jnp.float32)
     return (
-        layer_output.reshape(layer_input.shape),
-        input_grad.reshape(layer_input.shape),
+        layer_output,
+        input_grad,
         first_grad,
-        small[0],
-        grad_sums[:width],
-        grad_sums[width : 2 * width],
-        grad_sums[2 * width : 3 * width],
-        grad_sums[3 * width :],
-        small[1],
+        gain_grad.reshape(depth),
+        *projections,
+        feed_gain_grad.reshape(depth),
         feed_sums[0].T,
         feed_sums[1].T,
         feed_sums[2],
-        jnp.sqrt(small[2, :2]),
+        norms.reshape(2),
     )
 
 

time: 505 us -> 497 us (0.984)
  Pallas kernels: 463 us -> 456 us
    pallas_call x1, Pallas kernels: 63.4 us -> 57.5 us  [feed_forward(): pl.pallas_call(functools.partial(feed_kernel, chunk), out_shape=[jax.Shap...]
  transfers between devices with their start and end apart: 1 -> 1, of which waited for: 0 -> 1; matrix products, arithmetic and copies ran while one was open for 2% -> 2% of each run, Pallas kernels for 8% -> 8%
where the time goes in v5:
time: 497 us; the launch traced here: 492 us
  Pallas kernels  456 us (92%)
  local copies, waits for them, and re-layouts  16.9 us (3%)
  other arithmetic  14.7 us (3%)
    pallas_call x1, Pallas kernels, tail(): pl.pallas_call(functools.partial(tail_kernel, sizes, plan), out_shape=[ow...  224 us
    pallas_call x1, Pallas kernels, spread(): pl.pallas_call(functools.partial(spread_kernel, plans, sizes), out_shape=...  102 us
    pallas_call x1, Pallas kernels, feed_forward(): pl.pallas_call(functools.partial(feed_kernel, chunk), out_shape=[jax.Shap...  57.5 us
    pallas_call x2, Pallas kernels, exchange(): pl.pallas_call(kernel, out_shape=[jax.ShapeDtypeStruct(shape, array.dtype...  28.4 us
    pallas_call x1, Pallas kernels, attend_back(): pl.pallas_call(attend_back_kernel, grid_spec=pltpu.PrefetchScalarGridSpec...  25.9 us
    pallas_call x1, Pallas kernels, attend(): pl.pallas_call(attend_kernel, grid_spec=pltpu.PrefetchScalarGridSpec(num_...  18.1 us
  transfers between devices with their start and end apart: 1, of which 1 were waited for; matrix products, arithmetic and copies ran while one was open for 2% of the time, Pallas kernels for 8%

profile of v5, /device:TPU:0, one launch (start us, length us, event | category | flops | bytes accessed | tf_op | source)
XLA Modules:
  0.0 492.4 jit_solution(10899854268659721471)
XLA Ops:
  0.7 0.6 multiply_power_fusion.frequency_ref
  1.3 1.3 convert_element_type.63
  2.6 0.9 reduce_window_sum.11
  3.4 1.3 broadcast_in_dim.31
  5.1 0.6 iota_subtract_fusion
  5.7 0.6 copy-done.10
  6.9 102.0 %spread.1 = (bf16[1,8,4,64,1024]{4,3,2,1,0:T(8,128)(2,1)}, bf16[4,1,8,64,1024]{4,3,2,1,0:T(8,128)(2,1)}, bf16[1,8,256,256]{3,2,1,0:T(8,128)(2,1)}, bf16[4,256,10...) custom-call(bf16[2,4,64,1024]{3,2,1,0:T(8,128)(2,1)} %bitcast.112, ...), custom_call_target="tpu_custom_call" | custom-call | tf_op jit(solution)/shard_map/spread/pallas_call | solution.py:898
  108.9 18.1 %attend.1 = (bf16[1,2048,256]{2,1,0:T(8,128)(2,1)}, f32[1,4,2048]{2,1,0:T(4,128)}) custom-call(s32[8]{0:T(128)} %fusion.5.low_ref, bf16[1,2048,256]{2,1,0:T(8,128)(2,1)} %bitcast.93, bf16[1,2048,256]{2,1,0:T(8,128)(2,1)} %bitcast.95, bf16[1,2048,256]{2,1,0:T(8,128)(2,1)} %bitcast.97, s32[1,1,2048]{2,1,0:T(1,128)} %bitcast.114), custom_call_target="tpu_custom_call" | custom-call | tf_op jit(solution)/shard_map/attend/pallas_call | solution.py:128
  127.1 15.5 %exchange_1.1 = bf16[4,1,8,64,256]{4,3,2,1,0:T(8,128)(2,1)} custom-call(bf16[1,8,4,64,256]{4,3,2,1,0:T(8,128)(2,1)} %bitcast.99), custom_call_target="tpu_custom_call" | custom-call | tf_op jit(solution)/shard_map/exchange_1/pallas_call | solution.py:538
  142.6 1.4 constant_dynamic-slice_fusion.1
  144.1 1.4 multiply_reduce_fusion.2
  145.5 1.3 copy-done
  146.8 1.2 multiply_convert_fusion.feed_ref
  148.0 57.5 %feed_forward.1 = (f32[512,1024]{1,0:T(8,128)}, bf16[4,512,1024]{2,1,0:T(8,128)(2,1)}, bf16[3,352,1024]{2,1,0:T(8,128)(2,1)}, bf16[3,352,1024]{2,1,0:T(8,128)(2,1)}) custom-call(bf16[512,1024]{1,0:T(8,128)(2,1)} %multiply_convert_fusion.feed_ref, bf16[4,512,1024]{2,1,0:T(8,128)(2,1)} %bitcast.84, bf16[704,1024]{1,0:T(8,128)(2,1)} %bitcast.107, ...), custom_call_target="tpu_custom_call" | custom-call | tf_op jit(solution)/shard_map/feed_forward/pallas_call | solution.py:413
  206.0 1.0 reduce_sum.39
  207.0 1.3 constant_dynamic-slice_fusion
  208.3 2.4 multiply_reduce_fusion
  210.7 0.6 convert_add_fusion
  211.4 0.9 copy-done.18
  212.3 1.3 convolution_convert_fusion
  213.7 1.0 copy.30
  214.7 13.0 %exchange_2.1 = bf16[1,8,4,64,256]{4,3,2,1,0:T(8,128)(2,1)} custom-call(bf16[4,1,8,64,256]{4,3,2,1,0:T(8,128)(2,1)} %bitcast.92), custom_call_target="tpu_custom_call" | custom-call | tf_op jit(solution)/shard_map/exchange_2/pallas_call | solution.py:538
  227.8 0.6 pad.9.small_ref
  228.4 25.9 %attend_back.1 = (bf16[1,2048,256]{2,1,0:T(8,128)(2,1)}, bf16[1,2048,256]{2,1,0:T(8,128)(2,1)}, bf16[1,2048,256]{2,1,0:T(8,128)(2,1)}) custom-call(s32[8]{0:T(128)} %fusion.5.low_ref, bf16[1,2048,256]{2,1,0:T(8,128)(2,1)} %bitcast.94, bf16[1,2048,256]{2,1,0:T(8,128)(2,1)} %bitcast.96, bf16[1,2048,256]{2,1,0:T(8,128)(2,1)} %bitcast.98, ...), custom_call_target="tpu_custom_call" | custom-call | tf_op jit(solution)/shard_map/attend_back/pallas_call | solution.py:218
  254.2 0.6 collective-permute-done
  254.9 224.1 %tail.1 = (bf16[2,256,1024]{2,1,0:T(8,128)(2,1)}, bf16[2,256,1024]{2,1,0:T(8,128)(2,1)}, f32[8,256,256]{2,1,0:T(8,128)}, bf16[2,8,64,1024]{3,2,1,0:T(8,128)(2,1)...) custom-call(bf16[4,4,2,64,1024]{4,3,2,1,0:T(8,128)(2,1)} %bitcast.101, ...), custom_call_target="tpu_custom_call" | custom-call | tf_op jit(solution)/shard_map/tail/pallas_call | solution.py:1480
  479.0 3.9 fusion.1
  482.9 3.9 fusion.7
  486.7 1.0 copy.37
  487.7 0.6 copy-done.8
  488.3 1.0 copy.38
  489.3 1.3 copy.39
  (48 shorter events, 3.4 us)
Async XLA Ops:
  5.7 0.6 copy-start.10
  127.1 16.9 %copy-start.17 = (bf16[4,256,1024]{2,1,0:T(8,128)(2,1)S(1)}, bf16[4,256,1024]{2,1,0:T(8,128)(2,1)}, u32[]{:S(2)}) copy-start(bf16[4,256,1024]{2,1,0:T(8,128)(2,1)} %get-tuple-element.44) | copy-start | bytes 6291460
  142.6 1.5 copy-start.6
  144.0 1.5 copy-start.5
  144.1 2.7 copy-start.11
  145.5 1.3 copy-start
  145.5 2.5 copy-start.13
  205.5 2.8 copy-start.1
  205.5 2.8 copy-start.12
  205.5 2.8 copy-start.14
  205.5 49.3 %collective-permute-start = (bf16[3,352,1024]{2,1,0:T(8,128)(2,1)}, bf16[3,352,1024]{2,1,0:T(8,128)(2,1)}, u32[]{:S(2)}, u32[]{:S(2)}) collective-permute-start(bf16[3,352,1024]{2,1,0:T(8,128)(2,1)} %get-tuple-element.48), channel_id=1, source_target_pairs={{0,4},{4,0},{8,12},{12,8},{16,20},{20,16},{24,28},{28,24},{1,5},{5... | collective-permute-start | bytes 6488072 | tf_op jit(solution)/shard_map/ppermute | solution.py:1645
  208.3 2.4 copy-start.3
  210.7 1.6 copy-start.18
  211.4 2.3 copy-start.4
  479.0 3.9 copy-start.2
  482.9 3.9 copy-start.9
  486.7 1.6 copy-start.8
  486.7 2.6 copy-start.7
  489.3 1.3 copy-start.16
  489.3 1.9 copy-start.15
  489.3 2.5 copy-start.19

commit v6 on v5

--- a/solution.py
+++ b/solution.py
@@ -1167,12 +1167,13 @@
     for pair in feed_loads:
         for copy in pair:
             copy.start()
-    loads[8].start()
+    for n in (9, 10, 8):
+        loads[n].start()
     for copy in loads[:8]:
         copy.start()
     for n in range(2 * half):
         x_load(ordered(n)).start()
-    for copy in loads[9:]:
+    for copy in loads[11:]:
         copy.start()
 
     barrier = pltpu.get_barrier_semaphore()
@@ -1221,6 +1222,15 @@
 
         lax.fori_loop(0, feed_blocks.shape[1], join, 0)
         next(feeds[n])
+    fine = blocks.shape[2]
+    loads[9].wait()
+    loads[10].wait()
+    branch = middle_g[...].reshape(2 * half * middle_g.shape[2], depth).astype(jnp.bfloat16)
+    for i in range(tp_size):
+        product = columns_dot(attended[i], branch)
+        for n in range(seq_size // 2):
+            proj_full[i, n, 0] = product[n * fine : (n + 1) * fine].astype(jnp.bfloat16)
+    proj.start(0)
     loads[8].wait()
     out.start(0)
     out.start(1)
@@ -1264,9 +1274,10 @@
 
     quarter = half // 2
     project_back(0, quarter)
+    proj.pass_on(0)
+    next(feeds[0])
     out.pass_on(0)
     out.pass_on(1)
-    next(feeds[0])
     project_back(quarter, half)
     normed.start(0)
     next(feeds[1])
@@ -1276,25 +1287,23 @@
     next(feeds[0])
     project_back(half + quarter, 2 * half)
     normed.start(1)
-    fine = blocks.shape[2]
     for n in range(3 * seq_size // 2):
         blocks[n // seq_size, n % seq_size] = grad_acc[n * fine : (n + 1) * fine].astype(
             jnp.bfloat16
         )
     next(sums[0])
+    proj.arrive(0)
+
+    def put(b, carry):
+        blocks[1, seq_size // 2 + b] = proj.total(b, 0).astype(jnp.bfloat16)
+        return carry
+
+    lax.fori_loop(0, seq_size // 2, put, 0)
+    next(sums[1])
+    normed.pass_on(1)
     next(feeds[1])
-    loads[9].wait()
-    loads[10].wait()
-    branch = middle_g[...].reshape(2 * half * middle_g.shape[2], depth).astype(jnp.bfloat16)
-    for i in range(tp_size):
-        product = columns_dot(attended[i], branch)
-        for n in range(seq_size // 2):
-            proj_full[i, n, 0] = product[n * fine : (n + 1) * fine].astype(jnp.bfloat16)
-    proj.start(0)
-    normed.pass_on(1)
-    proj.pass_on(0)
+    next(feeds[0])
     next(feeds[2])
-    next(feeds[0])
 
     def own_part(target, slot, i):
         piece = source.shape[2]
@@ -1371,24 +1380,20 @@
 
     loads[12].wait()
     forward(0)
+    next(feeds[1])
+    next(feeds[0])
+    next(sums[0])
     forward(1)
-    next(feeds[1])
+    next(feeds[2])
+    next(sums[1])
     loads[11].wait()
     back(0)
-    proj.arrive(0)
-
-    def put(b, carry):
-        blocks[1, seq_size // 2 + b] = proj.total(b, 0).astype(jnp.bfloat16)
-        return carry
-
-    lax.fori_loop(0, seq_size // 2, put, 0)
-    next(sums[1])
+    next(feeds[1])
     next(sums[0])
-    next(feeds[2])
     back(1)
     for n in range(1, tp_size):
         tp_copy(n).start()
-    all_steps([feeds[0], sums[0], sums[1]])
+    all_steps([sums[1], feeds[2], sums[0]])
     for n in range(1, tp_size):
         tp_copy(n).wait()
     tp_held[0] = small[...]
@@ -1410,7 +1415,7 @@
     first_store = pltpu.make_async_copy(dv_cols, first_g_ref, first_sem)
     first_store.start()
     for _ in range(2 * count):
-        all_steps([feeds[1], sums[0], feeds[2], sums[1], feeds[0]])
+        all_steps([sums[1], sums[0], feeds[0], feeds[1], feeds[2]])
     for generator in sums + feeds:
         for _ in generator:
             pass

time: 497 us -> 489 us (0.984)
  Pallas kernels: 456 us -> 451 us
    pallas_call x1, Pallas kernels: 224 us -> 219 us  [tail(): pl.pallas_call(functools.partial(tail_kernel, sizes, plan), out_shape=[ow...]
where the time goes in v6:
time: 489 us; the launch traced here: 487 us
  Pallas kernels  451 us (92%)
  local copies, waits for them, and re-layouts  16.9 us (3%)
  other arithmetic  14.7 us (3%)
    pallas_call x1, Pallas kernels, tail(): pl.pallas_call(functools.partial(tail_kernel, sizes, plan), out_shape=[ow...  219 us
    pallas_call x1, Pallas kernels, spread(): pl.pallas_call(functools.partial(spread_kernel, plans, sizes), out_shape=...  102 us
    pallas_call x1, Pallas kernels, feed_forward(): pl.pallas_call(functools.partial(feed_kernel, chunk), out_shape=[jax.Shap...  57.5 us
    pallas_call x2, Pallas kernels, exchange(): pl.pallas_call(kernel, out_shape=[jax.ShapeDtypeStruct(shape, array.dtype...  28.4 us
    pallas_call x1, Pallas kernels, attend_back(): pl.pallas_call(attend_back_kernel, grid_spec=pltpu.PrefetchScalarGridSpec...  25.9 us
    pallas_call x1, Pallas kernels, attend(): pl.pallas_call(attend_kernel, grid_spec=pltpu.PrefetchScalarGridSpec(num_...  18.1 us
  transfers between devices with their start and end apart: 1, of which 1 were waited for; matrix products, arithmetic and copies ran while one was open for 2% of the time, Pallas kernels for 8%

profile of v6, /device:TPU:0, one launch (start us, length us, event | category | flops | bytes accessed | tf_op | source)
XLA Modules:
  0.0 487.1 jit_solution(114897747629498855)
XLA Ops:
  0.7 0.6 multiply_power_fusion.frequency_ref
  1.3 1.3 convert_element_type.63
  2.6 0.9 reduce_window_sum.11
  3.4 1.3 broadcast_in_dim.31
  5.1 0.6 iota_subtract_fusion
  5.7 0.6 copy-done.10
  6.9 102.0 %spread.1 = (bf16[1,8,4,64,1024]{4,3,2,1,0:T(8,128)(2,1)}, bf16[4,1,8,64,1024]{4,3,2,1,0:T(8,128)(2,1)}, bf16[1,8,256,256]{3,2,1,0:T(8,128)(2,1)}, bf16[4,256,10...) custom-call(bf16[2,4,64,1024]{3,2,1,0:T(8,128)(2,1)} %bitcast.112, ...), custom_call_target="tpu_custom_call" | custom-call | tf_op jit(solution)/shard_map/spread/pallas_call | solution.py:898
  108.9 18.1 %attend.1 = (bf16[1,2048,256]{2,1,0:T(8,128)(2,1)}, f32[1,4,2048]{2,1,0:T(4,128)}) custom-call(s32[8]{0:T(128)} %fusion.5.low_ref, bf16[1,2048,256]{2,1,0:T(8,128)(2,1)} %bitcast.93, bf16[1,2048,256]{2,1,0:T(8,128)(2,1)} %bitcast.95, bf16[1,2048,256]{2,1,0:T(8,128)(2,1)} %bitcast.97, s32[1,1,2048]{2,1,0:T(1,128)} %bitcast.114), custom_call_target="tpu_custom_call" | custom-call | tf_op jit(solution)/shard_map/attend/pallas_call | solution.py:128
  127.1 15.5 %exchange_1.1 = bf16[4,1,8,64,256]{4,3,2,1,0:T(8,128)(2,1)} custom-call(bf16[1,8,4,64,256]{4,3,2,1,0:T(8,128)(2,1)} %bitcast.99), custom_call_target="tpu_custom_call" | custom-call | tf_op jit(solution)/shard_map/exchange_1/pallas_call | solution.py:538
  142.6 1.4 constant_dynamic-slice_fusion.1
  144.1 1.4 multiply_reduce_fusion.2
  145.5 1.3 copy-done
  146.8 1.2 multiply_convert_fusion.feed_ref
  148.0 57.5 %feed_forward.1 = (f32[512,1024]{1,0:T(8,128)}, bf16[4,512,1024]{2,1,0:T(8,128)(2,1)}, bf16[3,352,1024]{2,1,0:T(8,128)(2,1)}, bf16[3,352,1024]{2,1,0:T(8,128)(2,1)}) custom-call(bf16[512,1024]{1,0:T(8,128)(2,1)} %multiply_convert_fusion.feed_ref, bf16[4,512,1024]{2,1,0:T(8,128)(2,1)} %bitcast.84, bf16[704,1024]{1,0:T(8,128)(2,1)} %bitcast.107, ...), custom_call_target="tpu_custom_call" | custom-call | tf_op jit(solution)/shard_map/feed_forward/pallas_call | solution.py:413
  206.0 1.0 reduce_sum.39
  207.0 1.3 constant_dynamic-slice_fusion
  208.3 2.4 multiply_reduce_fusion
  210.7 0.6 convert_add_fusion
  211.4 0.9 copy-done.18
  212.3 1.3 convolution_convert_fusion
  213.7 1.0 copy.30
  214.7 13.0 %exchange_2.1 = bf16[1,8,4,64,256]{4,3,2,1,0:T(8,128)(2,1)} custom-call(bf16[4,1,8,64,256]{4,3,2,1,0:T(8,128)(2,1)} %bitcast.92), custom_call_target="tpu_custom_call" | custom-call | tf_op jit(solution)/shard_map/exchange_2/pallas_call | solution.py:538
  227.8 0.6 pad.9.small_ref
  228.4 25.9 %attend_back.1 = (bf16[1,2048,256]{2,1,0:T(8,128)(2,1)}, bf16[1,2048,256]{2,1,0:T(8,128)(2,1)}, bf16[1,2048,256]{2,1,0:T(8,128)(2,1)}) custom-call(s32[8]{0:T(128)} %fusion.5.low_ref, bf16[1,2048,256]{2,1,0:T(8,128)(2,1)} %bitcast.94, bf16[1,2048,256]{2,1,0:T(8,128)(2,1)} %bitcast.96, bf16[1,2048,256]{2,1,0:T(8,128)(2,1)} %bitcast.98, ...), custom_call_target="tpu_custom_call" | custom-call | tf_op jit(solution)/shard_map/attend_back/pallas_call | solution.py:218
  254.2 0.6 collective-permute-done
  254.9 218.9 %tail.1 = (bf16[2,256,1024]{2,1,0:T(8,128)(2,1)}, bf16[2,256,1024]{2,1,0:T(8,128)(2,1)}, f32[8,256,256]{2,1,0:T(8,128)}, bf16[2,8,64,1024]{3,2,1,0:T(8,128)(2,1)...) custom-call(bf16[4,4,2,64,1024]{4,3,2,1,0:T(8,128)(2,1)} %bitcast.101, ...), custom_call_target="tpu_custom_call" | custom-call | tf_op jit(solution)/shard_map/tail/pallas_call | solution.py:1485
  473.7 3.9 fusion.1
  477.6 3.9 fusion.7
  481.5 1.0 copy.37
  482.5 0.6 copy-done.8
  483.1 1.0 copy.38
  484.1 1.3 copy.39
  (48 shorter events, 3.4 us)
Async XLA Ops:
  5.7 0.6 copy-start.10
  127.1 16.9 %copy-start.17 = (bf16[4,256,1024]{2,1,0:T(8,128)(2,1)S(1)}, bf16[4,256,1024]{2,1,0:T(8,128)(2,1)}, u32[]{:S(2)}) copy-start(bf16[4,256,1024]{2,1,0:T(8,128)(2,1)} %get-tuple-element.44) | copy-start | bytes 6291460
  142.6 1.5 copy-start.6
  144.0 1.5 copy-start.5
  144.1 2.7 copy-start.11
  145.5 1.3 copy-start
  145.5 2.5 copy-start.13
  205.5 2.8 copy-start.1
  205.5 2.8 copy-start.12
  205.5 2.8 copy-start.14
  205.5 49.3 %collective-permute-start = (bf16[3,352,1024]{2,1,0:T(8,128)(2,1)}, bf16[3,352,1024]{2,1,0:T(8,128)(2,1)}, u32[]{:S(2)}, u32[]{:S(2)}) collective-permute-start(bf16[3,352,1024]{2,1,0:T(8,128)(2,1)} %get-tuple-element.48), channel_id=1, source_target_pairs={{0,4},{4,0},{8,12},{12,8},{16,20},{20,16},{24,28},{28,24},{1,5},{5... | collective-permute-start | bytes 6488072 | tf_op jit(solution)/shard_map/ppermute | solution.py:1650
  208.3 2.4 copy-start.3
  210.7 1.6 copy-start.18
  211.4 2.3 copy-start.4
  473.7 3.9 copy-start.2
  477.6 3.9 copy-start.9
  481.5 1.6 copy-start.8
  481.5 2.6 copy-start.7
  484.1 1.3 copy-start.16
  484.1 1.9 copy-start.15
  484.1 2.5 copy-start.19

commit v7 on v6

--- a/solution.py
+++ b/solution.py
@@ -244,9 +244,10 @@
 
 def feed_kernel(
     chunk, feed_ref, cot_ref, gate_w, up_w, down_w,
-    feed_g_ref, out_ref, keep_ref, give_ref,
-    feed_all, part, core_in, pair_in, acc,
+    feed_g_ref, out_own_ref, out_give_ref, cot_own_ref, keep_ref, give_ref,
+    feed_all, part, core_in, pair_in, acc, out_all, out_in,
     feed_send, feed_core, feed_pair, relay_send, part_send, part_core, sum_send, sum_pair,
+    out_send, out_core,
 ):
     tokens = feed_ref.shape[0]
     chunks = tokens // chunk
@@ -305,6 +306,19 @@
             part_send.at[offset * chunks + c], part_core.at[offset * chunks + c], other,
         )
 
+    def out_to_core(offset, c):
+        at = lax.rem(pair + offset, pairs) * 2 + 1 - core
+        return copy(
+            out_all.at[at, rows(c)], out_in.at[offset, rows(c)],
+            out_send.at[offset * chunks + c], out_core.at[offset * chunks + c], other,
+        )
+
+    def out_sum(at, offset, c):
+        return (
+            out_all[at, rows(c), :].astype(jnp.float32)
+            + out_in[offset, rows(c), :].astype(jnp.float32)
+        ).astype(jnp.bfloat16)
+
     def sum_to_pair(offset, c):
         return copy(
             part.at[peer(offset), rows(c)], pair_in.at[pairs - offset, rows(c)],
@@ -317,6 +331,7 @@
         for offset in range(1, pairs):
             feed_to_pair(offset, c).start()
     feed_all[me] = feed_ref[...]
+    cot_own_ref[...] = cot_ref[me]
     acc[...] = jnp.zeros_like(acc)
 
     count = chunks * pairs
@@ -358,7 +373,12 @@
         def _():
             part_to_core(offset, c).start()
 
-        out_ref[owner, rows(c), :] = plain_dot(hidden, down_w[...]).astype(jnp.bfloat16)
+        out_all[owner, rows(c), :] = plain_dot(hidden, down_w[...]).astype(jnp.bfloat16)
+
+        @pl.when(which == 1)
+        def _():
+            out_to_core(offset, c).start()
+
         acc[0] += columns_dot(gate_g, feed)
         acc[1] += columns_dot(up_g, feed)
         acc[2] += columns_dot(hidden, cot)
@@ -372,6 +392,8 @@
                 + core_in[offset, rows(c), :].astype(jnp.float32)
             ).astype(jnp.bfloat16)
             sum_to_pair(offset, c).start()
+            out_to_core(offset, c).wait_recv()
+            out_give_ref[offset - 1, rows(c), :] = out_sum(to, offset, c)
 
         return carry
 
@@ -383,6 +405,9 @@
         give_ref[n] = acc[n, pl.ds(pl.multiple_of((1 - flag) * half, 8), half), :].astype(
             jnp.bfloat16
         )
+    for c in range(chunks):
+        out_to_core(0, c).wait_recv()
+        out_own_ref[rows(c), :] = out_sum(me, 0, c)
     for c in range(chunks):
         part_to_core(0, c).wait_recv()
         for offset in range(1, pairs):
@@ -394,10 +419,12 @@
     for c in range(chunks):
         feed_to_core(c).wait_send()
         part_to_core(0, c).wait_send()
+        out_to_core(0, c).wait_send()
         for offset in range(1, pairs):
             feed_to_pair(offset, c).wait_send()
             relay(offset, c).wait_send()
             part_to_core(offset, c).wait_send()
+            out_to_core(offset, c).wait_send()
             sum_to_pair(offset, c).wait_send()
 
 
@@ -414,20 +441,24 @@
         functools.partial(feed_kernel, chunk),
         out_shape=[
             jax.ShapeDtypeStruct((tokens, width), jnp.float32),
-            jax.ShapeDtypeStruct(cot_all.shape, jnp.bfloat16),
+            jax.ShapeDtypeStruct((tokens, width), jnp.bfloat16),
+            jax.ShapeDtypeStruct((pairs - 1, tokens, width), jnp.bfloat16),
+            jax.ShapeDtypeStruct((tokens, width), jnp.bfloat16),
             jax.ShapeDtypeStruct((3, hidden // 2, width), jnp.bfloat16),
             jax.ShapeDtypeStruct((3, hidden // 2, width), jnp.bfloat16),
         ],
         in_specs=[whole] * 5,
-        out_specs=[whole] * 4,
+        out_specs=[whole] * 6,
         scratch_shapes=[
             pltpu.VMEM(cot_all.shape, jnp.bfloat16),
             pltpu.VMEM(cot_all.shape, jnp.bfloat16),
             pltpu.VMEM((pairs, tokens, width), jnp.bfloat16),
             pltpu.VMEM((pairs, tokens, width), jnp.bfloat16),
             pltpu.VMEM((3, hidden, width), jnp.float32),
+            pltpu.VMEM(cot_all.shape, jnp.bfloat16),
+            pltpu.VMEM((pairs, tokens, width), jnp.bfloat16),
         ]
-        + [dma((pairs * chunks,))] * 8,
+        + [dma((pairs * chunks,))] * 10,
         compiler_params=pltpu.CompilerParams(
             collective_id=4, has_side_effects=True, vmem_limit_bytes=67043328
         ),
@@ -1101,12 +1132,12 @@
 
 
 def tail_kernel(
-    sizes, dv_plan, out_hbm, keep_hbm, got_hbm, x_hbm, q_hbm, k_hbm, v_hbm, cos_hbm, sin_hbm,
+    sizes, dv_plan, out_own_hbm, out_got_hbm, keep_hbm, got_hbm, x_hbm, q_hbm, k_hbm, v_hbm, cos_hbm, sin_hbm,
     qw_hbm, kw_hbm, vw_hbm, attended_hbm, source_hbm, middle_hbm, middle_g_hbm, dv_hbm, gain_ref, small_ref,
     out_ref, input_g_ref, first_g_ref, sums_ref, feed_ref, gain_g_ref, feed_gain_g_ref, norms_ref,
     x_rows, q_rows, k_rows, v_rows, cos_rows, sin_rows, weights, attended, grad_acc,
     normed_full, normed_core, normed_pair, proj_full, proj_core, proj_pair,
-    out_full, out_core, out_pair, source, middle, middle_g, input_g, result,
+    out_own, out_got, source, middle, middle_g, input_g, result,
     blocks, held, mine, feed_blocks, feed_got, feed_held, feed_mine,
     small, tp_held, tp_sum, seq_held, dv_rows, dv_cols,
     *sems,
@@ -1116,14 +1147,13 @@
     me = (s, t)
     pairs = tp_size // 2
     count = seq_size.bit_length() - 1
-    normed_sems, proj_sems, out_sems = sems[:4], sems[4:8], sems[8:12]
-    dv_sems, back_sems, lo_sems = sems[12:15], sems[15:18], sems[18:21]
-    load_sem, x_sem, feed_sem, store_sem, grad_send, grad_recv = sems[21:27]
-    feed_send, feed_recv, small_send, tp_sem, seq_sem, first_sem = sems[27:]
+    normed_sems, proj_sems = sems[:4], sems[4:8]
+    dv_sems, back_sems, lo_sems = sems[8:11], sems[11:14], sems[14:17]
+    load_sem, x_sem, feed_sem, store_sem, grad_send, grad_recv = sems[17:23]
+    feed_send, feed_recv, small_send, tp_sem, seq_sem, first_sem = sems[23:]
     place = (s, t, pairs)
     normed = Reduce(place, normed_full, normed_core, normed_pair, 2, normed_sems)
     proj = Reduce(place, proj_full, proj_core, proj_pair, 1, proj_sems)
-    out = Reduce(place, out_full, out_core, out_pair, 2, out_sems)
     dv_move = Exchange(dv_plan, me, dv_hbm, dv_rows, *dv_sems)
     half = source.shape[0]
     places, depth = x_rows.shape[1:]
@@ -1143,8 +1173,9 @@
         (q_hbm, q_rows), (k_hbm, k_rows), (v_hbm, v_rows), (cos_hbm, cos_rows),
         (sin_hbm, sin_rows), (qw_hbm, weights.at[pl.ds(0, width)]),
         (kw_hbm, weights.at[pl.ds(width, width)]), (vw_hbm, weights.at[pl.ds(2 * width, width)]),
-        (out_hbm, out_full), (attended_hbm, attended),
+        (out_own_hbm, out_own), (attended_hbm, attended),
         (middle_g_hbm, middle_g), (source_hbm, source), (middle_hbm, middle),
+        (out_got_hbm, out_got),
     )
     loads = [
         pltpu.make_async_copy(origin, target, load_sem.at[n])
@@ -1167,14 +1198,13 @@
     for pair in feed_loads:
         for copy in pair:
             copy.start()
-    for n in (9, 10, 8):
+    for n in (9, 10, 12, 8, 13):
         loads[n].start()
     for copy in loads[:8]:
         copy.start()
     for n in range(2 * half):
         x_load(ordered(n)).start()
-    for copy in loads[11:]:
-        copy.start()
+    loads[11].start()
 
     barrier = pltpu.get_barrier_semaphore()
     dv_move.greet(barrier)
@@ -1222,6 +1252,44 @@
 
         lax.fori_loop(0, feed_blocks.shape[1], join, 0)
         next(feeds[n])
+    def own_part(target, slot, i):
+        piece = source.shape[2]
+        return target.at[slot, pl.ds(pl.multiple_of(i * piece, piece), piece)]
+
+    def send_back(source_ref, target, trio, b, c, wait):
+        local_sem, send_sem, recv_sem = trio
+        flat = 2 * b + c
+        j, to = flat // seq_size, lax.rem(flat, seq_size)
+        row = group * rows_each + j
+        slot = lax.rem(row, rows_local)
+        place = (to, row // rows_local)
+        here = same(place, me)
+        view = own_part(target, slot, t)
+
+        @pl.when(here)
+        def _():
+            copy = pltpu.make_async_copy(source_ref.at[b, c], view, local_sem.at[flat])
+            copy.wait() if wait else copy.start()
+
+        @pl.when(jnp.logical_not(here))
+        def _():
+            copy = remote(
+                source_ref.at[b, c], view, send_sem.at[flat], recv_sem.at[slot * tp_size + t], place
+            )
+            copy.wait_send() if wait else copy.start()
+
+    def forward(c):
+        def one(n, carry):
+            b = lax.rem(n + s // 2, half)
+            value = middle[b, c] + out_own[b, c].astype(jnp.float32)
+            for offset in range(1, pairs):
+                value = value + out_got[offset - 1, b, c].astype(jnp.float32)
+            result[b, c] = value.astype(jnp.bfloat16)
+            send_back(result, out_ref, lo_sems, b, c, False)
+            return carry
+
+        lax.fori_loop(0, half, one, 0)
+
     fine = blocks.shape[2]
     loads[9].wait()
     loads[10].wait()
@@ -1231,9 +1299,10 @@
         for n in range(seq_size // 2):
             proj_full[i, n, 0] = product[n * fine : (n + 1) * fine].astype(jnp.bfloat16)
     proj.start(0)
-    loads[8].wait()
-    out.start(0)
-    out.start(1)
+    for n in (8, 12, 13):
+        loads[n].wait()
+    forward(0)
+    forward(1)
     dv_move.start()
     for copy in loads[:8]:
         copy.wait()
@@ -1276,8 +1345,6 @@
     project_back(0, quarter)
     proj.pass_on(0)
     next(feeds[0])
-    out.pass_on(0)
-    out.pass_on(1)
     project_back(quarter, half)
     normed.start(0)
     next(feeds[1])
@@ -1305,32 +1372,6 @@
     next(feeds[0])
     next(feeds[2])
 
-    def own_part(target, slot, i):
-        piece = source.shape[2]
-        return target.at[slot, pl.ds(pl.multiple_of(i * piece, piece), piece)]
-
-    def send_back(source_ref, target, trio, b, c, wait):
-        local_sem, send_sem, recv_sem = trio
-        flat = 2 * b + c
-        j, to = flat // seq_size, lax.rem(flat, seq_size)
-        row = group * rows_each + j
-        slot = lax.rem(row, rows_local)
-        place = (to, row // rows_local)
-        here = same(place, me)
-        view = own_part(target, slot, t)
-
-        @pl.when(here)
-        def _():
-            copy = pltpu.make_async_copy(source_ref.at[b, c], view, local_sem.at[flat])
-            copy.wait() if wait else copy.start()
-
-        @pl.when(jnp.logical_not(here))
-        def _():
-            copy = remote(
-                source_ref.at[b, c], view, send_sem.at[flat], recv_sem.at[slot * tp_size + t], place
-            )
-            copy.wait_send() if wait else copy.start()
-
     small[...] = small_ref[...]
 
     def back(c):
@@ -1351,17 +1392,6 @@
 
         lax.fori_loop(0, half, one, 0)
 
-    def forward(c):
-        out.arrive(c)
-
-        def one(n, carry):
-            b = lax.rem(n + s // 2, half)
-            result[b, c] = (middle[b, c] + out.total(b, c)).astype(jnp.bfloat16)
-            send_back(result, out_ref, lo_sems, b, c, False)
-            return carry
-
-        lax.fori_loop(0, half, one, 0)
-
     def tp_copy(n):
         return remote(
             small, tp_held.at[tp_size - n], small_send.at[n],
@@ -1378,12 +1408,9 @@
         for generator in generators:
             next(generator, None)
 
-    loads[12].wait()
-    forward(0)
     next(feeds[1])
     next(feeds[0])
     next(sums[0])
-    forward(1)
     next(feeds[2])
     next(sums[1])
     loads[11].wait()
@@ -1428,7 +1455,7 @@
     feed_gain_g_ref[...] = total[1:2]
     norms_ref[...] = jnp.sqrt(total[2:3, :2])
 
-    for reduce in (normed, proj, out):
+    for reduce in (normed, proj):
         reduce.finish()
     for c in range(2):
         def done(b, carry):
@@ -1448,7 +1475,7 @@
 
 
 def tail(
-    out_part, keep, got, x_rows, query_g, key_g, value_g, cosine, sine, query_weight, key_weight, value_weight,
+    out_own, out_got, keep, got, x_rows, query_g, key_g, value_g, cosine, sine, query_weight, key_weight, value_weight,
     attended, source, middle, middle_g, gain, small, sizes,
 ):
     seq_size, tp_size, rows_each, rows_local, _ = sizes
@@ -1494,7 +1521,7 @@
             jax.ShapeDtypeStruct((1, depth), f32),
             jax.ShapeDtypeStruct((1, 2), f32),
         ],
-        in_specs=[anywhere] * 17 + [vmem] * 2,
+        in_specs=[anywhere] * 18 + [vmem] * 2,
         out_specs=[anywhere] * 5 + [vmem] * 3,
         scratch_shapes=[
             pltpu.VMEM((blocks, places, depth), bf16),
@@ -1509,8 +1536,9 @@
         ]
         + reduce_shapes(shape)
         + reduce_shapes(proj_shape)
-        + reduce_shapes(shape)
         + [
+            pltpu.VMEM(shape, bf16),
+            pltpu.VMEM((pairs - 1,) + shape, bf16),
             pltpu.VMEM(shape, bf16),
             pltpu.VMEM(shape, f32),
             pltpu.VMEM(shape, f32),
@@ -1532,11 +1560,10 @@
         ]
         + reduce_sems(2)
         + reduce_sems(1)
-        + reduce_sems(2)
         + [dma((seq_size,))] * 3
         + ([dma((blocks,))] * 2 + [dma((rows_local * tp_size,))]) * 2
         + [
-            dma((13,)),
+            dma((14,)),
             dma((blocks,)),
             dma((6,)),
             dma((5,)),
@@ -1554,7 +1581,8 @@
         ),
         name="tail",
     )(
-        out_part.reshape((tp_size,) + shape),
+        out_own.reshape(shape),
+        out_got.reshape((pairs - 1,) + shape),
         keep.reshape(feed_shape),
         got.reshape(feed_shape),
         x_rows.reshape(blocks, places, depth),
@@ -1630,8 +1658,6 @@
     output_full = output_full.reshape(tp_size * width, depth)
     source_low = lax.dynamic_index_in_dim(x_rows, me, 2, keepdims=False).reshape(tokens, depth)
     source = source_low.astype(jnp.float32)
-    cotangent = lax.dynamic_index_in_dim(cot_all, me, 0, keepdims=False).reshape(tokens, depth)
-    cotangent = cotangent.astype(jnp.float32)
     x_rows = x_rows.reshape(rows_each * ROW, depth)
     queries, keys, values = (
         part.reshape(rows_each, ROW, width) for part in (queries, keys, values)
@@ -1644,12 +1670,12 @@
     middle = source + jnp.dot(attended, output_full, preferred_element_type=jnp.float32)
     unit_feed, inv_feed = norm_rows(middle)
     feed_in = (unit_feed * feed_scale).astype(jnp.bfloat16)
-    feed_in_g, out_part, keep, give = feed_forward(
+    feed_in_g, out_own, out_give, cotangent, keep, give = feed_forward(
         feed_in, cot_all.reshape(tp_size, tokens, depth), gate_weight.T, up_weight.T, down_weight
     )
     got = lax.ppermute(give, "seq", [(n, n + 1 - 2 * (n % 2)) for n in range(seq_size)])
     middle_extra, feed_gain_part = norm_back(feed_in_g, unit_feed, inv_feed, feed_scale)
-    middle_g = cotangent + middle_extra
+    middle_g = cotangent.astype(jnp.float32) + middle_extra
     branch_g = middle_g.astype(jnp.bfloat16)
     attended_g = jnp.einsum(
         "td,ed->te", branch_g, output_full, preferred_element_type=jnp.float32
@@ -1660,6 +1686,17 @@
         [tokens_to_heads(tp_size)],
         2,
     )
+    out_give, attended_g = lax.optimization_barrier((out_give, attended_g))
+    pairs = tp_size // 2
+    out_got = jnp.concatenate(
+        [
+            lax.ppermute(
+                out_give[k - 1 : k], "tp",
+                [(n, (n + 2 * k) % tp_size) for n in range(tp_size)],
+            )
+            for k in range(1, pairs)
+        ]
+    )
     query_g, key_g, value_g = attend_back(
         low, queries, keys, values, result, attended_g.reshape(result.shape), logsum, starts
     )
@@ -1669,7 +1706,8 @@
         layer_output, input_grad, first_grad, grad_sums, feed_sums,
         gain_grad, feed_gain_grad, norms,
     ) = tail(
-        out_part,
+        out_own,
+        out_got,
         keep,
         got,
         x_rows,

time: 489 us -> 490 us (level)
  transfers between devices with their start and end apart: 1 -> 2, of which waited for: 1 -> 0; matrix products, arithmetic and copies ran while one was open for 2% -> 2% of each run, Pallas kernels for 8% -> 8%
where the time goes in v7:
time: 490 us; the launch traced here: 489 us
  Pallas kernels  453 us (92%)
  other arithmetic  15.8 us (3%)
  local copies, waits for them, and re-layouts  15.2 us (3%)
    pallas_call x1, Pallas kernels, tail(): pl.pallas_call(functools.partial(tail_kernel, sizes, plan), out_shape=[ow...  221 us
    pallas_call x1, Pallas kernels, spread(): pl.pallas_call(functools.partial(spread_kernel, plans, sizes), out_shape=...  102 us
    pallas_call x1, Pallas kernels, feed_forward(): pl.pallas_call(functools.partial(feed_kernel, chunk), out_shape=[jax.Shap...  57.4 us
    pallas_call x2, Pallas kernels, exchange(): pl.pallas_call(kernel, out_shape=[jax.ShapeDtypeStruct(shape, array.dtype...  28.4 us
    pallas_call x1, Pallas kernels, attend_back(): pl.pallas_call(attend_back_kernel, grid_spec=pltpu.PrefetchScalarGridSpec...  25.9 us
    pallas_call x1, Pallas kernels, attend(): pl.pallas_call(attend_kernel, grid_spec=pltpu.PrefetchScalarGridSpec(num_...  18.1 us
  transfers between devices with their start and end apart: 2, of which 0 were waited for; matrix products, arithmetic and copies ran while one was open for 2% of the time, Pallas kernels for 8%

profile of v7, /device:TPU:0, one launch (start us, length us, event | category | flops | bytes accessed | tf_op | source)
XLA Modules:
  0.0 489.2 jit_solution(11972900383473695239)
XLA Ops:
  0.7 0.6 multiply_power_fusion.frequency_ref
  1.3 1.3 convert_element_type.60
  2.6 0.9 reduce_window_sum.11
  3.4 1.3 broadcast_in_dim.31
  5.1 0.6 iota_subtract_fusion
  5.7 0.6 copy-done.10
  6.4 0.5 fusion.5.low_ref
  6.9 102.1 %spread.1 = (bf16[1,8,4,64,1024]{4,3,2,1,0:T(8,128)(2,1)}, bf16[4,1,8,64,1024]{4,3,2,1,0:T(8,128)(2,1)}, bf16[1,8,256,256]{3,2,1,0:T(8,128)(2,1)}, bf16[4,256,10...) custom-call(bf16[2,4,64,1024]{3,2,1,0:T(8,128)(2,1)} %bitcast.110, ...), custom_call_target="tpu_custom_call" | custom-call | tf_op jit(solution)/shard_map/spread/pallas_call | solution.py:929
  109.0 18.1 %attend.1 = (bf16[1,2048,256]{2,1,0:T(8,128)(2,1)}, f32[1,4,2048]{2,1,0:T(4,128)}) custom-call(s32[8]{0:T(128)} %fusion.5.low_ref, bf16[1,2048,256]{2,1,0:T(8,128)(2,1)} %bitcast.91, bf16[1,2048,256]{2,1,0:T(8,128)(2,1)} %bitcast.93, bf16[1,2048,256]{2,1,0:T(8,128)(2,1)} %bitcast.95, s32[1,1,2048]{2,1,0:T(1,128)} %bitcast.112), custom_call_target="tpu_custom_call" | custom-call | tf_op jit(solution)/shard_map/attend/pallas_call | solution.py:128
  127.1 15.5 %exchange_1.1 = bf16[4,1,8,64,256]{4,3,2,1,0:T(8,128)(2,1)} custom-call(bf16[1,8,4,64,256]{4,3,2,1,0:T(8,128)(2,1)} %bitcast.97), custom_call_target="tpu_custom_call" | custom-call | tf_op jit(solution)/shard_map/exchange_1/pallas_call | solution.py:569
  142.6 1.4 constant_dynamic-slice_fusion
  144.1 1.4 multiply_reduce_fusion.2
  145.5 1.3 copy-done
  146.8 1.2 multiply_convert_fusion.feed_ref
  148.0 57.4 %feed_forward.1 = (f32[512,1024]{1,0:T(8,128)}, bf16[512,1024]{1,0:T(8,128)(2,1)}, bf16[1,512,1024]{2,1,0:T(8,128)(2,1)}, bf16[512,1024]{1,0:T(8,128)(2,1)}, bf1...) custom-call(bf16[512,1024]{1,0:T(8,128)(2,1)} %multiply_convert_fusion.feed_ref, ...), custom_call_target="tpu_custom_call" | custom-call | tf_op jit(solution)/shard_map/feed_forward/pallas_call | solution.py:440
  205.9 3.0 multiply_reduce_fusion
  209.4 2.0 multiply_add_fusion
  211.4 1.3 convolution_convert_fusion
  212.7 1.0 copy.30
  213.8 12.9 %exchange_2.1 = bf16[1,8,4,64,256]{4,3,2,1,0:T(8,128)(2,1)} custom-call(bf16[4,1,8,64,256]{4,3,2,1,0:T(8,128)(2,1)} %bitcast.90), custom_call_target="tpu_custom_call" | custom-call | tf_op jit(solution)/shard_map/exchange_2/pallas_call | solution.py:569
  226.7 1.3 collective-permute-start
  228.3 0.6 pad.9.small_ref
  228.9 25.9 %attend_back.1 = (bf16[1,2048,256]{2,1,0:T(8,128)(2,1)}, bf16[1,2048,256]{2,1,0:T(8,128)(2,1)}, bf16[1,2048,256]{2,1,0:T(8,128)(2,1)}) custom-call(s32[8]{0:T(128)} %fusion.5.low_ref, bf16[1,2048,256]{2,1,0:T(8,128)(2,1)} %bitcast.92, bf16[1,2048,256]{2,1,0:T(8,128)(2,1)} %bitcast.94, bf16[1,2048,256]{2,1,0:T(8,128)(2,1)} %bitcast.96, ...), custom_call_target="tpu_custom_call" | custom-call | tf_op jit(solution)/shard_map/attend_back/pallas_call | solution.py:218
  254.8 221.1 %tail.1 = (bf16[2,256,1024]{2,1,0:T(8,128)(2,1)}, bf16[2,256,1024]{2,1,0:T(8,128)(2,1)}, f32[8,256,256]{2,1,0:T(8,128)}, bf16[2,8,64,1024]{3,2,1,0:T(8,128)(2,1)...) custom-call(bf16[4,2,64,1024]{3,2,1,0:T(8,128)(2,1)} %bitcast.106, ...), custom_call_target="tpu_custom_call" | custom-call | tf_op jit(solution)/shard_map/tail/pallas_call | solution.py:1512
  475.9 3.9 fusion.1
  479.7 3.9 fusion.7
  483.6 1.0 copy.37
  484.6 0.6 copy-done.8
  485.2 1.0 copy.38
  486.2 1.3 copy.39
  487.5 0.6 copy.40
  488.1 0.6 copy.41
  (51 shorter events, 2.4 us)
Async XLA Ops:
  5.7 0.6 copy-start.10
  127.1 16.9 %copy-start.18 = (bf16[4,256,1024]{2,1,0:T(8,128)(2,1)S(1)}, bf16[4,256,1024]{2,1,0:T(8,128)(2,1)}, u32[]{:S(2)}) copy-start(bf16[4,256,1024]{2,1,0:T(8,128)(2,1)} %get-tuple-element.48) | copy-start | bytes 6291460
  142.6 1.5 copy-start.6
  144.0 1.5 copy-start.5
  144.1 2.7 copy-start.11
  145.5 1.3 copy-start
  145.5 2.5 copy-start.13
  205.4 49.4 %collective-permute-start.1 = (bf16[3,352,1024]{2,1,0:T(8,128)(2,1)}, bf16[3,352,1024]{2,1,0:T(8,128)(2,1)}, u32[]{:S(2)}, u32[]{:S(2)}) collective-permute-start(bf16[3,352,1024]{2,1,0:T(8,128)(2,1)} %get-tuple-element.56), channel_id=1, source_target_pairs={{0,4},{4,0},{8,12},{12,8},{16,20},{20,16},{24,28},{28,24},{1,5},{5... | collective-permute-start | bytes 6488072 | tf_op jit(solution)/shard_map/ppermute | solution.py:1676
  205.9 3.0 copy-start.1
  205.9 3.5 copy-start.4
  205.9 3.5 copy-start.12
  205.9 3.5 copy-start.14
  209.4 2.0 copy-start.19
  211.4 1.3 copy-start.3
  212.7 15.3 %copy-start.15 = (f32[8,256]{1,0:T(8,128)S(1)}, f32[8,256]{1,0:T(8,128)}, u32[]{:S(2)}) copy-start(f32[8,256]{1,0:T(8,128)} %get-tuple-element.64) | copy-start | bytes 24580
  226.7 28.0 %collective-permute-start = (bf16[1,512,1024]{2,1,0:T(8,128)(2,1)}, bf16[1,512,1024]{2,1,0:T(8,128)(2,1)}, u32[]{:S(2)}, u32[]{:S(2)}) collective-permute-start(bf16[1,512,1024]{2,1,0:T(8,128)(2,1)} %get-tuple-element.54), channel_id=1, source_target_pairs={{0,2},{1,3},{2,0},{3,1},{4,6},{5,7},{6,4},{7,5},{8,10},{9,11},{10,... | collective-permute-start | bytes 3145736 | tf_op jit(solution)/shard_map/ppermute | solution.py:1693
  475.8 3.9 copy-start.2
  479.7 3.9 copy-start.9
  483.6 1.6 copy-start.8
  483.6 2.6 copy-start.7
  486.2 1.3 copy-start.17
  486.2 1.9 copy-start.16
  486.2 2.5 copy-start.20
